TPU v7x, 32 devices: a whole 2x2x4 slice. The times are simulated.
32 devices in a mesh: cx: 4 (over z), cy: 8 (over y, x, core).
Axes of the slice: x: 2, y: 2, z: 4, core: 2. Of those that a mesh axis runs over, the one named last changes fastest.
Arguments:
- latent: float32 [64, 128, 256], P('cx', 'cy'), may hold values from -6 to 6
- observed: float32 [32768], P(('cx', 'cy')), may hold values from -12 to 12
- sigma: float32 [32768], P(('cx', 'cy')), may hold values from 0.5 to 1.5
- response: bfloat16 [16384, 64, 128], P(('cx', 'cy')), may hold values from -0.375 to 0.375
- offsets: int32 [64, 16384], P(None, ('cx', 'cy')), may hold values from 0 to 254
- fractions: float32 [64, 16384], P(None, ('cx', 'cy')), may hold values from 0 to 1
- tile_group: int32 [16384], P(('cx', 'cy')), may hold values from 0 to 7
- tile_slot: int32 [16384], P(('cx', 'cy')), may hold values from 0 to 511, as said below
- send_index: int32 [32, 32, 16], P(('cx', 'cy')), may hold values from -1 to 255, as said below
Outputs:
- gradient: float32 [64, 128, 256], P('cx', 'cy')
- predicted: float32 [32768], P(('cx', 'cy'))
Inputs may be any that keep to these rules, and one draw needn't show every extreme that they name: `send_index`: entries are local column numbers of the sending device, or -1 for an empty slot; for each sender and receiver the used slots come first, 8 to 16 of them; every sender uses all 16 slots for some receiver, and some receiver gets all 16 slots from every sender. `tile_slot`: tile slot q names slot q % 16 from sender q // 16, a slot that this sender uses for this device.
All inputs are finite; a program needn't handle non-finite values.
Results may differ from a plain program's by a relative error of at most 0.0036.
Values may be sent and summed in bfloat16 or wider, within the bound.
No kernel may reach another device: no remote copies, remote signals or barrier semaphores. Data moves between devices by JAX's collectives and lax.ppermute only.
A program may use at most 64 MiB of HBM per device.

v0:
```python
import jax
import jax.numpy as jnp
from jax import lax
from jax.sharding import PartitionSpec as P


def padded(cells, sides, width):
    for axis, dim in sides:
        count = lax.axis_size(axis)
        ends = count - 1
        head = lax.slice_in_dim(cells, 0, width, axis=dim)
        tail = lax.slice_in_dim(cells, cells.shape[dim] - width, cells.shape[dim], axis=dim)
        cells = jnp.concatenate(
            [
                lax.ppermute(tail, axis, [(i, (i + 1) % count) for i in range(ends)]),
                cells,
                lax.ppermute(head, axis, [((i + 1) % count, i) for i in range(ends)]),
            ],
            axis=dim,
        )
    return cells


def kernel_taps():
    shifts = jnp.arange(-16, 17).astype(jnp.float32)
    scaled = jnp.sqrt(jnp.float32(3.0)) * jnp.abs(shifts) / 8.0
    raw_taps = (1.0 + scaled) * jnp.exp(-scaled)
    return 0.8 * raw_taps / jnp.sqrt(jnp.sum(raw_taps * raw_taps))


def taps_over(widened, along, length, kernel):
    summed = kernel[0] * lax.slice_in_dim(widened, 0, length, axis=along)
    for shift_at in range(1, 33):
        summed = summed + kernel[shift_at] * lax.slice_in_dim(
            widened, shift_at, shift_at + length, axis=along
        )
    return summed


def smooth(values, kernel):
    rows_x, rows_y, depth = values.shape
    widened = padded(values, (("cx", 0),), 16)
    values = taps_over(widened, 0, rows_x, kernel)
    widened = padded(values, (("cy", 1),), 16)
    values = taps_over(widened, 1, rows_y, kernel)
    widened = jnp.pad(values, ((0, 0), (0, 0), (16, 16)))
    return taps_over(widened, 2, depth, kernel)


def on_device(
    latent, observed, sigma, response, offsets, fractions, tile_group, tile_slot, send_index
):
    kernel = kernel_taps()
    rows_x, rows_y, depth = latent.shape
    across_x = lax.axis_size("cx")
    across_y = lax.axis_size("cy")
    devices = across_x * across_y
    capacity = send_index.shape[2]
    star_tile = response.shape[2]
    groups = observed.shape[0] // star_tile
    density = jnp.exp(smooth(latent, kernel))
    columns = density.reshape(rows_x * rows_y, depth).astype(jnp.bfloat16)
    send_rows = send_index.reshape(devices, capacity)
    valid = send_rows >= 0
    packed = jnp.where(
        valid[..., None], columns[jnp.maximum(send_rows, 0)], jnp.zeros((), jnp.bfloat16)
    )
    received = lax.all_to_all(packed, ("cx", "cy"), split_axis=0, concat_axis=0, tiled=True)
    received = received.reshape(-1)
    sample_at = tile_slot[None, :] * depth + offsets
    lower = received[sample_at].astype(jnp.float32)
    upper = received[sample_at + 1].astype(jnp.float32)
    samples = ((1.0 - fractions) * lower + fractions * upper).astype(jnp.bfloat16)
    tile_pred = jnp.einsum("tms,mt->ts", response, samples, preferred_element_type=jnp.float32)
    one_hot = (tile_group[:, None] == jnp.arange(groups)[None, :]).astype(jnp.float32)
    predicted = jnp.dot(one_hot.T, tile_pred, precision=lax.Precision.HIGHEST)
    stars_obs = observed.reshape(groups, star_tile)
    stars_sig = sigma.reshape(groups, star_tile)
    resid = (predicted - stars_obs) / (stars_sig * stars_sig)
    tile_resid = jnp.dot(one_hot, resid, precision=lax.Precision.HIGHEST).astype(jnp.bfloat16)
    back = jnp.einsum("tms,ts->mt", response, tile_resid, preferred_element_type=jnp.float32)
    flat_grad = jnp.zeros((devices * capacity * depth,), jnp.float32)
    flat_grad = flat_grad.at[sample_at].add((1.0 - fractions) * back)
    flat_grad = flat_grad.at[sample_at + 1].add(fractions * back)
    returned = lax.all_to_all(
        flat_grad.reshape(devices, capacity, depth).astype(jnp.bfloat16),
        ("cx", "cy"),
        split_axis=0,
        concat_axis=0,
        tiled=True,
    ).astype(jnp.float32)
    returned = returned.reshape(devices * capacity, depth)
    targets = jnp.where(valid, send_rows, rows_x * rows_y).reshape(-1)
    column_grad = jax.ops.segment_sum(returned, targets, num_segments=rows_x * rows_y + 1)[
        : rows_x * rows_y
    ]
    dens_grad = column_grad.reshape(rows_x, rows_y, depth)
    gradient = latent + smooth(density * dens_grad, kernel)
    return (gradient, predicted.reshape(-1))


def solution(mesh):
    placed = (
        P("cx", "cy", None),
        P(("cx", "cy")),
        P(("cx", "cy")),
        P(("cx", "cy"), None, None),
        P(None, ("cx", "cy")),
        P(None, ("cx", "cy")),
        P(("cx", "cy")),
        P(("cx", "cy")),
        P(("cx", "cy"), None, None),
    )
    return jax.shard_map(
        on_device,
        mesh=mesh,
        in_specs=placed,
        out_specs=(P("cx", "cy", None), P(("cx", "cy"))),
        check_vma=False,
    )
```

profile of v0, /device:TPU:12, one launch (start us, length us, event | category | flops | bytes accessed | tf_op | source)
XLA Modules:
  0.0 978.7 jit_solution(17821146238110843146)
XLA Ops:
  0.6 0.0 copy-start.2
  0.6 3.5 collective-permute-start
  4.1 2.4 collective-permute-start.1
  6.5 0.6 multiply_reduce_fusion
  7.8 0.7 broadcast_multiply_fusion
  8.5 0.7 broadcast_maximum_fusion
  9.2 0.9 fusion.442
  10.2 0.7 fusion.451
  11.0 0.7 fusion.452
  11.7 0.1 copy.14
  11.8 0.1 reshape.83
  11.9 0.0 collective-permute-done
  11.9 1.0 constant_dynamic-update-slice_fusion
  12.9 1.1 collective-permute-done.1
  14.0 22.2 %fusion.404 = f32[16,16,256]{2,1,0:T(8,128)S(1)} fusion(f32[32,16,256]{2,1,0:T(8,128)S(1)} %constant_dynamic-update-slice_fusion.2, f32[32,16,256]{2,1,0:T(8,128)S(1)} %get-tuple-element.6, f32[16,16,256]{2,1,0:T(8,128)S(1)} %collective-permute-done.1, f32[16,16,256]{2,1,0:T(8,128)} %param.9, f32[16,16,256]{2,1,0:T(8,128)S(1)} %collective-permute-done, ...), kind=kLoop, calls=%fused_computation.652 | loop fusion | flops 4259840 | bytes 8913028 | tf_op jit(solution)/shard_map/add | solution.py:34
  36.2 1.9 collective-permute-start.3
  38.1 2.4 collective-permute-start.2
  40.5 0.0 copy-done.2
  40.6 0.1 copy.13
  40.7 1.3 collective-permute-done.3
  42.0 4.7 collective-permute-done.2
  46.7 22.1 %fusion.313 = f32[16,16,256]{2,1,0:T(8,128)S(1)} fusion(f32[16,16,256]{2,1,0:T(8,128)S(1)} %fusion.404, f32[16,16,256]{2,1,0:T(8,128)S(1)} %collective-permute-done.3, f32[16,16,256]{2,1,0:T(8,128)S(1)} %collective-permute-done.2, f32[]{:T(128)} %bitcast.32, f32[]{:T(128)} %bitcast.31, f32[]{:T(128)} %bitcast.30, f32[]{:T(128)} %bitcast.29, f32[]{:T(128)} %bitcast.28, ...), kind=kLoop, calls=%fused_computation.554 | loop fusion | flops 6225920 | bytes 1048708 | tf_op jit(solution)/shard_map/add | solution.py:34
  68.8 22.8 %fusion.449 = (bf16[16,16,256]{2,1,0:T(8,128)(2,1)S(1)}, f32[16,16,256]{2,1,0:T(8,128)S(1)}) fusion(f32[]{:T(128)} %bitcast.32, f32[]{:T(128)} %bitcast.31, f32[]{:T(128)} %bitcast.30, f32[]{:T(128)} %bitcast.29, f32[]{:T(128)} %bitcast.28, f32[]{:T(128)} %bitcast.27, f32[]{:T(128)} %bitcast.26, f32[]{:T(128)} %bitcast.25, f32[]{:T(128)} %bitcast.24, ...), kind=kLoop, calls=%fused_computation.747 | loop fusion | flops 4325376 | bytes 655492 | tf_op jit(solution)/shard_map/convert_element_type | solution.py:62
  91.7 2.0 gather_fusion
  93.7 0.8 broadcast_select_fusion
  94.5 4.3 all-to-all-start
  98.8 8.8 all-to-all-done
  107.7 0.2 copy.20
  107.9 200.5 %gather_fusion.2 = bf16[32768]{0:T(1024)(128)(2,1)S(1)} fusion(bf16[131072]{0:T(1024)(128)(2,1)S(1)} %bitcast.83, s32[32768]{0:T(1024)S(1)} %broadcast_clamp_fusion), kind=kCustom, calls=%fused_computation.2 | custom fusion | bytes 262144 | tf_op jit(solution)/shard_map/gather | solution.py:72
  308.4 0.0 copy-start.1
  308.4 200.5 %gather_fusion.1 = bf16[32768]{0:T(1024)(128)(2,1)S(1)} fusion(bf16[131072]{0:T(1024)(128)(2,1)S(1)} %bitcast.84, s32[32768]{0:T(1024)S(1)} %broadcast_clamp_fusion.1), kind=kCustom, calls=%fused_computation.1 | custom fusion | bytes 262144 | tf_op jit(solution)/shard_map/gather | solution.py:71
  509.0 0.0 copy-done.1
  509.0 0.2 copy.15
  509.2 0.0 copy-start.4
  509.2 0.0 copy-start.5
  509.2 0.0 copy-start.6
  509.2 5.7 fusion.453
  514.9 0.0 copy-done.4
  514.9 0.4 fusion.437
  515.4 0.0 copy-done.6
  515.4 0.0 copy-start.3
  515.4 0.3 fusion
  515.7 7.8 fusion.435
  523.5 0.1 copy.18
  523.8 171.2 %scatter_custom_fusion = f32[131072]{0:T(1024)S(1)} fusion(s32[32768]{0:T(1024)S(1)} %bitcast.94, f32[32768]{0:T(1024)S(1)} %bitcast.96, f32[]{:T(128)} %constant.15.clone.1), kind=kCustom, calls=%fused_computation.716 | custom fusion | flops 32768 | bytes 524292 | tf_op jit(solution)/shard_map/scatter-add | solution.py:83
  695.0 0.0 copy-start
  695.0 175.2 %scatter_fusion = f32[131072]{0:T(1024)S(1)} fusion(f32[131072]{0:T(1024)S(1)} %scatter_custom_fusion, s32[32768]{0:T(1024)S(1)} %bitcast.87, f32[32768]{0:T(1024)S(1)} %bitcast.92), kind=kCustom, calls=%fused_computation.4 | custom fusion | flops 32768 | bytes 524288 | tf_op jit(solution)/shard_map/scatter-add | solution.py:84
  870.3 0.8 convert_element_type.42
  871.1 4.2 all-to-all-start.1
  875.3 0.1 copy.12
  875.4 0.1 reshape.72
  875.5 8.8 all-to-all-done.1
  884.2 3.4 scatter_custom_fusion.2
  887.7 3.3 collective-permute-start.5
  891.0 2.8 collective-permute-start.4
  893.8 4.0 collective-permute-done.5
  897.8 2.3 collective-permute-done.4
  900.1 21.2 %fusion.225 = f32[16,16,256]{2,1,0:T(8,128)S(1)} fusion(f32[16,16,256]{2,1,0:T(8,128)S(1)} %mul.1046, f32[16,16,256]{2,1,0:T(8,128)S(1)} %collective-permute-done.5, f32[16,16,256]{2,1,0:T(8,128)S(1)} %collective-permute-done.4, f32[]{:T(128)} %bitcast.32, f32[]{:T(128)} %bitcast.31, f32[]{:T(128)} %bitcast.30, f32[]{:T(128)} %bitcast.29, f32[]{:T(128)} %bitcast.28, ...), kind=kLoop, calls=%fused_computation.466 | loop fusion | flops 6225920 | bytes 1048708 | tf_op jit(solution)/shard_map/add | solution.py:34
  921.3 3.1 collective-permute-start.7
  924.4 1.9 collective-permute-start.6
  926.3 3.2 collective-permute-done.7
  929.6 3.4 collective-permute-done.6
  933.0 22.1 %fusion.137 = f32[16,16,256]{2,1,0:T(8,128)S(1)} fusion(f32[16,16,256]{2,1,0:T(8,128)S(1)} %fusion.225, f32[16,16,256]{2,1,0:T(8,128)S(1)} %collective-permute-done.7, f32[16,16,256]{2,1,0:T(8,128)S(1)} %collective-permute-done.6, f32[]{:T(128)} %bitcast.32, f32[]{:T(128)} %bitcast.31, f32[]{:T(128)} %bitcast.30, f32[]{:T(128)} %bitcast.29, f32[]{:T(128)} %bitcast.28, ...), kind=kLoop, calls=%fused_computation.378 | loop fusion | flops 6225920 | bytes 1048708 | tf_op jit(solution)/shard_map/add | solution.py:34
  955.1 23.6 %fusion.123 = f32[16,16,256]{2,1,0:T(8,128)} fusion(f32[16,16,256]{2,1,0:T(8,128)S(1)} %copy-done, f32[16,16,256]{2,1,0:T(8,128)S(1)} %fusion.137, f32[]{:T(128)} %bitcast.32, f32[]{:T(128)} %bitcast.31, f32[]{:T(128)} %bitcast.30, f32[]{:T(128)} %bitcast.29, f32[]{:T(128)} %bitcast.28, f32[]{:T(128)} %bitcast.27, f32[]{:T(128)} %bitcast.26, f32[]{:T(128)} %bitcast.25, ...), kind=kLoop, calls=%fused_computation.364 | loop fusion | flops 4325376 | bytes 786564 | tf_op jit(solution)/shard_map/add | solution.py:98
  (22 shorter events, 0.5 us)
Async XLA Ops:
  0.6 39.9 %copy-start.2 = (s32[1,32,16]{1,2,0:T(8,128)S(1)}, s32[1,32,16]{1,2,0:T(8,128)}, u32[]{:S(2)}) copy-start(s32[1,32,16]{1,2,0:T(8,128)} %param.17) | copy-start | bytes 6148
  0.6 11.2 %collective-permute-start = (f32[16,16,256]{2,1,0:T(8,128)}, f32[16,16,256]{2,1,0:T(8,128)S(1)}, u32[]{:S(2)}, u32[]{:S(2)}) collective-permute-start(f32[16,16,256]{2,1,0:T(8,128)} %param.9), channel_id=1, source_target_pairs={{0,8},{8,16},{16,24},{1,9},{9,17},{17,25},{2,10},{10,18},{18,26},{... | collective-permute-start | bytes 786440 | tf_op jit(solution)/shard_map/ppermute | solution.py:15
  4.1 9.9 %collective-permute-start.1 = (f32[16,16,256]{2,1,0:T(8,128)}, f32[16,16,256]{2,1,0:T(8,128)S(1)}, u32[]{:S(2)}, u32[]{:S(2)}) collective-permute-start(f32[16,16,256]{2,1,0:T(8,128)} %param.9), channel_id=1, source_target_pairs={{8,0},{16,8},{24,16},{9,1},{17,9},{25,17},{10,2},{18,10},{26,18},{... | collective-permute-start | bytes 786440 | tf_op jit(solution)/shard_map/ppermute | solution.py:17
  36.2 5.8 collective-permute-start.3
  38.1 8.6 collective-permute-start.2
  94.5 13.2 %all-to-all-start = ((bf16[32,16,256]{2,1,0:T(8,128)(2,1)}), bf16[32,16,256]{2,1,0:T(8,128)(2,1)S(1)}, u32[]{:S(2)}, u32[]{:S(2)}) async-start(bf16[32,16,256]{2,1,0:T(8,128)(2,1)} %broadcast_select_fusion), calls=%async_computation | async-start | bytes 524288 | tf_op jit(solution)/shard_map/all_to_all | solution.py:68
  308.4 200.6 %copy-start.1 = (f32[64,512]{1,0:T(8,128)S(1)}, f32[64,512]{1,0:T(8,128)}, u32[]{:S(2)}) copy-start(f32[64,512]{1,0:T(8,128)} %param.14) | copy-start | bytes 393220
  509.2 5.7 copy-start.4
  509.2 6.2 copy-start.5
  509.2 6.2 copy-start.6
  515.4 354.8 %copy-start.3 = (f32[8,128]{1,0:T(8,128)}, f32[8,128]{1,0:T(8,128)S(1)}, u32[]{:S(2)}) copy-start(f32[8,128]{1,0:T(8,128)S(1)} %fusion.437) | copy-start | bytes 12292
  695.0 260.1 %copy-start = (f32[16,16,256]{2,1,0:T(8,128)S(1)}, f32[16,16,256]{2,1,0:T(8,128)}, u32[]{:S(2)}) copy-start(f32[16,16,256]{2,1,0:T(8,128)} %param.9) | copy-start | bytes 786436
  871.1 13.2 %all-to-all-start.1 = ((bf16[32,16,256]{2,1,0:T(8,128)(2,1)}), bf16[32,16,256]{2,1,0:T(8,128)(2,1)S(1)}, u32[]{:S(2)}, u32[]{:S(2)}) async-start(bf16[32,16,256]{2,1,0:T(8,128)(2,1)} %convert_element_type.42), calls=%async_computation.1 | async-start | bytes 524288 | tf_op jit(solution)/shard_map/all_to_all | solution.py:85
  887.7 10.1 %collective-permute-start.5 = (f32[16,16,256]{2,1,0:T(8,128)S(1)}, f32[16,16,256]{2,1,0:T(8,128)S(1)}, u32[]{:S(2)}, u32[]{:S(2)}) collective-permute-start(f32[16,16,256]{2,1,0:T(8,128)S(1)} %mul.1046), channel_id=1, source_target_pairs={{8,0},{16,8},{24,16},{9,1},{17,9},{25,17},{10,2},{18,10},{26,18},{... | collective-permute-start | bytes 786440 | tf_op jit(solution)/shard_map/ppermute | solution.py:17
  891.0 9.1 collective-permute-start.4
  921.3 8.2 collective-permute-start.7
  924.4 8.6 collective-permute-start.6
where the time goes:
time: 981 us; the launch traced here: 979 us
  other arithmetic  488 us (50%)
  local copies, waits for them, and re-layouts  407 us (41%)
  waiting for transfers between devices  37.7 us (4%)
  starting transfers between devices  29.8 us (3%)
  matrix products  14.2 us (1%)
    gather x1, local copies, waits for them, and re-layouts, on_device(): upper = received[sample_at + 1].astype(jnp.float32)  200 us
    gather x1, local copies, waits for them, and re-layouts, on_device(): lower = received[sample_at].astype(jnp.float32)  200 us
    scatter-add x1, other arithmetic, on_device(): flat_grad = flat_grad.at[sample_at + 1].add(fractions * back)  175 us
    scatter-add x1, other arithmetic, on_device(): flat_grad = flat_grad.at[sample_at].add((1.0 - fractions) * back)  171 us
    add x4, other arithmetic, taps_over(): summed + kernel[shift_at] * lax.slice_in_dim(widened, shift_at, shift_at...  87.6 us
    add x1, other arithmetic, on_device(): gradient = latent + smooth(density * dens_grad, kernel)  23.6 us
    convert_element_type x1, other arithmetic, on_device(): columns = density.reshape(rows_x * rows_y, depth).astype(jnp.bfloat16)  22.8 us
  transfers between devices with their start and end apart: 10, of which 9 were waited for; matrix products, arithmetic and copies ran while one was open for 1% of the time, Pallas kernels for 0%

commit v1 on v0

v1 whole, which is shorter than its diff:
```python
import functools
import math

import jax
import jax.numpy as jnp
from jax import lax
from jax.experimental import pallas as pl
from jax.experimental.pallas import tpu as pltpu
from jax.sharding import PartitionSpec as P

REACH = 16
LANES = 128
F32 = jnp.float32
BF16 = jnp.bfloat16
HALO = BF16


def tap_scale():
    total = 0.0
    for shift in range(-REACH, REACH + 1):
        a = math.sqrt(3.0) * abs(shift) / 8.0
        total += ((1.0 + a) * math.exp(-a)) ** 2
    return 0.8 / math.sqrt(total)


def split(values):
    high = values.astype(BF16)
    low = (values - high.astype(F32)).astype(BF16)
    return high, low


def mm(a, b):
    return jnp.dot(a, b, preferred_element_type=F32)


def mm_nt(a, b):
    return lax.dot_general(a, b, (((1,), (1,)), ((), ())), preferred_element_type=F32)


def iota(shape, dim):
    return lax.broadcasted_iota(jnp.int32, shape, dim)


def apply_left(mat_high, mat_low, values):
    if values.dtype == BF16:
        return mm(mat_high, values) + mm(mat_low, values)
    high, low = split(values)
    return mm(mat_high, high) + (mm(mat_high, low) + mm(mat_low, high))


def apply_right(values, mat_high, mat_low):
    high, low = split(values)
    return mm(high, mat_high) + (mm(low, mat_high) + mm(high, mat_low))


def call(body, outs, *args, scratch=(), limit=16, flops=0, name=None):
    shapes = [jax.ShapeDtypeStruct(s, d) for s, d in outs]
    moved = sum(math.prod(a.shape) * a.dtype.itemsize for a in args) + sum(
        math.prod(s.shape) * s.dtype.itemsize for s in shapes
    )
    return pl.pallas_call(
        body,
        out_shape=shapes,
        in_specs=[pl.BlockSpec(memory_space=pltpu.VMEM)] * len(args),
        out_specs=[pl.BlockSpec(memory_space=pltpu.VMEM)] * len(shapes),
        scratch_shapes=list(scratch),
        compiler_params=pltpu.CompilerParams(vmem_limit_bytes=limit << 20),
        cost_estimate=pl.CostEstimate(flops=flops, bytes_accessed=moved, transcendentals=0),
        name=name,
    )(*args)


def taps_matrix(distance, kept):
    a = (math.sqrt(3.0) / 8.0) * jnp.abs(distance).astype(F32)
    value = (tap_scale() * (1.0 + a)) * jnp.exp(-a)
    return jnp.where(kept & (jnp.abs(distance) <= REACH), value, 0.0)


def operators_body(rows_x, rows_y, depth, hx_ref, hy_ref, hz_ref):
    cells = rows_x * rows_y
    out = iota((cells, cells), 0)
    inp = iota((cells, cells), 1)
    out_x, out_y = out // rows_y, out % rows_y
    inp_x, inp_y = inp // rows_y, inp % rows_y
    for at, block in enumerate((0, 1, -1)):
        high, low = split(taps_matrix(out_x - inp_x + block * rows_x, out_y == inp_y))
        hx_ref[2 * at], hx_ref[2 * at + 1] = high, low
        high, low = split(taps_matrix(out_y - inp_y + block * rows_y, out_x == inp_x))
        hy_ref[2 * at], hy_ref[2 * at + 1] = high, low
    shift = iota((depth, depth), 0) - iota((depth, depth), 1)
    high, low = split(taps_matrix(shift, shift == shift))
    hz_ref[0], hz_ref[1] = high, low


def one_hot(hits):
    return jnp.where(hits, 1.0, 0.0).astype(BF16)


def tables_body(
    off_ref, frac_ref, group_ref, slot_ref, send_ref,
    idx_ref, w_ref, grp_ref, take_ref, give_ref, pack_ref, sum_ref, keep,
):
    tiles = off_ref.shape[1]
    slots = take_ref.shape[1]
    cells = pack_ref.shape[1]
    off = off_ref[...]
    frac = frac_ref[...]
    idx_ref[...] = jnp.concatenate([off, off + 1], axis=0).T
    w_ref[...] = jnp.concatenate([1.0 - frac, frac], axis=0).T
    keep[...] = jnp.broadcast_to(group_ref[...], (LANES, tiles)).T
    first = iota((tiles // 2, LANES), 1) < LANES // 2
    grp_ref[...] = jnp.where(
        first, keep[pl.ds(0, tiles // 2, 2), :], keep[pl.ds(1, tiles // 2, 2), :]
    )
    slot = slot_ref[...]
    wide = jnp.broadcast_to(slot, (LANES, tiles)).T
    for at in range(0, slots, LANES):
        take_ref[:, at : at + LANES] = one_hot(wide == iota((tiles, LANES), 1) + at)
    give_ref[...] = one_hot(jnp.broadcast_to(slot, (slots, tiles)) == iota((slots, tiles), 0))
    send = send_ref[...]
    wide = jnp.broadcast_to(send, (LANES, slots)).T
    for at in range(0, cells, LANES):
        pack_ref[:, at : at + LANES] = one_hot(wide == iota((slots, LANES), 1) + at)
    sum_ref[...] = one_hot(jnp.broadcast_to(send, (cells, slots)) == iota((cells, slots), 0))


def three(mats_ref, own, before, after):
    total = apply_left(mats_ref[0], mats_ref[1], own)
    total += apply_left(mats_ref[2], mats_ref[3], before)
    return total + apply_left(mats_ref[4], mats_ref[5], after)


def first_body(own_ref, before_ref, after_ref, mats_ref, out_ref, *sent_ref):
    out = three(mats_ref, own_ref[...], before_ref[...], after_ref[...])
    out_ref[...] = out
    for ref in sent_ref:
        ref[...] = out.astype(ref.dtype)


def density_body(own_ref, before_ref, after_ref, mats_ref, hz_ref, pack_ref, dens_ref, packed_ref):
    out = three(mats_ref, own_ref[...], before_ref[...], after_ref[...])
    dens = jnp.exp(apply_right(out, hz_ref[0], hz_ref[1]))
    dens_ref[...] = dens
    packed_ref[...] = mm(pack_ref[...], dens.astype(BF16)).astype(BF16)


def owner_body(sum_ref, back_ref, dens_ref, hz_ref, out_ref, sent_ref):
    grad = dens_ref[...] * mm(sum_ref[...], back_ref[...])
    out = apply_right(grad, hz_ref[0], hz_ref[1])
    out_ref[...] = out
    sent_ref[...] = out.astype(sent_ref.dtype)


def last_body(own_ref, before_ref, after_ref, mats_ref, latent_ref, out_ref):
    out_ref[...] = latent_ref[...] + three(mats_ref, own_ref[...], before_ref[...], after_ref[...])


def cone_body(
    got_ref, resp_ref, idx_ref, w_ref, grp_ref, take_ref, give_ref, obs_ref, sig_ref,
    pred_ref, grad_ref, both, pairs, weights, cells,
):
    tiles, samples, star_tile = resp_ref.shape
    depth = got_ref.shape[1]
    groups = obs_ref.shape[0]
    half = LANES // 2
    layers = depth // LANES
    step_pairs = 8
    step_tiles = 2 * step_pairs
    steps = tiles // step_tiles
    idx = idx_ref[...]
    columns = mm(take_ref[...], got_ref[...])
    value = jnp.zeros((tiles, LANES), F32)
    for at in range(layers):
        piece = jnp.take_along_axis(columns[:, at * LANES : (at + 1) * LANES], idx % LANES, axis=1)
        value = jnp.where(idx // LANES == at, piece, value)
    value = w_ref[...] * value
    both[...] = value + pltpu.roll(value, half, 1)
    first = iota((tiles // 2, LANES), 1) < half
    pairs[...] = jnp.where(
        first, both[pl.ds(0, tiles // 2, 2), :], both[pl.ds(1, tiles // 2, 2), :]
    )
    group_at = iota((groups, LANES), 0)

    def rows_of(ref, step):
        return ref[pl.ds(pl.multiple_of(step * step_tiles, step_tiles), step_tiles)].reshape(
            step_tiles * samples, star_tile
        )

    def pair_rows(ref, step):
        return ref[pl.ds(pl.multiple_of(step * step_pairs, step_pairs), step_pairs), :]

    def predict(step, total):
        pair = pair_rows(pairs, step)
        group = pair_rows(grp_ref, step)
        left = [
            jnp.where(group[i : i + 1] == group_at, pair[i : i + 1], 0.0)
            for i in range(step_pairs)
        ]
        return total + mm(jnp.concatenate(left, axis=1).astype(BF16), rows_of(resp_ref, step))

    pred = lax.fori_loop(0, steps, predict, jnp.zeros((groups, star_tile), F32))
    pred_ref[...] = pred
    sig = sig_ref[...]
    resid = ((pred - obs_ref[...]) / (sig * sig)).astype(BF16)
    rows = 2 * layers
    at_row = iota((2 * rows, LANES), 0)
    row_layer = at_row % layers
    row_tile = (at_row % rows) // layers
    row_high = at_row < rows
    lane_first = iota((step_pairs, LANES), 1) < half
    level = [(iota((16, LANES), 0) + 16 * k).astype(F32).astype(BF16) for k in range(LANES // 16)]
    one = jnp.ones((16, LANES), BF16)
    zero = jnp.zeros((16, LANES), BF16)

    def backward(step, carry):
        group = pair_rows(grp_ref, step)
        back = mm_nt(resid, rows_of(resp_ref, step))
        picked = [
            jnp.sum(
                jnp.where(group[i : i + 1] == group_at, back[:, i * LANES : (i + 1) * LANES], 0.0),
                axis=0, keepdims=True,
            )
            for i in range(step_pairs)
        ]
        picked = jnp.concatenate(picked, axis=0)
        swapped = pltpu.roll(picked, half, 1)
        base = pl.multiple_of(step * step_tiles, step_tiles)
        even = jnp.where(lane_first, picked, swapped) * w_ref[pl.ds(base, step_pairs, 2), :]
        odd = jnp.where(lane_first, swapped, picked) * w_ref[pl.ds(base + 1, step_pairs, 2), :]
        spots = (idx_ref[pl.ds(base, step_pairs, 2), :], idx_ref[pl.ds(base + 1, step_pairs, 2), :])
        made = []
        for i in range(step_pairs):
            left, right = [], []
            for which, weight in enumerate((even, odd)):
                spot = spots[which][i : i + 1]
                row = weight[i : i + 1]
                high = row.astype(BF16).astype(F32)
                kept = (row_tile == which) & (row_layer == spot // LANES)
                left.append(jnp.where(kept, jnp.where(row_high, high, row - high), 0.0))
                lane = jnp.broadcast_to((spot % LANES).astype(F32), (16, LANES)).astype(BF16)
                right.append(
                    jnp.concatenate([jnp.where(lane == lv, one, zero) for lv in level], axis=0)
                )
            out = mm_nt(
                jnp.concatenate(left, axis=1).astype(BF16), jnp.concatenate(right, axis=1)
            )
            made.append(out[:rows] + out[rows:])
        count = step_pairs * rows
        cells[pl.ds(pl.multiple_of(step * count, count), count), :] = jnp.concatenate(made, axis=0)
        return carry

    lax.fori_loop(0, steps, backward, 0)
    give = give_ref[...]
    for at in range(layers):
        high, low = split(cells[pl.ds(at, tiles, layers), :])
        grad_ref[:, at * LANES : (at + 1) * LANES] = (mm(give, high) + mm(give, low)).astype(BF16)


def shifted(values, axis):
    count = lax.axis_size(axis)
    up = [(i, i + 1) for i in range(count - 1)]
    down = [(i + 1, i) for i in range(count - 1)]
    return lax.ppermute(values, axis, up), lax.ppermute(values, axis, down)


def on_device(
    latent, observed, sigma, response, offsets, fractions, tile_group, tile_slot, send_index
):
    rows_x, rows_y, depth = latent.shape
    cells = rows_x * rows_y
    axes = ("cx", "cy")
    devices = lax.axis_size("cx") * lax.axis_size("cy")
    slots = devices * send_index.shape[2]
    tiles, samples, star_tile = response.shape
    groups = observed.shape[0] // star_tile
    own = latent.reshape(cells, depth)

    hx, hy, hz = call(
        functools.partial(operators_body, rows_x, rows_y, depth),
        [((6, cells, cells), BF16), ((6, cells, cells), BF16), ((2, depth, depth), BF16)],
        name="operators",
    )
    idx, weight, grp, take, give, pack, add_up = call(
        tables_body,
        [
            ((tiles, LANES), jnp.int32),
            ((tiles, LANES), F32),
            ((tiles // 2, LANES), jnp.int32),
            ((tiles, slots), BF16),
            ((slots, tiles), BF16),
            ((slots, cells), BF16),
            ((cells, slots), BF16),
        ],
        offsets, fractions, tile_group.reshape(1, tiles), tile_slot.reshape(1, tiles),
        send_index.reshape(1, slots),
        scratch=[pltpu.VMEM((tiles, LANES), jnp.int32)],
        name="tables",
    )
    halo = own.astype(HALO)
    before, after = shifted(halo, "cx")
    field, sent = call(
        first_body, [((cells, depth), F32), ((cells, depth), HALO)], own, before, after, hx,
        name="along_x",
    )
    before, after = shifted(sent, "cy")
    dens, packed = call(
        density_body, [((cells, depth), F32), ((slots, depth), BF16)],
        field, before, after, hy, hz, pack, name="density",
    )
    got = lax.all_to_all(packed, axes, split_axis=0, concat_axis=0, tiled=True)
    pred, grad = call(
        cone_body, [((groups, star_tile), F32), ((slots, depth), BF16)],
        got, response, idx, weight, grp, take, give,
        observed.reshape(groups, star_tile), sigma.reshape(groups, star_tile),
        scratch=[
            pltpu.VMEM((tiles, LANES), F32),
            pltpu.VMEM((tiles // 2, LANES), F32),
            pltpu.VMEM((tiles, LANES), F32),
            pltpu.VMEM((tiles * (depth // LANES), LANES), F32),
        ],
        limit=40,
        name="cones",
    )
    back = lax.all_to_all(grad, axes, split_axis=0, concat_axis=0, tiled=True)
    field, sent = call(
        owner_body, [((cells, depth), F32), ((cells, depth), BF16)], add_up, back, dens, hz,
        name="owners",
    )
    before, after = shifted(sent, "cy")
    field, sent = call(
        first_body, [((cells, depth), F32), ((cells, depth), BF16)], field, before, after, hy,
        name="along_y",
    )
    before, after = shifted(sent, "cx")
    (gradient,) = call(
        last_body, [((cells, depth), F32)], field, before, after, hx, own, name="finish"
    )
    return gradient.reshape(rows_x, rows_y, depth), pred.reshape(-1)


def solution(mesh):
    both = ("cx", "cy")
    placed = (
        P("cx", "cy", None),
        P(both),
        P(both),
        P(both, None, None),
        P(None, both),
        P(None, both),
        P(both),
        P(both),
        P(both, None, None),
    )
    return jax.shard_map(
        on_device,
        mesh=mesh,
        in_specs=placed,
        out_specs=(P("cx", "cy", None), P(both)),
        check_vma=False,
    )
```

time: 981 us -> 99.4 us (0.10)
  other arithmetic: 488 us -> 0.97 us
  local copies, waits for them, and re-layouts: 407 us -> 9.74 us
  blocking collectives: 0 us -> 27.4 us
  Pallas kernels: 0 us -> 27.1 us
  waiting for transfers between devices: 37.7 us -> 12 us
  matrix products: 14.2 us -> 0 us
    gather x3 -> x0, local copies, waits for them, and re-layouts: 403 us -> none  [the longest x1 200 us: on_device(): upper = received[sample_at + 1].astype(jnp.float32)]
    scatter-add x3 -> x0, other arithmetic: 350 us -> none  [the longest x1 175 us: on_device(): flat_grad = flat_grad.at[sample_at + 1].add(fractions * back)]
    add x5 -> x0, other arithmetic: 111 us -> none  [the longest x4 87.6 us: taps_over(): summed + kernel[shift_at] * lax.slice_in_dim(widened, shift_at, shift_at...]
    all_to_all x0 -> x2, blocking collectives: none -> 27.4 us  [the longest x1 14.7 us: on_device(): got = lax.all_to_all(packed, axes, split_axis=0, concat_axis=0, tiled=True)]
    pallas_call x0 -> x8, Pallas kernels: none -> 27.1 us  [call(): pl.pallas_call(body, out_shape=shapes, in_specs=[pl.BlockSpec(memory_spac...]
    convert_element_type x3 -> x1, other arithmetic: 22.9 us -> 0.97 us  [on_device(): halo = own.astype(HALO)]
    all_to_all x2 -> x0, waiting for transfers between devices: 17.6 us -> none  [the longest x1 8.84 us: on_device(): lax.all_to_all(packed, ('cx', 'cy'), split_axis=0, concat_axis=0, tiled=T...]
    dot_general x4 -> x0, matrix products: 14.2 us -> none  [the longest x1 7.79 us: on_device(): jnp.einsum('tms,ts->mt', response, tile_resid, preferred_element_type=jnp...]
  transfers between devices with their start and end apart: 10 -> 8, of which waited for: 9 -> 6; matrix products, arithmetic and copies ran while one was open for 1% -> 1% of each run, Pallas kernels for 0% -> 2%
where the time goes in v1:
time: 99.4 us; the launch traced here: 98.8 us
  blocking collectives  27.4 us (28%)
  Pallas kernels  27.1 us (27%)
  starting transfers between devices  20.8 us (21%)
  waiting for transfers between devices  12 us (12%)
  local copies, waits for them, and re-layouts  9.74 us (10%)
    pallas_call x8, Pallas kernels, call(): pl.pallas_call(body, out_shape=shapes, in_specs=[pl.BlockSpec(memory_spac...  27.1 us
    ppermute x8, starting transfers between devices, shifted(): return (lax.ppermute(values, axis, up), lax.ppermute(values, axis, down))  20.8 us
    all_to_all x1, blocking collectives, on_device(): got = lax.all_to_all(packed, axes, split_axis=0, concat_axis=0, tiled=True)  14.7 us
    all_to_all x1, blocking collectives, on_device(): back = lax.all_to_all(grad, axes, split_axis=0, concat_axis=0, tiled=True)  12.8 us
    ppermute x8, waiting for transfers between devices, shifted(): return (lax.ppermute(values, axis, up), lax.ppermute(values, axis, down))  12 us
    unnamed x19, local copies, waits for them, and re-layouts  9.65 us
  transfers between devices with their start and end apart: 8, of which 6 were waited for; matrix products, arithmetic and copies ran while one was open for 1% of the time, Pallas kernels for 2%

profile of v1, /device:TPU:12, one launch (start us, length us, event | category | flops | bytes accessed | tf_op | source)
XLA Modules:
  0.0 98.8 jit_solution(4441486095510806161)
XLA Ops:
  0.6 1.0 bitcast_convert_fusion
  1.6 2.4 %collective-permute-start.1 = (bf16[256,256]{1,0:T(8,128)(2,1)S(1)}, bf16[256,256]{1,0:T(8,128)(2,1)S(1)}, u32[]{:S(2)}, u32[]{:S(2)}) collective-permute-start(bf16[256,256]{1,0:T(8,128)(2,1)S(1)} %bitcast_convert_fusion), channel_id=1, source_target_pairs={{8,0},{16,8},{24,16},{9,1},{17,9},{25,17},{10,2},{18,10},{26,18},{... | collective-permute-start | bytes 393224 | tf_op jit(solution)/shard_map/ppermute | solution.py:263
  4.0 3.5 %collective-permute-start = (bf16[256,256]{1,0:T(8,128)(2,1)S(1)}, bf16[256,256]{1,0:T(8,128)(2,1)S(1)}, u32[]{:S(2)}, u32[]{:S(2)}) collective-permute-start(bf16[256,256]{1,0:T(8,128)(2,1)S(1)} %bitcast_convert_fusion), channel_id=1, source_target_pairs={{0,8},{8,16},{16,24},{1,9},{9,17},{17,25},{2,10},{10,18},{18,26},{... | collective-permute-start | bytes 393224 | tf_op jit(solution)/shard_map/ppermute | solution.py:263
  7.5 0.9 operators.1
  8.4 0.3 collective-permute-done.1.after_ref
  8.7 2.1 %collective-permute-done.before_ref = bf16[256,256]{1,0:T(8,128)(2,1)S(1)} collective-permute-done((bf16[256,256]{1,0:T(8,128)(2,1)S(1)}, bf16[256,256]{1,0:T(8,128)(2,1)S(1)}, u32[]{:S(2)}, u32[]{:S(2)}) %collective-permute-start) | collective-permute-done | bytes 131104 | tf_op jit(solution)/shard_map/ppermute | solution.py:263
  10.8 0.0 copy-start.1
  10.8 0.9 copy-done.1
  11.8 0.0 copy-start.2
  11.8 0.4 along_x.1
  12.2 1.9 %collective-permute-start.3 = (bf16[256,256]{1,0:T(8,128)(2,1)S(1)}, bf16[256,256]{1,0:T(8,128)(2,1)S(1)}, u32[]{:S(2)}, u32[]{:S(2)}) collective-permute-start(bf16[256,256]{1,0:T(8,128)(2,1)S(1)} %get-tuple-element.25), channel_id=1, source_target_pairs={{1,0},{2,1},{3,2},{4,3},{5,4},{6,5},{7,6},{9,8},{10,9},{11,10},{12... | collective-permute-start | bytes 393224 | tf_op jit(solution)/shard_map/ppermute | solution.py:263
  14.1 2.4 %collective-permute-start.2 = (bf16[256,256]{1,0:T(8,128)(2,1)S(1)}, bf16[256,256]{1,0:T(8,128)(2,1)S(1)}, u32[]{:S(2)}, u32[]{:S(2)}) collective-permute-start(bf16[256,256]{1,0:T(8,128)(2,1)S(1)} %get-tuple-element.25), channel_id=1, source_target_pairs={{0,1},{1,2},{2,3},{3,4},{4,5},{5,6},{6,7},{8,9},{9,10},{10,11},{11... | collective-permute-start | bytes 393224 | tf_op jit(solution)/shard_map/ppermute | solution.py:263
  16.5 0.8 copy.12
  17.3 0.1 reshape.34.send_ref
  17.4 0.0 copy-start.3
  17.4 0.9 copy-done.3
  18.3 0.0 copy-start.4
  18.3 0.9 copy-done.4
  19.2 0.0 copy-start.7
  19.2 0.7 copy-done.7
  19.9 0.0 copy-start.8
  19.9 0.7 copy-done.8
  20.6 0.7 tables.1
  21.3 0.0 collective-permute-done.3.after_ref
  21.3 0.0 collective-permute-done.2.before_ref
  21.3 1.1 %density.1 = (f32[256,256]{1,0:T(8,128)S(1)}, bf16[512,256]{1,0:T(8,128)(2,1)S(1)}) custom-call(f32[256,256]{1,0:T(8,128)S(1)} %get-tuple-element.24.own_ref, bf16[256,256]{1,0:T(8,128)(2,1)S(1)} %collective-permute-done.2.before_ref, bf16[256,256]{1,0:T(8,128)(2,1)S(1)} %collective-permute-done.3.after_ref, ...), custom_call_target="tpu_custom_call" | custom-call | bytes 2359296 | tf_op jit(solution)/shard_map/density/pallas_call | solution.py:61
  22.4 14.7 %all_to_all.22 = bf16[32,16,256]{2,1,0:T(8,128)(2,1)S(1)} all-to-all(bf16[32,16,256]{2,1,0:T(8,128)(2,1)S(1)} %bitcast.17), channel_id=1, replica_groups=mesh['cx'=4,'cy'=8] {'cx','cy'}, dimensions={0} | all-to-all | bytes 524288 | tf_op jit(solution)/shard_map/all_to_all | solution.py:310
  37.1 0.0 copy-start
  37.1 3.4 %copy-done = bf16[512,64,128]{2,1,0:T(8,128)(2,1)S(1)} copy-done((bf16[512,64,128]{2,1,0:T(8,128)(2,1)S(1)}, bf16[512,64,128]{2,1,0:T(8,128)(2,1)}, u32[]{:S(2)}) %copy-start) | copy-done | bytes 8388632
  40.4 0.0 copy-start.5
  40.4 0.7 copy-done.5
  41.1 0.0 copy-start.6
  41.1 0.7 copy-done.6
  41.8 21.9 %cones.1 = (f32[8,128]{1,0:T(8,128)}, bf16[512,256]{1,0:T(8,128)(2,1)S(1)}) custom-call(bf16[512,256]{1,0:T(8,128)(2,1)S(1)} %bitcast.14, bf16[512,64,128]{2,1,0:T(8,128)(2,1)S(1)} %copy-done, s32[512,128]{1,0:T(8,128)S(1)} %get-tuple-element.30.idx_ref, f32[512,128]{1,0:T(8,128)S(1)} %get-tuple-element.31.w_ref, s32[256,128]{1,0:T(8,128)S(1)} %get-tuple-element.32.grp_ref, ...), custom_call_target="tpu_custom_call" | custom-call | bytes 10629120 | tf_op jit(solution)/shard_map/cones/pallas_call | solution.py:61
  63.7 12.8 %all_to_all.23 = bf16[32,16,256]{2,1,0:T(8,128)(2,1)S(1)} all-to-all(bf16[32,16,256]{2,1,0:T(8,128)(2,1)S(1)} %bitcast.16), channel_id=1, replica_groups=mesh['cx'=4,'cy'=8] {'cx','cy'}, dimensions={0} | all-to-all | bytes 524288 | tf_op jit(solution)/shard_map/all_to_all | solution.py:324
  76.5 0.5 owners.1
  77.0 2.9 %collective-permute-start.5 = (bf16[256,256]{1,0:T(8,128)(2,1)S(1)}, bf16[256,256]{1,0:T(8,128)(2,1)S(1)}, u32[]{:S(2)}, u32[]{:S(2)}) collective-permute-start(bf16[256,256]{1,0:T(8,128)(2,1)S(1)} %get-tuple-element.38), channel_id=1, source_target_pairs={{1,0},{2,1},{3,2},{4,3},{5,4},{6,5},{7,6},{9,8},{10,9},{11,10},{12... | collective-permute-start | bytes 393224 | tf_op jit(solution)/shard_map/ppermute | solution.py:263
  80.0 1.9 %collective-permute-start.4 = (bf16[256,256]{1,0:T(8,128)(2,1)S(1)}, bf16[256,256]{1,0:T(8,128)(2,1)S(1)}, u32[]{:S(2)}, u32[]{:S(2)}) collective-permute-start(bf16[256,256]{1,0:T(8,128)(2,1)S(1)} %get-tuple-element.38), channel_id=1, source_target_pairs={{0,1},{1,2},{2,3},{3,4},{4,5},{5,6},{6,7},{8,9},{9,10},{10,11},{11... | collective-permute-start | bytes 393224 | tf_op jit(solution)/shard_map/ppermute | solution.py:263
  81.9 0.6 collective-permute-done.5.after_ref
  82.5 4.7 %collective-permute-done.4.before_ref = bf16[256,256]{1,0:T(8,128)(2,1)S(1)} collective-permute-done((bf16[256,256]{1,0:T(8,128)(2,1)S(1)}, bf16[256,256]{1,0:T(8,128)(2,1)S(1)}, u32[]{:S(2)}, u32[]{:S(2)}) %collective-permute-start.4) | collective-permute-done | bytes 131104 | tf_op jit(solution)/shard_map/ppermute | solution.py:263
  87.1 0.4 along_y.1
  87.6 3.3 %collective-permute-start.7 = (bf16[256,256]{1,0:T(8,128)(2,1)S(1)}, bf16[256,256]{1,0:T(8,128)(2,1)S(1)}, u32[]{:S(2)}, u32[]{:S(2)}) collective-permute-start(bf16[256,256]{1,0:T(8,128)(2,1)S(1)} %get-tuple-element.40), channel_id=1, source_target_pairs={{8,0},{16,8},{24,16},{9,1},{17,9},{25,17},{10,2},{18,10},{26,18},{... | collective-permute-start | bytes 393224 | tf_op jit(solution)/shard_map/ppermute | solution.py:263
  90.8 2.6 %collective-permute-start.6 = (bf16[256,256]{1,0:T(8,128)(2,1)S(1)}, bf16[256,256]{1,0:T(8,128)(2,1)S(1)}, u32[]{:S(2)}, u32[]{:S(2)}) collective-permute-start(bf16[256,256]{1,0:T(8,128)(2,1)S(1)} %get-tuple-element.40), channel_id=1, source_target_pairs={{0,8},{8,16},{16,24},{1,9},{9,17},{17,25},{2,10},{10,18},{18,26},{... | collective-permute-start | bytes 393224 | tf_op jit(solution)/shard_map/ppermute | solution.py:263
  93.4 1.0 %collective-permute-done.7.after_ref = bf16[256,256]{1,0:T(8,128)(2,1)S(1)} collective-permute-done((bf16[256,256]{1,0:T(8,128)(2,1)S(1)}, bf16[256,256]{1,0:T(8,128)(2,1)S(1)}, u32[]{:S(2)}, u32[]{:S(2)}) %collective-permute-start.7) | collective-permute-done | bytes 131104 | tf_op jit(solution)/shard_map/ppermute | solution.py:263
  94.4 3.3 %collective-permute-done.6.before_ref = bf16[256,256]{1,0:T(8,128)(2,1)S(1)} collective-permute-done((bf16[256,256]{1,0:T(8,128)(2,1)S(1)}, bf16[256,256]{1,0:T(8,128)(2,1)S(1)}, u32[]{:S(2)}, u32[]{:S(2)}) %collective-permute-start.6) | collective-permute-done | bytes 131104 | tf_op jit(solution)/shard_map/ppermute | solution.py:263
  97.7 0.0 copy-done.2
  97.7 1.1 %finish.1 = f32[256,256]{1,0:T(8,128)} custom-call(f32[256,256]{1,0:T(8,128)S(1)} %get-tuple-element.39.own_ref, bf16[256,256]{1,0:T(8,128)(2,1)S(1)} %collective-permute-done.6.before_ref, bf16[256,256]{1,0:T(8,128)(2,1)S(1)} %collective-permute-done.7.after_ref, bf16[6,256,256]{2,1,0:T(8,128)(2,1)S(1)} %get-tuple-element.23.mats_ref, f32[256,256]{1,0:T(8,128)S(1)} %bitcast.13), custom_call_target="tpu_custom_call" | custom-call | bytes 1835008 | tf_op jit(solution)/shard_map/finish/pallas_call | solution.py:61
Async XLA Ops:
  1.6 7.1 %collective-permute-start.1 = (bf16[256,256]{1,0:T(8,128)(2,1)S(1)}, bf16[256,256]{1,0:T(8,128)(2,1)S(1)}, u32[]{:S(2)}, u32[]{:S(2)}) collective-permute-start(bf16[256,256]{1,0:T(8,128)(2,1)S(1)} %bitcast_convert_fusion), channel_id=1, source_target_pairs={{8,0},{16,8},{24,16},{9,1},{17,9},{25,17},{10,2},{18,10},{26,18},{... | collective-permute-start | bytes 393224 | tf_op jit(solution)/shard_map/ppermute | solution.py:263
  4.0 6.9 %collective-permute-start = (bf16[256,256]{1,0:T(8,128)(2,1)S(1)}, bf16[256,256]{1,0:T(8,128)(2,1)S(1)}, u32[]{:S(2)}, u32[]{:S(2)}) collective-permute-start(bf16[256,256]{1,0:T(8,128)(2,1)S(1)} %bitcast_convert_fusion), channel_id=1, source_target_pairs={{0,8},{8,16},{16,24},{1,9},{9,17},{17,25},{2,10},{10,18},{18,26},{... | collective-permute-start | bytes 393224 | tf_op jit(solution)/shard_map/ppermute | solution.py:263
  10.8 1.0 copy-start.1
  11.8 85.9 %copy-start.2 = (f32[16,16,256]{2,1,0:T(8,128)S(1)}, f32[16,16,256]{2,1,0:T(8,128)}, u32[]{:S(2)}) copy-start(f32[16,16,256]{2,1,0:T(8,128)} %param.9) | copy-start | bytes 786436
  12.2 9.1 %collective-permute-start.3 = (bf16[256,256]{1,0:T(8,128)(2,1)S(1)}, bf16[256,256]{1,0:T(8,128)(2,1)S(1)}, u32[]{:S(2)}, u32[]{:S(2)}) collective-permute-start(bf16[256,256]{1,0:T(8,128)(2,1)S(1)} %get-tuple-element.25), channel_id=1, source_target_pairs={{1,0},{2,1},{3,2},{4,3},{5,4},{6,5},{7,6},{9,8},{10,9},{11,10},{12... | collective-permute-start | bytes 393224 | tf_op jit(solution)/shard_map/ppermute | solution.py:263
  14.1 7.2 %collective-permute-start.2 = (bf16[256,256]{1,0:T(8,128)(2,1)S(1)}, bf16[256,256]{1,0:T(8,128)(2,1)S(1)}, u32[]{:S(2)}, u32[]{:S(2)}) collective-permute-start(bf16[256,256]{1,0:T(8,128)(2,1)S(1)} %get-tuple-element.25), channel_id=1, source_target_pairs={{0,1},{1,2},{2,3},{3,4},{4,5},{5,6},{6,7},{8,9},{9,10},{10,11},{11... | collective-permute-start | bytes 393224 | tf_op jit(solution)/shard_map/ppermute | solution.py:263
  17.4 0.9 copy-start.3
  18.3 0.9 copy-start.4
  19.2 0.7 copy-start.7
  19.9 0.7 copy-start.8
  37.1 3.4 %copy-start = (bf16[512,64,128]{2,1,0:T(8,128)(2,1)S(1)}, bf16[512,64,128]{2,1,0:T(8,128)(2,1)}, u32[]{:S(2)}) copy-start(bf16[512,64,128]{2,1,0:T(8,128)(2,1)} %resp_ref.1) | copy-start | bytes 25165828
  40.4 0.7 copy-start.5
  41.1 0.7 copy-start.6
  77.0 5.4 %collective-permute-start.5 = (bf16[256,256]{1,0:T(8,128)(2,1)S(1)}, bf16[256,256]{1,0:T(8,128)(2,1)S(1)}, u32[]{:S(2)}, u32[]{:S(2)}) collective-permute-start(bf16[256,256]{1,0:T(8,128)(2,1)S(1)} %get-tuple-element.38), channel_id=1, source_target_pairs={{1,0},{2,1},{3,2},{4,3},{5,4},{6,5},{7,6},{9,8},{10,9},{11,10},{12... | collective-permute-start | bytes 393224 | tf_op jit(solution)/shard_map/ppermute | solution.py:263
  80.0 7.2 %collective-permute-start.4 = (bf16[256,256]{1,0:T(8,128)(2,1)S(1)}, bf16[256,256]{1,0:T(8,128)(2,1)S(1)}, u32[]{:S(2)}, u32[]{:S(2)}) collective-permute-start(bf16[256,256]{1,0:T(8,128)(2,1)S(1)} %get-tuple-element.38), channel_id=1, source_target_pairs={{0,1},{1,2},{2,3},{3,4},{4,5},{5,6},{6,7},{8,9},{9,10},{10,11},{11... | collective-permute-start | bytes 393224 | tf_op jit(solution)/shard_map/ppermute | solution.py:263
  87.6 6.9 %collective-permute-start.7 = (bf16[256,256]{1,0:T(8,128)(2,1)S(1)}, bf16[256,256]{1,0:T(8,128)(2,1)S(1)}, u32[]{:S(2)}, u32[]{:S(2)}) collective-permute-start(bf16[256,256]{1,0:T(8,128)(2,1)S(1)} %get-tuple-element.40), channel_id=1, source_target_pairs={{8,0},{16,8},{24,16},{9,1},{17,9},{25,17},{10,2},{18,10},{26,18},{... | collective-permute-start | bytes 393224 | tf_op jit(solution)/shard_map/ppermute | solution.py:263
  90.8 6.9 %collective-permute-start.6 = (bf16[256,256]{1,0:T(8,128)(2,1)S(1)}, bf16[256,256]{1,0:T(8,128)(2,1)S(1)}, u32[]{:S(2)}, u32[]{:S(2)}) collective-permute-start(bf16[256,256]{1,0:T(8,128)(2,1)S(1)} %get-tuple-element.40), channel_id=1, source_target_pairs={{0,8},{8,16},{16,24},{1,9},{9,17},{17,25},{2,10},{10,18},{18,26},{... | collective-permute-start | bytes 393224 | tf_op jit(solution)/shard_map/ppermute | solution.py:263

commit v2 on v1

--- a/solution.py
+++ b/solution.py
@@ -12,7 +12,8 @@
 LANES = 128
 F32 = jnp.float32
 BF16 = jnp.bfloat16
-HALO = BF16
+PREDICT_PAIRS = 64
+BACK_PAIRS = 64
 
 
 def tap_scale():
@@ -53,15 +54,17 @@
     return mm(high, mat_high) + (mm(low, mat_high) + mm(high, mat_low))
 
 
-def call(body, outs, *args, scratch=(), limit=16, flops=0, name=None):
+def call(body, outs, *args, scratch=(), limit=16, flops=0, name=None, space=pltpu.VMEM):
     shapes = [jax.ShapeDtypeStruct(s, d) for s, d in outs]
+    if space is pltpu.HBM:
+        args = [pltpu.with_memory_space_constraint(a, pltpu.HBM) for a in args]
     moved = sum(math.prod(a.shape) * a.dtype.itemsize for a in args) + sum(
         math.prod(s.shape) * s.dtype.itemsize for s in shapes
     )
     return pl.pallas_call(
         body,
         out_shape=shapes,
-        in_specs=[pl.BlockSpec(memory_space=pltpu.VMEM)] * len(args),
+        in_specs=[pl.BlockSpec(memory_space=space)] * len(args),
         out_specs=[pl.BlockSpec(memory_space=pltpu.VMEM)] * len(shapes),
         scratch_shapes=list(scratch),
         compiler_params=pltpu.CompilerParams(vmem_limit_bytes=limit << 20),
@@ -76,16 +79,18 @@
     return jnp.where(kept & (jnp.abs(distance) <= REACH), value, 0.0)
 
 
-def operators_body(rows_x, rows_y, depth, hx_ref, hy_ref, hz_ref):
+def operators(rows_x, rows_y, depth, hx_ref, hy_ref, hz_ref):
     cells = rows_x * rows_y
     out = iota((cells, cells), 0)
     inp = iota((cells, cells), 1)
     out_x, out_y = out // rows_y, out % rows_y
     inp_x, inp_y = inp // rows_y, inp % rows_y
-    for at, block in enumerate((0, 1, -1)):
-        high, low = split(taps_matrix(out_x - inp_x + block * rows_x, out_y == inp_y))
+    near_x = 2 * lax.rem(lax.axis_index("cx"), 2) - 1
+    near_y = 2 * lax.rem(lax.axis_index("cy"), 2) - 1
+    for at, side in enumerate((0, 1, -1)):
+        high, low = split(taps_matrix(out_x - inp_x + side * near_x * rows_x, out_y == inp_y))
         hx_ref[2 * at], hx_ref[2 * at + 1] = high, low
-        high, low = split(taps_matrix(out_y - inp_y + block * rows_y, out_x == inp_x))
+        high, low = split(taps_matrix(out_y - inp_y + side * near_y * rows_y, out_x == inp_x))
         hy_ref[2 * at], hy_ref[2 * at + 1] = high, low
     shift = iota((depth, depth), 0) - iota((depth, depth), 1)
     high, low = split(taps_matrix(shift, shift == shift))
@@ -96,10 +101,29 @@
     return jnp.where(hits, 1.0, 0.0).astype(BF16)
 
 
-def tables_body(
-    off_ref, frac_ref, group_ref, slot_ref, send_ref,
-    idx_ref, w_ref, grp_ref, take_ref, give_ref, pack_ref, sum_ref, keep,
+def prepare_body(
+    rows_x, rows_y,
+    own_hbm, resp_hbm, off_hbm, frac_hbm, group_hbm, slot_hbm, send_hbm, obs_hbm, sig_hbm,
+    hx_ref, hy_ref, hz_ref, part_ref, resp_ref, obs_ref, var_ref,
+    idx_ref, w_ref, grp_ref, take_ref, give_ref, pack_ref, sum_ref,
+    own_ref, off_ref, frac_ref, group_ref, slot_ref, send_ref, sig_ref, keep, sems,
 ):
+    moves = (
+        (own_hbm, own_ref), (off_hbm, off_ref), (frac_hbm, frac_ref), (group_hbm, group_ref),
+        (slot_hbm, slot_ref), (send_hbm, send_ref), (obs_hbm, obs_ref), (sig_hbm, sig_ref),
+        (resp_hbm, resp_ref),
+    )
+    copies = [
+        pltpu.make_async_copy(src, dst, sems.at[at]) for at, (src, dst) in enumerate(moves)
+    ]
+    for copy in copies:
+        copy.start()
+    operators(rows_x, rows_y, hz_ref.shape[1], hx_ref, hy_ref, hz_ref)
+    for copy in copies[:-1]:
+        copy.wait()
+    part_ref[...] = apply_left(hx_ref[0], hx_ref[1], own_ref[...])
+    sig = sig_ref[...]
+    var_ref[...] = sig * sig
     tiles = off_ref.shape[1]
     slots = take_ref.shape[1]
     cells = pack_ref.shape[1]
@@ -122,23 +146,31 @@
     for at in range(0, cells, LANES):
         pack_ref[:, at : at + LANES] = one_hot(wide == iota((slots, LANES), 1) + at)
     sum_ref[...] = one_hot(jnp.broadcast_to(send, (cells, slots)) == iota((cells, slots), 0))
-
-
-def three(mats_ref, own, before, after):
-    total = apply_left(mats_ref[0], mats_ref[1], own)
-    total += apply_left(mats_ref[2], mats_ref[3], before)
-    return total + apply_left(mats_ref[4], mats_ref[5], after)
-
-
-def first_body(own_ref, before_ref, after_ref, mats_ref, out_ref, *sent_ref):
-    out = three(mats_ref, own_ref[...], before_ref[...], after_ref[...])
+    copies[-1].wait()
+
+
+def sides(mats_ref, near, far):
+    return apply_left(mats_ref[2], mats_ref[3], near) + apply_left(mats_ref[4], mats_ref[5], far)
+
+
+def three(mats_ref, own, near, far):
+    return apply_left(mats_ref[0], mats_ref[1], own) + sides(mats_ref, near, far)
+
+
+def join_body(part_ref, near_ref, far_ref, mats_ref, out_ref, sent_ref):
+    out = part_ref[...] + sides(mats_ref, near_ref[...], far_ref[...])
     out_ref[...] = out
-    for ref in sent_ref:
-        ref[...] = out.astype(ref.dtype)
-
-
-def density_body(own_ref, before_ref, after_ref, mats_ref, hz_ref, pack_ref, dens_ref, packed_ref):
-    out = three(mats_ref, own_ref[...], before_ref[...], after_ref[...])
+    sent_ref[...] = out.astype(sent_ref.dtype)
+
+
+def smooth_body(own_ref, near_ref, far_ref, mats_ref, out_ref, sent_ref):
+    out = three(mats_ref, own_ref[...], near_ref[...], far_ref[...])
+    out_ref[...] = out
+    sent_ref[...] = out.astype(sent_ref.dtype)
+
+
+def density_body(own_ref, near_ref, far_ref, mats_ref, hz_ref, pack_ref, dens_ref, packed_ref):
+    out = three(mats_ref, own_ref[...], near_ref[...], far_ref[...])
     dens = jnp.exp(apply_right(out, hz_ref[0], hz_ref[1]))
     dens_ref[...] = dens
     packed_ref[...] = mm(pack_ref[...], dens.astype(BF16)).astype(BF16)
@@ -151,22 +183,19 @@
     sent_ref[...] = out.astype(sent_ref.dtype)
 
 
-def last_body(own_ref, before_ref, after_ref, mats_ref, latent_ref, out_ref):
-    out_ref[...] = latent_ref[...] + three(mats_ref, own_ref[...], before_ref[...], after_ref[...])
+def last_body(own_ref, near_ref, far_ref, mats_ref, latent_ref, out_ref):
+    out_ref[...] = latent_ref[...] + three(mats_ref, own_ref[...], near_ref[...], far_ref[...])
 
 
 def cone_body(
-    got_ref, resp_ref, idx_ref, w_ref, grp_ref, take_ref, give_ref, obs_ref, sig_ref,
-    pred_ref, grad_ref, both, pairs, weights, cells,
+    got_ref, resp_ref, idx_ref, w_ref, grp_ref, take_ref, give_ref, obs_ref, var_ref,
+    pred_ref, grad_ref, both, pairs, cells,
 ):
     tiles, samples, star_tile = resp_ref.shape
     depth = got_ref.shape[1]
     groups = obs_ref.shape[0]
     half = LANES // 2
     layers = depth // LANES
-    step_pairs = 8
-    step_tiles = 2 * step_pairs
-    steps = tiles // step_tiles
     idx = idx_ref[...]
     columns = mm(take_ref[...], got_ref[...])
     value = jnp.zeros((tiles, LANES), F32)
@@ -181,40 +210,45 @@
     )
     group_at = iota((groups, LANES), 0)
 
-    def rows_of(ref, step):
-        return ref[pl.ds(pl.multiple_of(step * step_tiles, step_tiles), step_tiles)].reshape(
-            step_tiles * samples, star_tile
+    def rows_of(ref, step, count):
+        return ref[pl.ds(pl.multiple_of(step * count, count), count)].reshape(
+            count * samples, star_tile
         )
 
-    def pair_rows(ref, step):
-        return ref[pl.ds(pl.multiple_of(step * step_pairs, step_pairs), step_pairs), :]
+    def pair_rows(ref, step, count):
+        return ref[pl.ds(pl.multiple_of(step * count, count), count), :]
 
     def predict(step, total):
-        pair = pair_rows(pairs, step)
-        group = pair_rows(grp_ref, step)
+        pair = pair_rows(pairs, step, PREDICT_PAIRS)
+        group = pair_rows(grp_ref, step, PREDICT_PAIRS)
         left = [
             jnp.where(group[i : i + 1] == group_at, pair[i : i + 1], 0.0)
-            for i in range(step_pairs)
+            for i in range(PREDICT_PAIRS)
         ]
-        return total + mm(jnp.concatenate(left, axis=1).astype(BF16), rows_of(resp_ref, step))
-
-    pred = lax.fori_loop(0, steps, predict, jnp.zeros((groups, star_tile), F32))
+        left = jnp.concatenate(left, axis=1).astype(BF16)
+        return total + mm(left, rows_of(resp_ref, step, 2 * PREDICT_PAIRS))
+
+    pred = lax.fori_loop(
+        0, tiles // (2 * PREDICT_PAIRS), predict, jnp.zeros((groups, star_tile), F32)
+    )
     pred_ref[...] = pred
-    sig = sig_ref[...]
-    resid = ((pred - obs_ref[...]) / (sig * sig)).astype(BF16)
+    resid = ((pred - obs_ref[...]) / var_ref[...]).astype(BF16)
     rows = 2 * layers
     at_row = iota((2 * rows, LANES), 0)
     row_layer = at_row % layers
     row_tile = (at_row % rows) // layers
     row_high = at_row < rows
-    lane_first = iota((step_pairs, LANES), 1) < half
     level = [(iota((16, LANES), 0) + 16 * k).astype(F32).astype(BF16) for k in range(LANES // 16)]
     one = jnp.ones((16, LANES), BF16)
     zero = jnp.zeros((16, LANES), BF16)
 
+    step_pairs = BACK_PAIRS
+    step_tiles = 2 * step_pairs
+    lane_first = iota((step_pairs, LANES), 1) < half
+
     def backward(step, carry):
-        group = pair_rows(grp_ref, step)
-        back = mm_nt(resid, rows_of(resp_ref, step))
+        group = pair_rows(grp_ref, step, step_pairs)
+        back = mm_nt(resid, rows_of(resp_ref, step, step_tiles))
         picked = [
             jnp.sum(
                 jnp.where(group[i : i + 1] == group_at, back[:, i * LANES : (i + 1) * LANES], 0.0),
@@ -249,18 +283,22 @@
         cells[pl.ds(pl.multiple_of(step * count, count), count), :] = jnp.concatenate(made, axis=0)
         return carry
 
-    lax.fori_loop(0, steps, backward, 0)
+    lax.fori_loop(0, tiles // step_tiles, backward, 0)
     give = give_ref[...]
     for at in range(layers):
         high, low = split(cells[pl.ds(at, tiles, layers), :])
         grad_ref[:, at * LANES : (at + 1) * LANES] = (mm(give, high) + mm(give, low)).astype(BF16)
 
 
-def shifted(values, axis):
+def exchanged(values, axis):
     count = lax.axis_size(axis)
-    up = [(i, i + 1) for i in range(count - 1)]
-    down = [(i + 1, i) for i in range(count - 1)]
-    return lax.ppermute(values, axis, up), lax.ppermute(values, axis, down)
+    return [
+        lax.ppermute(
+            values, axis,
+            [pair for i in range(first, count - 1, 2) for pair in ((i, i + 1), (i + 1, i))],
+        )
+        for first in (0, 1)
+    ]
 
 
 def on_device(
@@ -274,15 +312,20 @@
     tiles, samples, star_tile = response.shape
     groups = observed.shape[0] // star_tile
     own = latent.reshape(cells, depth)
-
-    hx, hy, hz = call(
-        functools.partial(operators_body, rows_x, rows_y, depth),
-        [((6, cells, cells), BF16), ((6, cells, cells), BF16), ((2, depth, depth), BF16)],
-        name="operators",
-    )
-    idx, weight, grp, take, give, pack, add_up = call(
-        tables_body,
+    field_out = ((cells, depth), F32)
+    sent_out = ((cells, depth), BF16)
+
+    near, far = exchanged(own.astype(BF16), "cx")
+    hx, hy, hz, part, resp, obs, var, idx, weight, grp, take, give, pack, add_up = call(
+        functools.partial(prepare_body, rows_x, rows_y),
         [
+            ((6, cells, cells), BF16),
+            ((6, cells, cells), BF16),
+            ((2, depth, depth), BF16),
+            field_out,
+            (response.shape, BF16),
+            ((groups, star_tile), F32),
+            ((groups, star_tile), F32),
             ((tiles, LANES), jnp.int32),
             ((tiles, LANES), F32),
             ((tiles // 2, LANES), jnp.int32),
@@ -291,50 +334,50 @@
             ((slots, cells), BF16),
             ((cells, slots), BF16),
         ],
-        offsets, fractions, tile_group.reshape(1, tiles), tile_slot.reshape(1, tiles),
-        send_index.reshape(1, slots),
-        scratch=[pltpu.VMEM((tiles, LANES), jnp.int32)],
-        name="tables",
-    )
-    halo = own.astype(HALO)
-    before, after = shifted(halo, "cx")
-    field, sent = call(
-        first_body, [((cells, depth), F32), ((cells, depth), HALO)], own, before, after, hx,
-        name="along_x",
-    )
-    before, after = shifted(sent, "cy")
+        own, response, offsets, fractions,
+        tile_group.reshape(1, tiles), tile_slot.reshape(1, tiles), send_index.reshape(1, slots),
+        observed.reshape(groups, star_tile), sigma.reshape(groups, star_tile),
+        scratch=[
+            pltpu.VMEM((cells, depth), F32),
+            pltpu.VMEM((samples, tiles), jnp.int32),
+            pltpu.VMEM((samples, tiles), F32),
+            pltpu.VMEM((1, tiles), jnp.int32),
+            pltpu.VMEM((1, tiles), jnp.int32),
+            pltpu.VMEM((1, slots), jnp.int32),
+            pltpu.VMEM((groups, star_tile), F32),
+            pltpu.VMEM((tiles, LANES), jnp.int32),
+            pltpu.SemaphoreType.DMA((9,)),
+        ],
+        limit=20,
+        space=pltpu.HBM,
+        name="prepare",
+    )
+    field, sent = call(join_body, [field_out, sent_out], part, near, far, hx, name="along_x")
+    near, far = exchanged(sent, "cy")
     dens, packed = call(
-        density_body, [((cells, depth), F32), ((slots, depth), BF16)],
-        field, before, after, hy, hz, pack, name="density",
+        density_body, [field_out, ((slots, depth), BF16)],
+        field, near, far, hy, hz, pack, name="density",
     )
     got = lax.all_to_all(packed, axes, split_axis=0, concat_axis=0, tiled=True)
     pred, grad = call(
         cone_body, [((groups, star_tile), F32), ((slots, depth), BF16)],
-        got, response, idx, weight, grp, take, give,
-        observed.reshape(groups, star_tile), sigma.reshape(groups, star_tile),
+        got, resp, idx, weight, grp, take, give, obs, var,
         scratch=[
             pltpu.VMEM((tiles, LANES), F32),
             pltpu.VMEM((tiles // 2, LANES), F32),
-            pltpu.VMEM((tiles, LANES), F32),
             pltpu.VMEM((tiles * (depth // LANES), LANES), F32),
         ],
-        limit=40,
+        limit=20,
         name="cones",
     )
     back = lax.all_to_all(grad, axes, split_axis=0, concat_axis=0, tiled=True)
+    field, sent = call(owner_body, [field_out, sent_out], add_up, back, dens, hz, name="owners")
+    near, far = exchanged(sent, "cy")
     field, sent = call(
-        owner_body, [((cells, depth), F32), ((cells, depth), BF16)], add_up, back, dens, hz,
-        name="owners",
-    )
-    before, after = shifted(sent, "cy")
-    field, sent = call(
-        first_body, [((cells, depth), F32), ((cells, depth), BF16)], field, before, after, hy,
-        name="along_y",
-    )
-    before, after = shifted(sent, "cx")
-    (gradient,) = call(
-        last_body, [((cells, depth), F32)], field, before, after, hx, own, name="finish"
-    )
+        smooth_body, [field_out, sent_out], field, near, far, hy, name="along_y"
+    )
+    near, far = exchanged(sent, "cx")
+    (gradient,) = call(last_body, [field_out], field, near, far, hx, own, name="finish")
     return gradient.reshape(rows_x, rows_y, depth), pred.reshape(-1)
 
 

time: 99.4 us -> 73.6 us (0.74)
  Pallas kernels: 27.1 us -> 17.3 us
  local copies, waits for them, and re-layouts: 9.74 us -> 1.44 us
  starting transfers between devices: 20.8 us -> 12.8 us
  waiting for transfers between devices: 12 us -> 13.5 us
  blocking collectives: 27.4 us -> 26.2 us
    pallas_call x8 -> x7, Pallas kernels: 27.1 us -> 17.3 us  [call(): pl.pallas_call(body, out_shape=shapes, in_specs=[pl.BlockSpec(memory_spac...]
    unnamed x19 -> x3, local copies, waits for them, and re-layouts: 9.65 us -> 0.78 us
    ppermute x8, starting transfers between devices: 20.8 us -> 12.8 us  [exchanged(): lax.ppermute(values, axis, [pair for i in range(first, count - 1, 2) for...]
    ppermute x8, waiting for transfers between devices: 12 us -> 13.5 us  [exchanged(): lax.ppermute(values, axis, [pair for i in range(first, count - 1, 2) for...]
    all_to_all x1, blocking collectives: 14.7 us -> 13.4 us  [on_device(): got = lax.all_to_all(packed, axes, split_axis=0, concat_axis=0, tiled=True)]
  transfers between devices with their start and end apart: 8 -> 8, of which waited for: 6 -> 4; matrix products, arithmetic and copies ran while one was open for 1% -> 2% of each run, Pallas kernels for 2% -> 5%
where the time goes in v2:
time: 73.6 us; the launch traced here: 73 us
  blocking collectives  26.2 us (36%)
  Pallas kernels  17.3 us (24%)
  waiting for transfers between devices  13.5 us (18%)
  starting transfers between devices  12.8 us (17%)
  local copies, waits for them, and re-layouts  1.44 us (2%)
  other arithmetic  0.97 us (1%)
  between operations  0.75 us (1%)
    pallas_call x7, Pallas kernels, call(): pl.pallas_call(body, out_shape=shapes, in_specs=[pl.BlockSpec(memory_spac...  17.3 us
    ppermute x8, waiting for transfers between devices, exchanged(): lax.ppermute(values, axis, [pair for i in range(first, count - 1, 2) for...  13.5 us
    all_to_all x1, blocking collectives, on_device(): got = lax.all_to_all(packed, axes, split_axis=0, concat_axis=0, tiled=True)  13.4 us
    ppermute x8, starting transfers between devices, exchanged(): lax.ppermute(values, axis, [pair for i in range(first, count - 1, 2) for...  12.8 us
    all_to_all x1, blocking collectives, on_device(): back = lax.all_to_all(grad, axes, split_axis=0, concat_axis=0, tiled=True)  12.8 us
  transfers between devices with their start and end apart: 8, of which 4 were waited for; matrix products, arithmetic and copies ran while one was open for 2% of the time, Pallas kernels for 5%

profile of v2, /device:TPU:12, one launch (start us, length us, event | category | flops | bytes accessed | tf_op | source)
XLA Modules:
  0.0 73.0 jit_solution(13968566758023440426)
XLA Ops:
  0.6 1.0 %bitcast_convert_fusion = bf16[256,256]{1,0:T(8,128)(2,1)S(1)} fusion(f32[16,16,256]{2,1,0:T(8,128)} %param.9), kind=kLoop, calls=%fused_computation | loop fusion | flops 65536 | bytes 393216 | tf_op jit(solution)/shard_map/convert_element_type | solution.py:318
  1.6 3.5 %collective-permute-start.1 = (bf16[256,256]{1,0:T(8,128)(2,1)S(1)}, bf16[256,256]{1,0:T(8,128)(2,1)S(1)}, u32[]{:S(2)}, u32[]{:S(2)}) collective-permute-start(bf16[256,256]{1,0:T(8,128)(2,1)S(1)} %bitcast_convert_fusion), channel_id=1, source_target_pairs={{8,16},{16,8},{9,17},{17,9},{10,18},{18,10},{11,19},{19,11},{12,20... | collective-permute-start | bytes 393224 | tf_op jit(solution)/shard_map/ppermute | solution.py:296
  5.1 0.1 collective-permute-start
  5.2 0.8 %copy.12 = s32[1,32,16]{2,1,0:T(8,128)S(1)} copy(s32[1,32,16]{1,2,0:T(8,128)} %param.17) | data formatting | bytes 4096 | tf_op args[8]
  5.9 0.7 reshape.35.send_hbm
  6.6 3.8 %prepare.1 = (bf16[6,256,256]{2,1,0:T(8,128)(2,1)S(1)}, bf16[6,256,256]{2,1,0:T(8,128)(2,1)S(1)}, bf16[2,256,256]{2,1,0:T(8,128)(2,1)S(1)}, f32[256,256]{1,0:T(8...) custom-call(f32[256,256]{1,0:T(8,128)} %bitcast.12, ...), custom_call_target="tpu_custom_call" | custom-call | bytes 21649408 | tf_op jit(solution)/shard_map/prepare/pallas_call | solution.py:64
  10.4 0.0 collective-permute-done.1.far_ref
  10.4 0.0 collective-permute-done.near_ref
  10.4 0.0 copy-start
  10.4 0.3 along_x.1
  10.7 2.5 %collective-permute-start.3 = (bf16[256,256]{1,0:T(8,128)(2,1)S(1)}, bf16[256,256]{1,0:T(8,128)(2,1)S(1)}, u32[]{:S(2)}, u32[]{:S(2)}) collective-permute-start(bf16[256,256]{1,0:T(8,128)(2,1)S(1)} %get-tuple-element.30), channel_id=1, source_target_pairs={{1,2},{2,1},{3,4},{4,3},{5,6},{6,5},{9,10},{10,9},{11,12},{12,11},... | collective-permute-start | bytes 393224 | tf_op jit(solution)/shard_map/ppermute | solution.py:296
  13.3 1.1 %collective-permute-start.2 = (bf16[256,256]{1,0:T(8,128)(2,1)S(1)}, bf16[256,256]{1,0:T(8,128)(2,1)S(1)}, u32[]{:S(2)}, u32[]{:S(2)}) collective-permute-start(bf16[256,256]{1,0:T(8,128)(2,1)S(1)} %get-tuple-element.30), channel_id=1, source_target_pairs={{0,1},{1,0},{2,3},{3,2},{4,5},{5,4},{6,7},{7,6},{8,9},{9,8},{10,11... | collective-permute-start | bytes 393224 | tf_op jit(solution)/shard_map/ppermute | solution.py:296
  14.3 4.1 %collective-permute-done.3.far_ref = bf16[256,256]{1,0:T(8,128)(2,1)S(1)} collective-permute-done((bf16[256,256]{1,0:T(8,128)(2,1)S(1)}, bf16[256,256]{1,0:T(8,128)(2,1)S(1)}, u32[]{:S(2)}, u32[]{:S(2)}) %collective-permute-start.3) | collective-permute-done | bytes 131104 | tf_op jit(solution)/shard_map/ppermute | solution.py:296
  18.4 0.0 collective-permute-done.2.near_ref
  18.4 1.1 %density.1 = (f32[256,256]{1,0:T(8,128)S(1)}, bf16[512,256]{1,0:T(8,128)(2,1)S(1)}) custom-call(f32[256,256]{1,0:T(8,128)S(1)} %get-tuple-element.29.own_ref, bf16[256,256]{1,0:T(8,128)(2,1)S(1)} %collective-permute-done.2.near_ref, bf16[256,256]{1,0:T(8,128)(2,1)S(1)} %collective-permute-done.3.far_ref, ...), custom_call_target="tpu_custom_call" | custom-call | bytes 2359296 | tf_op jit(solution)/shard_map/density/pallas_call | solution.py:64
  19.5 13.4 %all_to_all.22 = bf16[32,16,256]{2,1,0:T(8,128)(2,1)S(1)} all-to-all(bf16[32,16,256]{2,1,0:T(8,128)(2,1)S(1)} %bitcast.17), channel_id=1, replica_groups=mesh['cx'=4,'cy'=8] {'cx','cy'}, dimensions={0} | all-to-all | bytes 524288 | tf_op jit(solution)/shard_map/all_to_all | solution.py:361
  32.9 10.1 %cones.1 = (f32[8,128]{1,0:T(8,128)}, bf16[512,256]{1,0:T(8,128)(2,1)S(1)}) custom-call(bf16[512,256]{1,0:T(8,128)(2,1)S(1)} %bitcast.14, bf16[512,64,128]{2,1,0:T(8,128)(2,1)S(1)} %get-tuple-element.35.resp_ref, s32[512,128]{1,0:T(8,128)S(1)} %get-tuple-element.36.idx_ref, f32[512,128]{1,0:T(8,128)S(1)} %get-tuple-element.37.w_ref, ...), custom_call_target="tpu_custom_call" | custom-call | bytes 10629120 | tf_op jit(solution)/shard_map/cones/pallas_call | solution.py:64
  43.0 12.8 %all_to_all.23 = bf16[32,16,256]{2,1,0:T(8,128)(2,1)S(1)} all-to-all(bf16[32,16,256]{2,1,0:T(8,128)(2,1)S(1)} %bitcast.16), channel_id=1, replica_groups=mesh['cx'=4,'cy'=8] {'cx','cy'}, dimensions={0} | all-to-all | bytes 524288 | tf_op jit(solution)/shard_map/all_to_all | solution.py:373
  55.8 0.5 owners.1
  56.3 2.9 %collective-permute-start.5 = (bf16[256,256]{1,0:T(8,128)(2,1)S(1)}, bf16[256,256]{1,0:T(8,128)(2,1)S(1)}, u32[]{:S(2)}, u32[]{:S(2)}) collective-permute-start(bf16[256,256]{1,0:T(8,128)(2,1)S(1)} %get-tuple-element.46), channel_id=1, source_target_pairs={{1,2},{2,1},{3,4},{4,3},{5,6},{6,5},{9,10},{10,9},{11,12},{12,11},... | collective-permute-start | bytes 393224 | tf_op jit(solution)/shard_map/ppermute | solution.py:296
  59.3 0.1 collective-permute-start.4
  59.3 4.8 %collective-permute-done.5.far_ref = bf16[256,256]{1,0:T(8,128)(2,1)S(1)} collective-permute-done((bf16[256,256]{1,0:T(8,128)(2,1)S(1)}, bf16[256,256]{1,0:T(8,128)(2,1)S(1)}, u32[]{:S(2)}, u32[]{:S(2)}) %collective-permute-start.5) | collective-permute-done | bytes 131104 | tf_op jit(solution)/shard_map/ppermute | solution.py:296
  64.1 0.0 collective-permute-done.4.near_ref
  64.2 0.4 along_y.1
  64.6 2.2 %collective-permute-start.7 = (bf16[256,256]{1,0:T(8,128)(2,1)S(1)}, bf16[256,256]{1,0:T(8,128)(2,1)S(1)}, u32[]{:S(2)}, u32[]{:S(2)}) collective-permute-start(bf16[256,256]{1,0:T(8,128)(2,1)S(1)} %get-tuple-element.48), channel_id=1, source_target_pairs={{8,16},{16,8},{9,17},{17,9},{10,18},{18,10},{11,19},{19,11},{12,20... | collective-permute-start | bytes 393224 | tf_op jit(solution)/shard_map/ppermute | solution.py:296
  66.8 0.4 collective-permute-start.6
  67.2 4.2 %collective-permute-done.7.far_ref = bf16[256,256]{1,0:T(8,128)(2,1)S(1)} collective-permute-done((bf16[256,256]{1,0:T(8,128)(2,1)S(1)}, bf16[256,256]{1,0:T(8,128)(2,1)S(1)}, u32[]{:S(2)}, u32[]{:S(2)}) %collective-permute-start.7) | collective-permute-done | bytes 131104 | tf_op jit(solution)/shard_map/ppermute | solution.py:296
  71.4 0.4 collective-permute-done.6.near_ref
  71.8 0.0 copy-done
  71.9 1.1 %finish.1 = f32[256,256]{1,0:T(8,128)} custom-call(f32[256,256]{1,0:T(8,128)S(1)} %get-tuple-element.47.own_ref, bf16[256,256]{1,0:T(8,128)(2,1)S(1)} %collective-permute-done.6.near_ref, bf16[256,256]{1,0:T(8,128)(2,1)S(1)} %collective-permute-done.7.far_ref, bf16[6,256,256]{2,1,0:T(8,128)(2,1)S(1)} %get-tuple-element.28.mats_ref, f32[256,256]{1,0:T(8,128)S(1)} %bitcast.13), custom_call_target="tpu_custom_call" | custom-call | bytes 1835008 | tf_op jit(solution)/shard_map/finish/pallas_call | solution.py:64
Async XLA Ops:
  1.6 8.8 %collective-permute-start.1 = (bf16[256,256]{1,0:T(8,128)(2,1)S(1)}, bf16[256,256]{1,0:T(8,128)(2,1)S(1)}, u32[]{:S(2)}, u32[]{:S(2)}) collective-permute-start(bf16[256,256]{1,0:T(8,128)(2,1)S(1)} %bitcast_convert_fusion), channel_id=1, source_target_pairs={{8,16},{16,8},{9,17},{17,9},{10,18},{18,10},{11,19},{19,11},{12,20... | collective-permute-start | bytes 393224 | tf_op jit(solution)/shard_map/ppermute | solution.py:296
  5.1 5.3 %collective-permute-start = (bf16[256,256]{1,0:T(8,128)(2,1)S(1)}, bf16[256,256]{1,0:T(8,128)(2,1)S(1)}, u32[]{:S(2)}, u32[]{:S(2)}) collective-permute-start(bf16[256,256]{1,0:T(8,128)(2,1)S(1)} %bitcast_convert_fusion), channel_id=1, source_target_pairs={{0,8},{8,0},{16,24},{24,16},{1,9},{9,1},{17,25},{25,17},{2,10},{10... | collective-permute-start | bytes 393224 | tf_op jit(solution)/shard_map/ppermute | solution.py:296
  10.4 61.4 %copy-start = (f32[16,16,256]{2,1,0:T(8,128)S(1)}, f32[16,16,256]{2,1,0:T(8,128)}, u32[]{:S(2)}) copy-start(f32[16,16,256]{2,1,0:T(8,128)} %param.9) | copy-start | bytes 786436
  10.7 7.7 %collective-permute-start.3 = (bf16[256,256]{1,0:T(8,128)(2,1)S(1)}, bf16[256,256]{1,0:T(8,128)(2,1)S(1)}, u32[]{:S(2)}, u32[]{:S(2)}) collective-permute-start(bf16[256,256]{1,0:T(8,128)(2,1)S(1)} %get-tuple-element.30), channel_id=1, source_target_pairs={{1,2},{2,1},{3,4},{4,3},{5,6},{6,5},{9,10},{10,9},{11,12},{12,11},... | collective-permute-start | bytes 393224 | tf_op jit(solution)/shard_map/ppermute | solution.py:296
  13.3 5.2 %collective-permute-start.2 = (bf16[256,256]{1,0:T(8,128)(2,1)S(1)}, bf16[256,256]{1,0:T(8,128)(2,1)S(1)}, u32[]{:S(2)}, u32[]{:S(2)}) collective-permute-start(bf16[256,256]{1,0:T(8,128)(2,1)S(1)} %get-tuple-element.30), channel_id=1, source_target_pairs={{0,1},{1,0},{2,3},{3,2},{4,5},{5,4},{6,7},{7,6},{8,9},{9,8},{10,11... | collective-permute-start | bytes 393224 | tf_op jit(solution)/shard_map/ppermute | solution.py:296
  56.3 7.8 %collective-permute-start.5 = (bf16[256,256]{1,0:T(8,128)(2,1)S(1)}, bf16[256,256]{1,0:T(8,128)(2,1)S(1)}, u32[]{:S(2)}, u32[]{:S(2)}) collective-permute-start(bf16[256,256]{1,0:T(8,128)(2,1)S(1)} %get-tuple-element.46), channel_id=1, source_target_pairs={{1,2},{2,1},{3,4},{4,3},{5,6},{6,5},{9,10},{10,9},{11,12},{12,11},... | collective-permute-start | bytes 393224 | tf_op jit(solution)/shard_map/ppermute | solution.py:296
  59.3 4.9 %collective-permute-start.4 = (bf16[256,256]{1,0:T(8,128)(2,1)S(1)}, bf16[256,256]{1,0:T(8,128)(2,1)S(1)}, u32[]{:S(2)}, u32[]{:S(2)}) collective-permute-start(bf16[256,256]{1,0:T(8,128)(2,1)S(1)} %get-tuple-element.46), channel_id=1, source_target_pairs={{0,1},{1,0},{2,3},{3,2},{4,5},{5,4},{6,7},{7,6},{8,9},{9,8},{10,11... | collective-permute-start | bytes 393224 | tf_op jit(solution)/shard_map/ppermute | solution.py:296
  64.6 6.9 %collective-permute-start.7 = (bf16[256,256]{1,0:T(8,128)(2,1)S(1)}, bf16[256,256]{1,0:T(8,128)(2,1)S(1)}, u32[]{:S(2)}, u32[]{:S(2)}) collective-permute-start(bf16[256,256]{1,0:T(8,128)(2,1)S(1)} %get-tuple-element.48), channel_id=1, source_target_pairs={{8,16},{16,8},{9,17},{17,9},{10,18},{18,10},{11,19},{19,11},{12,20... | collective-permute-start | bytes 393224 | tf_op jit(solution)/shard_map/ppermute | solution.py:296
  66.8 5.0 %collective-permute-start.6 = (bf16[256,256]{1,0:T(8,128)(2,1)S(1)}, bf16[256,256]{1,0:T(8,128)(2,1)S(1)}, u32[]{:S(2)}, u32[]{:S(2)}) collective-permute-start(bf16[256,256]{1,0:T(8,128)(2,1)S(1)} %get-tuple-element.48), channel_id=1, source_target_pairs={{0,8},{8,0},{16,24},{24,16},{1,9},{9,1},{17,25},{25,17},{2,10},{10... | collective-permute-start | bytes 393224 | tf_op jit(solution)/shard_map/ppermute | solution.py:296

commit v3 on v2

v3 whole, which is shorter than its diff:
```python
import functools
import math

import jax
import jax.numpy as jnp
from jax import lax
from jax.experimental import pallas as pl
from jax.experimental.pallas import tpu as pltpu
from jax.sharding import PartitionSpec as P

REACH = 16
LANES = 128
F32 = jnp.float32
BF16 = jnp.bfloat16
PREDICT_PAIRS = 64
BACK_PAIRS = 64
PART = 64


def tap_scale():
    total = 0.0
    for shift in range(-REACH, REACH + 1):
        a = math.sqrt(3.0) * abs(shift) / 8.0
        total += ((1.0 + a) * math.exp(-a)) ** 2
    return 0.8 / math.sqrt(total)


def split(values):
    high = values.astype(BF16)
    low = (values - high.astype(F32)).astype(BF16)
    return high, low


def mm(a, b):
    return jnp.dot(a, b, preferred_element_type=F32)


def mm_nt(a, b):
    return lax.dot_general(a, b, (((1,), (1,)), ((), ())), preferred_element_type=F32)


def iota(shape, dim):
    return lax.broadcasted_iota(jnp.int32, shape, dim)


def apply_left(mat_high, mat_low, values):
    if values.dtype == BF16:
        return mm(mat_high, values) + mm(mat_low, values)
    high, low = split(values)
    return mm(mat_high, high) + (mm(mat_high, low) + mm(mat_low, high))


def apply_right(values, mat_high, mat_low):
    high, low = split(values)
    return mm(high, mat_high) + (mm(low, mat_high) + mm(high, mat_low))


def hbm(array):
    return pltpu.with_memory_space_constraint(array, pltpu.HBM)


def is_hbm(array):
    return getattr(jax.typeof(array), "memory_space", None) is pltpu.HBM


def call(body, outs, *args, scratch=(), limit=16, name=None):
    shapes = [jax.ShapeDtypeStruct(s, d) for s, d in outs]
    moved = sum(math.prod(a.shape) * a.dtype.itemsize for a in args) + sum(
        math.prod(s.shape) * s.dtype.itemsize for s in shapes
    )
    return pl.pallas_call(
        body,
        out_shape=shapes,
        in_specs=[
            pl.BlockSpec(memory_space=pltpu.HBM if is_hbm(a) else pltpu.VMEM) for a in args
        ],
        out_specs=[pl.BlockSpec(memory_space=pltpu.VMEM)] * len(shapes),
        scratch_shapes=list(scratch),
        compiler_params=pltpu.CompilerParams(vmem_limit_bytes=limit << 20),
        cost_estimate=pl.CostEstimate(flops=0, bytes_accessed=moved, transcendentals=0),
        name=name,
    )(*args)


def taps_matrix(distance, kept):
    a = (math.sqrt(3.0) / 8.0) * jnp.abs(distance).astype(F32)
    value = (tap_scale() * (1.0 + a)) * jnp.exp(-a)
    return jnp.where(kept & (jnp.abs(distance) <= REACH), value, 0.0)


def operators(rows_x, rows_y, depth, hx_ref, hy_ref, hz_ref):
    cells = rows_x * rows_y
    out = iota((cells, cells), 0)
    inp = iota((cells, cells), 1)
    out_x, out_y = out // rows_y, out % rows_y
    inp_x, inp_y = inp // rows_y, inp % rows_y
    near_x = 2 * lax.rem(lax.axis_index("cx"), 2) - 1
    near_y = 2 * lax.rem(lax.axis_index("cy"), 2) - 1
    for at, side in enumerate((0, 1, -1)):
        high, low = split(taps_matrix(out_x - inp_x + side * near_x * rows_x, out_y == inp_y))
        hx_ref[2 * at], hx_ref[2 * at + 1] = high, low
        high, low = split(taps_matrix(out_y - inp_y + side * near_y * rows_y, out_x == inp_x))
        hy_ref[2 * at], hy_ref[2 * at + 1] = high, low
    shift = iota((depth, depth), 0) - iota((depth, depth), 1)
    high, low = split(taps_matrix(shift, shift == shift))
    hz_ref[0], hz_ref[1] = high, low


def one_hot(hits):
    return jnp.where(hits, 1.0, 0.0).astype(BF16)


def fetch(moves, sems):
    copies = [
        pltpu.make_async_copy(src, dst, sems.at[at]) for at, (src, dst) in enumerate(moves)
    ]
    for copy in copies:
        copy.start()
    return copies


def operators_body(
    rows_x, rows_y, own_hbm, resp_hbm, after_hbm,
    hx_ref, hy_ref, hz_ref, part_ref, resp_ref, own_ref, sems,
):
    count = resp_ref.shape[0]
    copies = fetch([(own_hbm, own_ref), (resp_hbm.at[pl.ds(0, count)], resp_ref)], sems)
    operators(rows_x, rows_y, hz_ref.shape[1], hx_ref, hy_ref, hz_ref)
    copies[0].wait()
    part_ref[...] = apply_left(hx_ref[0], hx_ref[1], own_ref[...])
    copies[1].wait()


def tables_body(
    off_hbm, frac_hbm, group_hbm, slot_hbm, send_hbm, obs_hbm, sig_hbm, resp_hbm,
    field_ref, hy_ref, hz_ref,
    part_ref, resp_ref, obs_ref, var_ref, idx_ref, w_ref, grp_ref, take_ref, give_ref, pack_ref, sum_ref,
    off_ref, frac_ref, group_ref, slot_ref, send_ref, sig_ref, keep, sems,
):
    count = resp_ref.shape[0]
    copies = fetch(
        [
            (send_hbm, send_ref), (slot_hbm, slot_ref), (group_hbm, group_ref),
            (off_hbm, off_ref), (frac_hbm, frac_ref), (obs_hbm, obs_ref), (sig_hbm, sig_ref),
            (resp_hbm.at[pl.ds(resp_hbm.shape[0] - count, count)], resp_ref),
        ],
        sems,
    )
    part = apply_left(hy_ref[0], hy_ref[1], field_ref[...])
    part_ref[...] = apply_right(part, hz_ref[0], hz_ref[1])
    for copy in copies[:-1]:
        copy.wait()
    sig = sig_ref[...]
    var_ref[...] = sig * sig
    tiles = off_ref.shape[1]
    slots = take_ref.shape[1]
    cells = pack_ref.shape[1]
    off = off_ref[...]
    frac = frac_ref[...]
    idx_ref[...] = jnp.concatenate([off, off + 1], axis=0).T
    w_ref[...] = jnp.concatenate([1.0 - frac, frac], axis=0).T
    keep[...] = jnp.broadcast_to(group_ref[...], (LANES, tiles)).T
    first = iota((tiles // 2, LANES), 1) < LANES // 2
    grp_ref[...] = jnp.where(
        first, keep[pl.ds(0, tiles // 2, 2), :], keep[pl.ds(1, tiles // 2, 2), :]
    )
    slot = slot_ref[...]
    wide = jnp.broadcast_to(slot, (LANES, tiles)).T
    for at in range(0, slots, LANES):
        take_ref[:, at : at + LANES] = one_hot(wide == iota((tiles, LANES), 1) + at)
    give_ref[...] = one_hot(jnp.broadcast_to(slot, (slots, tiles)) == iota((slots, tiles), 0))
    send = send_ref[...]
    wide = jnp.broadcast_to(send, (LANES, slots)).T
    for at in range(0, cells, LANES):
        pack_ref[:, at : at + LANES] = one_hot(wide == iota((slots, LANES), 1) + at)
    sum_ref[...] = one_hot(jnp.broadcast_to(send, (cells, slots)) == iota((cells, slots), 0))
    copies[-1].wait()


def sides(mats_ref, near, far):
    return apply_left(mats_ref[2], mats_ref[3], near) + apply_left(mats_ref[4], mats_ref[5], far)


def own_body(own_ref, mats_ref, part_ref):
    part_ref[...] = apply_left(mats_ref[0], mats_ref[1], own_ref[...])


def own_latent_body(own_ref, mats_ref, latent_ref, part_ref):
    part_ref[...] = latent_ref[...] + apply_left(mats_ref[0], mats_ref[1], own_ref[...])


def join_body(part_ref, near_ref, far_ref, mats_ref, out_ref, *sent_ref):
    out = part_ref[...] + sides(mats_ref, near_ref[...], far_ref[...])
    out_ref[...] = out
    for ref in sent_ref:
        ref[...] = out.astype(ref.dtype)


def density_body(part_ref, near_ref, far_ref, mats_ref, hz_ref, pack_ref, dens_ref, packed_ref):
    out = sides(mats_ref, near_ref[...], far_ref[...])
    dens = jnp.exp(part_ref[...] + apply_right(out, hz_ref[0], hz_ref[1]))
    dens_ref[...] = dens
    packed_ref[...] = mm(pack_ref[...], dens.astype(BF16)).astype(BF16)


def owner_body(sum_ref, back_ref, dens_ref, hz_ref, out_ref, sent_ref):
    grad = dens_ref[...] * mm(sum_ref[...], back_ref[...])
    out = apply_right(grad, hz_ref[0], hz_ref[1])
    out_ref[...] = out
    sent_ref[...] = out.astype(sent_ref.dtype)


def cone_body(
    got_ref, early_ref, late_ref, idx_ref, w_ref, grp_ref, take_ref, give_ref, obs_ref, var_ref,
    pred_ref, grad_ref, both, pairs, cells,
):
    early, samples, star_tile = early_ref.shape
    tiles = idx_ref.shape[0]
    depth = got_ref.shape[1]
    groups = obs_ref.shape[0]
    half = LANES // 2
    idx = idx_ref[...]
    columns = mm(take_ref[...], got_ref[...])
    value = jnp.zeros((tiles, LANES), F32)
    for at in range(0, depth, LANES):
        piece = jnp.take_along_axis(columns[:, at : at + LANES], idx & (LANES - 1), axis=1)
        value = jnp.where((idx >= at) & (idx < at + LANES), piece, value) if at else piece
    value = w_ref[...] * value
    both[...] = value + pltpu.roll(value, half, 1)
    first = iota((tiles // 2, LANES), 1) < half
    pairs[...] = jnp.where(
        first, both[pl.ds(0, tiles // 2, 2), :], both[pl.ds(1, tiles // 2, 2), :]
    )
    group_at = iota((groups, LANES), 0)

    def pair_rows(ref, step, count):
        return ref[pl.ds(pl.multiple_of(step * count, count), count), :]

    def rays(ref, step, count):
        rows = ref[pl.ds(pl.multiple_of(step * count, count), count)]
        return rows.reshape(count * samples, star_tile)

    def predict(ref, before, step, total):
        pair = pair_rows(pairs, step + before, PREDICT_PAIRS)
        group = pair_rows(grp_ref, step + before, PREDICT_PAIRS)
        left = [
            jnp.where(group[i : i + 1] == group_at, pair[i : i + 1], 0.0)
            for i in range(PREDICT_PAIRS)
        ]
        left = jnp.concatenate(left, axis=1).astype(BF16)
        return total + mm(left, rays(ref, step, 2 * PREDICT_PAIRS))

    count = 2 * PREDICT_PAIRS
    pred = jnp.zeros((groups, star_tile), F32)
    for ref, before in ((early_ref, 0), (late_ref, early)):
        pred = lax.fori_loop(
            0, ref.shape[0] // count, functools.partial(predict, ref, before // count), pred
        )
    pred_ref[...] = pred
    resid = ((pred - obs_ref[...]) / var_ref[...]).astype(BF16)
    parts = depth // PART
    rows = 2 * parts
    at_row = iota((2 * rows, LANES), 0)
    row_part = at_row & (parts - 1)
    row_second = (at_row & parts) != 0
    row_high = at_row < rows
    level = [(iota((16, LANES), 0) + at).astype(F32).astype(BF16) for at in range(0, PART, 16)]
    one = jnp.ones((16, LANES), BF16)
    zero = jnp.zeros((16, LANES), BF16)
    step_pairs = BACK_PAIRS
    step_tiles = 2 * step_pairs
    lane_first = iota((step_pairs, LANES), 1) < half

    def backward(ref, before, step, carry):
        back = mm_nt(resid, rays(ref, step, step_tiles))
        step = step + before
        group = pair_rows(grp_ref, step, step_pairs)
        picked = [
            jnp.sum(
                jnp.where(group[i : i + 1] == group_at, back[:, i * LANES : (i + 1) * LANES], 0.0),
                axis=0, keepdims=True,
            )
            for i in range(step_pairs)
        ]
        picked = jnp.concatenate(picked, axis=0)
        swapped = pltpu.roll(picked, half, 1)
        base = pl.multiple_of(step * step_tiles, step_tiles)
        even, odd = pl.ds(base, step_pairs, 2), pl.ds(base + 1, step_pairs, 2)
        weights = (
            jnp.where(lane_first, picked, swapped) * w_ref[even, :],
            jnp.where(lane_first, swapped, picked) * w_ref[odd, :],
        )
        highs = [weight.astype(BF16).astype(F32) for weight in weights]
        lows = [weight - high for weight, high in zip(weights, highs)]
        spots = (idx_ref[even, :], idx_ref[odd, :])
        lanes = [(spot & (PART - 1)).astype(F32) for spot in spots]
        shift = PART.bit_length() - 1
        blocks = [lax.shift_right_logical(spot, shift) for spot in spots]
        made = []
        for i in range(step_pairs):
            left, right = [], []
            for which in (0, 1):
                block = blocks[which][i : i + 1]
                kept = (row_second == bool(which)) & (row_part == block)
                both_parts = jnp.where(
                    row_high, highs[which][i : i + 1], lows[which][i : i + 1]
                )
                left.append(jnp.where(kept, both_parts, 0.0))
                lane = jnp.broadcast_to(lanes[which][i : i + 1], (16, LANES)).astype(BF16)
                right.append(
                    jnp.concatenate([jnp.where(lane == lv, one, zero) for lv in level], axis=0)
                )
            out = mm_nt(
                jnp.concatenate(left, axis=1).astype(BF16), jnp.concatenate(right, axis=1)
            )
            made.append(out[:rows] + out[rows:])
        count = step_pairs * rows
        cells[pl.ds(pl.multiple_of(step * count, count), count), :] = jnp.concatenate(made, axis=0)
        return carry

    for ref, before in ((early_ref, 0), (late_ref, early)):
        steps = ref.shape[0] // step_tiles
        lax.fori_loop(0, steps, functools.partial(backward, ref, before // step_tiles), 0)
    give = give_ref[...]
    for at in range(0, depth, LANES):
        pieces = [
            cells[pl.ds(part, tiles, parts), :]
            for part in range(at // PART, (at + LANES) // PART)
        ]
        high, low = split(jnp.concatenate(pieces, axis=1))
        grad_ref[:, at : at + LANES] = (mm(give, high) + mm(give, low)).astype(BF16)


def exchanged(values, axis):
    count = lax.axis_size(axis)
    return [
        lax.ppermute(
            values, axis,
            [pair for i in range(first, count - 1, 2) for pair in ((i, i + 1), (i + 1, i))],
        )
        for first in (0, 1)
    ]


def on_device(
    latent, observed, sigma, response, offsets, fractions, tile_group, tile_slot, send_index
):
    rows_x, rows_y, depth = latent.shape
    cells = rows_x * rows_y
    axes = ("cx", "cy")
    devices = lax.axis_size("cx") * lax.axis_size("cy")
    slots = devices * send_index.shape[2]
    tiles, samples, star_tile = response.shape
    groups = observed.shape[0] // star_tile
    own = latent.reshape(cells, depth)
    field_out = ((cells, depth), F32)
    sent_out = ((cells, depth), BF16)

    send = send_index.reshape(1, slots)
    ray_out = ((tiles // 2, samples, star_tile), BF16)
    near, far = exchanged(own.astype(BF16), "cx")
    hx, hy, hz, part, early = call(
        functools.partial(operators_body, rows_x, rows_y),
        [
            ((6, cells, cells), BF16), ((6, cells, cells), BF16), ((2, depth, depth), BF16),
            field_out, ray_out,
        ],
        hbm(own), hbm(response), hbm(send),
        scratch=[pltpu.VMEM((cells, depth), F32), pltpu.SemaphoreType.DMA((2,))],
        name="operators",
    )
    field, sent = call(join_body, [field_out, sent_out], part, near, far, hx, name="along_x")
    near, far = exchanged(sent, "cy")
    part, late, obs, var, idx, weight, grp, take, give, pack, add_up = call(
        tables_body,
        [
            field_out,
            ray_out,
            ((groups, star_tile), F32),
            ((groups, star_tile), F32),
            ((tiles, LANES), jnp.int32),
            ((tiles, LANES), F32),
            ((tiles // 2, LANES), jnp.int32),
            ((tiles, slots), BF16),
            ((slots, tiles), BF16),
            ((slots, cells), BF16),
            ((cells, slots), BF16),
        ],
        hbm(offsets), hbm(fractions), hbm(tile_group.reshape(1, tiles)),
        hbm(tile_slot.reshape(1, tiles)), hbm(send),
        hbm(observed.reshape(groups, star_tile)), hbm(sigma.reshape(groups, star_tile)),
        hbm(response), field, hy, hz,
        scratch=[
            pltpu.VMEM((samples, tiles), jnp.int32),
            pltpu.VMEM((samples, tiles), F32),
            pltpu.VMEM((1, tiles), jnp.int32),
            pltpu.VMEM((1, tiles), jnp.int32),
            pltpu.VMEM((1, slots), jnp.int32),
            pltpu.VMEM((groups, star_tile), F32),
            pltpu.VMEM((tiles, LANES), jnp.int32),
            pltpu.SemaphoreType.DMA((8,)),
        ],
        name="tables",
    )
    dens, packed = call(
        density_body, [field_out, ((slots, depth), BF16)],
        part, near, far, hy, hz, pack, name="density",
    )
    got = lax.all_to_all(packed, axes, split_axis=0, concat_axis=0, tiled=True)
    pred, grad = call(
        cone_body, [((groups, star_tile), F32), ((slots, depth), BF16)],
        got, early, late, idx, weight, grp, take, give, obs, var,
        scratch=[
            pltpu.VMEM((tiles, LANES), F32),
            pltpu.VMEM((tiles // 2, LANES), F32),
            pltpu.VMEM((tiles * (depth // PART), PART), F32),
        ],
        limit=20,
        name="cones",
    )
    back = lax.all_to_all(grad, axes, split_axis=0, concat_axis=0, tiled=True)
    field, sent = call(owner_body, [field_out, sent_out], add_up, back, dens, hz, name="owners")
    near, far = exchanged(sent, "cy")
    (part,) = call(own_body, [field_out], field, hy, name="own_y")
    field, sent = call(join_body, [field_out, sent_out], part, near, far, hy, name="along_y")
    near, far = exchanged(sent, "cx")
    (part,) = call(own_latent_body, [field_out], field, hx, own, name="own_x")
    (gradient,) = call(join_body, [field_out], part, near, far, hx, name="finish")
    return gradient.reshape(rows_x, rows_y, depth), pred.reshape(-1)


def solution(mesh):
    both = ("cx", "cy")
    placed = (
        P("cx", "cy", None),
        P(both),
        P(both),
        P(both, None, None),
        P(None, both),
        P(None, both),
        P(both),
        P(both),
        P(both, None, None),
    )
    return jax.shard_map(
        on_device,
        mesh=mesh,
        in_specs=placed,
        out_specs=(P("cx", "cy", None), P(both)),
        check_vma=False,
    )
```

time: 73.6 us -> 69.7 us (0.947)
  waiting for transfers between devices: 13.5 us -> 11.4 us
  blocking collectives: 26.2 us -> 25 us
    ppermute x8, waiting for transfers between devices: 13.5 us -> 11.4 us  [exchanged(): lax.ppermute(values, axis, [pair for i in range(first, count - 1, 2) for...]
    all_to_all x1, blocking collectives: 13.4 us -> 12.2 us  [on_device(): got = lax.all_to_all(packed, axes, split_axis=0, concat_axis=0, tiled=True)]
    pallas_call x7 -> x10, Pallas kernels: 17.3 us -> 16.8 us  [call(): pl.pallas_call(body, out_shape=shapes, in_specs=[pl.BlockSpec(memory_spac...]
  transfers between devices with their start and end apart: 8 -> 8, of which waited for: 4 -> 5; matrix products, arithmetic and copies ran while one was open for 2% -> 2% of each run, Pallas kernels for 5% -> 8%
where the time goes in v3:
time: 69.7 us; the launch traced here: 69 us
  blocking collectives  25 us (36%)
  Pallas kernels  16.8 us (24%)
  starting transfers between devices  12.8 us (18%)
  waiting for transfers between devices  11.4 us (16%)
  local copies, waits for them, and re-layouts  1.44 us (2%)
  other arithmetic  0.97 us (1%)
  between operations  0.77 us (1%)
    pallas_call x10, Pallas kernels, call(): pl.pallas_call(body, out_shape=shapes, in_specs=[pl.BlockSpec(memory_spac...  16.8 us
    ppermute x8, starting transfers between devices, exchanged(): lax.ppermute(values, axis, [pair for i in range(first, count - 1, 2) for...  12.8 us
    all_to_all x1, blocking collectives, on_device(): back = lax.all_to_all(grad, axes, split_axis=0, concat_axis=0, tiled=True)  12.8 us
    all_to_all x1, blocking collectives, on_device(): got = lax.all_to_all(packed, axes, split_axis=0, concat_axis=0, tiled=True)  12.2 us
    ppermute x8, waiting for transfers between devices, exchanged(): lax.ppermute(values, axis, [pair for i in range(first, count - 1, 2) for...  11.4 us
  transfers between devices with their start and end apart: 8, of which 5 were waited for; matrix products, arithmetic and copies ran while one was open for 2% of the time, Pallas kernels for 8%

profile of v3, /device:TPU:12, one launch (start us, length us, event | category | flops | bytes accessed | tf_op | source)
XLA Modules:
  0.0 69.0 jit_solution(14743689515045636206)
XLA Ops:
  0.6 1.0 %bitcast_convert_fusion = bf16[256,256]{1,0:T(8,128)(2,1)S(1)} fusion(f32[16,16,256]{2,1,0:T(8,128)} %param.9), kind=kLoop, calls=%fused_computation | loop fusion | flops 65536 | bytes 393216 | tf_op jit(solution)/shard_map/convert_element_type | solution.py:361
  1.6 3.5 %collective-permute-start.1 = (bf16[256,256]{1,0:T(8,128)(2,1)S(1)}, bf16[256,256]{1,0:T(8,128)(2,1)S(1)}, u32[]{:S(2)}, u32[]{:S(2)}) collective-permute-start(bf16[256,256]{1,0:T(8,128)(2,1)S(1)} %bitcast_convert_fusion), channel_id=1, source_target_pairs={{8,16},{16,8},{9,17},{17,9},{10,18},{18,10},{11,19},{19,11},{12,20... | collective-permute-start | bytes 393224 | tf_op jit(solution)/shard_map/ppermute | solution.py:337
  5.1 0.1 collective-permute-start
  5.2 0.8 %copy.12 = s32[1,32,16]{2,1,0:T(8,128)S(1)} copy(s32[1,32,16]{1,2,0:T(8,128)} %param.17) | data formatting | bytes 4096 | tf_op args[8]
  5.9 0.7 reshape.34.after_hbm.send_hbm
  6.6 2.3 %operators.1 = (bf16[6,256,256]{2,1,0:T(8,128)(2,1)S(1)}, bf16[6,256,256]{2,1,0:T(8,128)(2,1)S(1)}, bf16[2,256,256]{2,1,0:T(8,128)(2,1)S(1)}, f32[256,256]{1,0:T(8,128)S(1)}, bf16[256,64,128]{2,1,0:T(8,128)(2,1)S(1)}) custom-call(f32[256,256]{1,0:T(8,128)} %bitcast.12, bf16[512,64,128]{2,1,0:T(8,128)(2,1)} %resp_hbm.3, s32[1,512]{1,0:T(1,128)} %reshape.34.after_hbm.send_hbm), custom_call_target="tpu_custom_call" | custom-call | bytes 14944256 | tf_op jit(solution)/shard_map/operators/pallas_call | solution.py:71
  8.9 0.0 collective-permute-done.1.far_ref
  8.9 1.2 %collective-permute-done.near_ref = bf16[256,256]{1,0:T(8,128)(2,1)S(1)} collective-permute-done((bf16[256,256]{1,0:T(8,128)(2,1)S(1)}, bf16[256,256]{1,0:T(8,128)(2,1)S(1)}, u32[]{:S(2)}, u32[]{:S(2)}) %collective-permute-start) | collective-permute-done | bytes 131104 | tf_op jit(solution)/shard_map/ppermute | solution.py:337
  10.1 0.3 along_x.1
  10.4 1.9 %collective-permute-start.3 = (bf16[256,256]{1,0:T(8,128)(2,1)S(1)}, bf16[256,256]{1,0:T(8,128)(2,1)S(1)}, u32[]{:S(2)}, u32[]{:S(2)}) collective-permute-start(bf16[256,256]{1,0:T(8,128)(2,1)S(1)} %get-tuple-element.35), channel_id=1, source_target_pairs={{1,2},{2,1},{3,4},{4,3},{5,6},{6,5},{9,10},{10,9},{11,12},{12,11},... | collective-permute-start | bytes 393224 | tf_op jit(solution)/shard_map/ppermute | solution.py:337
  12.4 1.7 %collective-permute-start.2 = (bf16[256,256]{1,0:T(8,128)(2,1)S(1)}, bf16[256,256]{1,0:T(8,128)(2,1)S(1)}, u32[]{:S(2)}, u32[]{:S(2)}) collective-permute-start(bf16[256,256]{1,0:T(8,128)(2,1)S(1)} %get-tuple-element.35), channel_id=1, source_target_pairs={{0,1},{1,0},{2,3},{3,2},{4,5},{5,4},{6,7},{7,6},{8,9},{9,8},{10,11... | collective-permute-start | bytes 393224 | tf_op jit(solution)/shard_map/ppermute | solution.py:337
  14.0 2.8 %tables.1 = (f32[256,256]{1,0:T(8,128)S(1)}, bf16[256,64,128]{2,1,0:T(8,128)(2,1)S(1)}, f32[8,128]{1,0:T(8,128)S(1)}, f32[8,128]{1,0:T(8,128)S(1)}, s32[512,128]...) custom-call(s32[64,512]{1,0:T(8,128)} %off_hbm.1, ...), custom_call_target="tpu_custom_call" | custom-call | bytes 16668672 | tf_op jit(solution)/shard_map/tables/pallas_call | solution.py:71
  16.8 1.3 %collective-permute-done.3.far_ref = bf16[256,256]{1,0:T(8,128)(2,1)S(1)} collective-permute-done((bf16[256,256]{1,0:T(8,128)(2,1)S(1)}, bf16[256,256]{1,0:T(8,128)(2,1)S(1)}, u32[]{:S(2)}, u32[]{:S(2)}) %collective-permute-start.3) | collective-permute-done | bytes 131104 | tf_op jit(solution)/shard_map/ppermute | solution.py:337
  18.1 0.0 collective-permute-done.2.near_ref
  18.1 0.9 %density.1 = (f32[256,256]{1,0:T(8,128)S(1)}, bf16[512,256]{1,0:T(8,128)(2,1)S(1)}) custom-call(f32[256,256]{1,0:T(8,128)S(1)} %get-tuple-element.34.part_ref, bf16[256,256]{1,0:T(8,128)(2,1)S(1)} %collective-permute-done.2.near_ref, bf16[256,256]{1,0:T(8,128)(2,1)S(1)} %collective-permute-done.3.far_ref, ...), custom_call_target="tpu_custom_call" | custom-call | bytes 2359296 | tf_op jit(solution)/shard_map/density/pallas_call | solution.py:71
  19.1 12.2 %all_to_all.22 = bf16[32,16,256]{2,1,0:T(8,128)(2,1)S(1)} all-to-all(bf16[32,16,256]{2,1,0:T(8,128)(2,1)S(1)} %bitcast.17), channel_id=1, replica_groups=mesh['cx'=4,'cy'=8] {'cx','cy'}, dimensions={0} | all-to-all | bytes 524288 | tf_op jit(solution)/shard_map/all_to_all | solution.py:409
  31.2 8.0 %cones.1 = (f32[8,128]{1,0:T(8,128)}, bf16[512,256]{1,0:T(8,128)(2,1)S(1)}) custom-call(bf16[512,256]{1,0:T(8,128)(2,1)S(1)} %bitcast.14, bf16[256,64,128]{2,1,0:T(8,128)(2,1)S(1)} %get-tuple-element.38.early_ref, bf16[256,64,128]{2,1,0:T(8,128)(2,1)S(1)} %get-tuple-element.39.late_ref, s32[512,128]{1,0:T(8,128)S(1)} %get-tuple-element.40.idx_ref, ...), custom_call_target="tpu_custom_call" | custom-call | bytes 10629120 | tf_op jit(solution)/shard_map/cones/pallas_call | solution.py:71
  39.3 0.0 copy-start
  39.3 12.8 %all_to_all.23 = bf16[32,16,256]{2,1,0:T(8,128)(2,1)S(1)} all-to-all(bf16[32,16,256]{2,1,0:T(8,128)(2,1)S(1)} %bitcast.16), channel_id=1, replica_groups=mesh['cx'=4,'cy'=8] {'cx','cy'}, dimensions={0} | all-to-all | bytes 524288 | tf_op jit(solution)/shard_map/all_to_all | solution.py:421
  52.1 0.5 owners.1
  52.6 2.9 %collective-permute-start.5 = (bf16[256,256]{1,0:T(8,128)(2,1)S(1)}, bf16[256,256]{1,0:T(8,128)(2,1)S(1)}, u32[]{:S(2)}, u32[]{:S(2)}) collective-permute-start(bf16[256,256]{1,0:T(8,128)(2,1)S(1)} %get-tuple-element.50), channel_id=1, source_target_pairs={{1,2},{2,1},{3,4},{4,3},{5,6},{6,5},{9,10},{10,9},{11,12},{12,11},... | collective-permute-start | bytes 393224 | tf_op jit(solution)/shard_map/ppermute | solution.py:337
  55.5 0.1 collective-permute-start.4
  55.6 0.3 own_y.1.part_ref
  55.9 4.5 %collective-permute-done.5.far_ref = bf16[256,256]{1,0:T(8,128)(2,1)S(1)} collective-permute-done((bf16[256,256]{1,0:T(8,128)(2,1)S(1)}, bf16[256,256]{1,0:T(8,128)(2,1)S(1)}, u32[]{:S(2)}, u32[]{:S(2)}) %collective-permute-start.5) | collective-permute-done | bytes 131104 | tf_op jit(solution)/shard_map/ppermute | solution.py:337
  60.4 0.0 collective-permute-done.4.near_ref
  60.4 0.3 along_y.1
  60.7 2.2 %collective-permute-start.7 = (bf16[256,256]{1,0:T(8,128)(2,1)S(1)}, bf16[256,256]{1,0:T(8,128)(2,1)S(1)}, u32[]{:S(2)}, u32[]{:S(2)}) collective-permute-start(bf16[256,256]{1,0:T(8,128)(2,1)S(1)} %get-tuple-element.52), channel_id=1, source_target_pairs={{8,16},{16,8},{9,17},{17,9},{10,18},{18,10},{11,19},{19,11},{12,20... | collective-permute-start | bytes 393224 | tf_op jit(solution)/shard_map/ppermute | solution.py:337
  63.0 0.4 collective-permute-start.6
  63.4 0.0 copy-done
  63.4 0.3 own_x.1.part_ref
  63.7 3.9 %collective-permute-done.7.far_ref = bf16[256,256]{1,0:T(8,128)(2,1)S(1)} collective-permute-done((bf16[256,256]{1,0:T(8,128)(2,1)S(1)}, bf16[256,256]{1,0:T(8,128)(2,1)S(1)}, u32[]{:S(2)}, u32[]{:S(2)}) %collective-permute-start.7) | collective-permute-done | bytes 131104 | tf_op jit(solution)/shard_map/ppermute | solution.py:337
  67.6 0.4 collective-permute-done.6.near_ref
  68.0 1.0 %finish.1 = f32[256,256]{1,0:T(8,128)} custom-call(f32[256,256]{1,0:T(8,128)S(1)} %own_x.1.part_ref, bf16[256,256]{1,0:T(8,128)(2,1)S(1)} %collective-permute-done.6.near_ref, bf16[256,256]{1,0:T(8,128)(2,1)S(1)} %collective-permute-done.7.far_ref, bf16[6,256,256]{2,1,0:T(8,128)(2,1)S(1)} %get-tuple-element.29.mats_ref), custom_call_target="tpu_custom_call" | custom-call | bytes 1572864 | tf_op jit(solution)/shard_map/finish/pallas_call | solution.py:71
Async XLA Ops:
  1.6 7.3 %collective-permute-start.1 = (bf16[256,256]{1,0:T(8,128)(2,1)S(1)}, bf16[256,256]{1,0:T(8,128)(2,1)S(1)}, u32[]{:S(2)}, u32[]{:S(2)}) collective-permute-start(bf16[256,256]{1,0:T(8,128)(2,1)S(1)} %bitcast_convert_fusion), channel_id=1, source_target_pairs={{8,16},{16,8},{9,17},{17,9},{10,18},{18,10},{11,19},{19,11},{12,20... | collective-permute-start | bytes 393224 | tf_op jit(solution)/shard_map/ppermute | solution.py:337
  5.1 5.0 %collective-permute-start = (bf16[256,256]{1,0:T(8,128)(2,1)S(1)}, bf16[256,256]{1,0:T(8,128)(2,1)S(1)}, u32[]{:S(2)}, u32[]{:S(2)}) collective-permute-start(bf16[256,256]{1,0:T(8,128)(2,1)S(1)} %bitcast_convert_fusion), channel_id=1, source_target_pairs={{0,8},{8,0},{16,24},{24,16},{1,9},{9,1},{17,25},{25,17},{2,10},{10... | collective-permute-start | bytes 393224 | tf_op jit(solution)/shard_map/ppermute | solution.py:337
  10.4 7.7 %collective-permute-start.3 = (bf16[256,256]{1,0:T(8,128)(2,1)S(1)}, bf16[256,256]{1,0:T(8,128)(2,1)S(1)}, u32[]{:S(2)}, u32[]{:S(2)}) collective-permute-start(bf16[256,256]{1,0:T(8,128)(2,1)S(1)} %get-tuple-element.35), channel_id=1, source_target_pairs={{1,2},{2,1},{3,4},{4,3},{5,6},{6,5},{9,10},{10,9},{11,12},{12,11},... | collective-permute-start | bytes 393224 | tf_op jit(solution)/shard_map/ppermute | solution.py:337
  12.4 5.8 %collective-permute-start.2 = (bf16[256,256]{1,0:T(8,128)(2,1)S(1)}, bf16[256,256]{1,0:T(8,128)(2,1)S(1)}, u32[]{:S(2)}, u32[]{:S(2)}) collective-permute-start(bf16[256,256]{1,0:T(8,128)(2,1)S(1)} %get-tuple-element.35), channel_id=1, source_target_pairs={{0,1},{1,0},{2,3},{3,2},{4,5},{5,4},{6,7},{7,6},{8,9},{9,8},{10,11... | collective-permute-start | bytes 393224 | tf_op jit(solution)/shard_map/ppermute | solution.py:337
  39.3 24.1 %copy-start = (f32[16,16,256]{2,1,0:T(8,128)S(1)}, f32[16,16,256]{2,1,0:T(8,128)}, u32[]{:S(2)}) copy-start(f32[16,16,256]{2,1,0:T(8,128)} %param.9) | copy-start | bytes 786436
  52.6 7.8 %collective-permute-start.5 = (bf16[256,256]{1,0:T(8,128)(2,1)S(1)}, bf16[256,256]{1,0:T(8,128)(2,1)S(1)}, u32[]{:S(2)}, u32[]{:S(2)}) collective-permute-start(bf16[256,256]{1,0:T(8,128)(2,1)S(1)} %get-tuple-element.50), channel_id=1, source_target_pairs={{1,2},{2,1},{3,4},{4,3},{5,6},{6,5},{9,10},{10,9},{11,12},{12,11},... | collective-permute-start | bytes 393224 | tf_op jit(solution)/shard_map/ppermute | solution.py:337
  55.5 4.9 %collective-permute-start.4 = (bf16[256,256]{1,0:T(8,128)(2,1)S(1)}, bf16[256,256]{1,0:T(8,128)(2,1)S(1)}, u32[]{:S(2)}, u32[]{:S(2)}) collective-permute-start(bf16[256,256]{1,0:T(8,128)(2,1)S(1)} %get-tuple-element.50), channel_id=1, source_target_pairs={{0,1},{1,0},{2,3},{3,2},{4,5},{5,4},{6,7},{7,6},{8,9},{9,8},{10,11... | collective-permute-start | bytes 393224 | tf_op jit(solution)/shard_map/ppermute | solution.py:337
  60.7 6.9 %collective-permute-start.7 = (bf16[256,256]{1,0:T(8,128)(2,1)S(1)}, bf16[256,256]{1,0:T(8,128)(2,1)S(1)}, u32[]{:S(2)}, u32[]{:S(2)}) collective-permute-start(bf16[256,256]{1,0:T(8,128)(2,1)S(1)} %get-tuple-element.52), channel_id=1, source_target_pairs={{8,16},{16,8},{9,17},{17,9},{10,18},{18,10},{11,19},{19,11},{12,20... | collective-permute-start | bytes 393224 | tf_op jit(solution)/shard_map/ppermute | solution.py:337
  63.0 5.0 %collective-permute-start.6 = (bf16[256,256]{1,0:T(8,128)(2,1)S(1)}, bf16[256,256]{1,0:T(8,128)(2,1)S(1)}, u32[]{:S(2)}, u32[]{:S(2)}) collective-permute-start(bf16[256,256]{1,0:T(8,128)(2,1)S(1)} %get-tuple-element.52), channel_id=1, source_target_pairs={{0,8},{8,0},{16,24},{24,16},{1,9},{9,1},{17,25},{25,17},{2,10},{10... | collective-permute-start | bytes 393224 | tf_op jit(solution)/shard_map/ppermute | solution.py:337

commit v4 on v3

--- a/solution.py
+++ b/solution.py
@@ -12,9 +12,10 @@
 LANES = 128
 F32 = jnp.float32
 BF16 = jnp.bfloat16
-PREDICT_PAIRS = 64
-BACK_PAIRS = 64
-PART = 64
+AHEAD = 256
+CHUNK = 256
+GIVE = 256
+PART = 32
 
 
 def tap_scale():
@@ -212,123 +213,101 @@
 
 def cone_body(
     got_ref, early_ref, late_ref, idx_ref, w_ref, grp_ref, take_ref, give_ref, obs_ref, var_ref,
-    pred_ref, grad_ref, both, pairs, cells,
+    pred_ref, grad_ref, both, cells,
 ):
     early, samples, star_tile = early_ref.shape
     tiles = idx_ref.shape[0]
     depth = got_ref.shape[1]
     groups = obs_ref.shape[0]
     half = LANES // 2
-    idx = idx_ref[...]
-    columns = mm(take_ref[...], got_ref[...])
-    value = jnp.zeros((tiles, LANES), F32)
-    for at in range(0, depth, LANES):
-        piece = jnp.take_along_axis(columns[:, at : at + LANES], idx & (LANES - 1), axis=1)
-        value = jnp.where((idx >= at) & (idx < at + LANES), piece, value) if at else piece
-    value = w_ref[...] * value
-    both[...] = value + pltpu.roll(value, half, 1)
-    first = iota((tiles // 2, LANES), 1) < half
-    pairs[...] = jnp.where(
-        first, both[pl.ds(0, tiles // 2, 2), :], both[pl.ds(1, tiles // 2, 2), :]
-    )
+
+    def rays(first, count):
+        ref, first = (early_ref, first) if first < early else (late_ref, first - early)
+        return ref[first : first + count].reshape(count * samples, star_tile)
+
     group_at = iota((groups, LANES), 0)
-
-    def pair_rows(ref, step, count):
-        return ref[pl.ds(pl.multiple_of(step * count, count), count), :]
-
-    def rays(ref, step, count):
-        rows = ref[pl.ds(pl.multiple_of(step * count, count), count)]
-        return rows.reshape(count * samples, star_tile)
-
-    def predict(ref, before, step, total):
-        pair = pair_rows(pairs, step + before, PREDICT_PAIRS)
-        group = pair_rows(grp_ref, step + before, PREDICT_PAIRS)
+    lane_first = iota((AHEAD // 2, LANES), 1) < half
+    got = got_ref[...]
+    pred = jnp.zeros((groups, star_tile), F32)
+    for base in range(0, tiles, AHEAD):
+        span = pl.ds(base, AHEAD)
+        idx = idx_ref[span, :]
+        columns = mm(take_ref[span, :], got)
+        for at in range(0, depth, LANES):
+            piece = jnp.take_along_axis(
+                columns[:, at : at + LANES], idx & (LANES - 1), axis=1
+            )
+            value = jnp.where(idx >= at, piece, value) if at else piece
+        value = w_ref[span, :] * value
+        both[span, :] = value + pltpu.roll(value, half, 1)
+    for base in range(0, tiles, AHEAD):
+        pair = jnp.where(
+            lane_first, both[pl.ds(base, AHEAD // 2, 2), :], both[pl.ds(base + 1, AHEAD // 2, 2), :]
+        )
+        group = grp_ref[pl.ds(base // 2, AHEAD // 2), :]
         left = [
             jnp.where(group[i : i + 1] == group_at, pair[i : i + 1], 0.0)
-            for i in range(PREDICT_PAIRS)
+            for i in range(AHEAD // 2)
         ]
-        left = jnp.concatenate(left, axis=1).astype(BF16)
-        return total + mm(left, rays(ref, step, 2 * PREDICT_PAIRS))
-
-    count = 2 * PREDICT_PAIRS
-    pred = jnp.zeros((groups, star_tile), F32)
-    for ref, before in ((early_ref, 0), (late_ref, early)):
-        pred = lax.fori_loop(
-            0, ref.shape[0] // count, functools.partial(predict, ref, before // count), pred
-        )
+        pred += mm(jnp.concatenate(left, axis=1).astype(BF16), rays(base, AHEAD))
+
     pred_ref[...] = pred
     resid = ((pred - obs_ref[...]) / var_ref[...]).astype(BF16)
     parts = depth // PART
     rows = 2 * parts
-    at_row = iota((2 * rows, LANES), 0)
+    at_row = iota((rows, LANES), 0)
     row_part = at_row & (parts - 1)
     row_second = (at_row & parts) != 0
-    row_high = at_row < rows
     level = [(iota((16, LANES), 0) + at).astype(F32).astype(BF16) for at in range(0, PART, 16)]
     one = jnp.ones((16, LANES), BF16)
     zero = jnp.zeros((16, LANES), BF16)
-    step_pairs = BACK_PAIRS
-    step_tiles = 2 * step_pairs
-    lane_first = iota((step_pairs, LANES), 1) < half
-
-    def backward(ref, before, step, carry):
-        back = mm_nt(resid, rays(ref, step, step_tiles))
-        step = step + before
-        group = pair_rows(grp_ref, step, step_pairs)
+    shift = PART.bit_length() - 1
+    total = jnp.zeros(grad_ref.shape, F32)
+    lane_first = iota((CHUNK // 2, LANES), 1) < half
+    for base in range(0, tiles, CHUNK):
+        back = mm_nt(resid, rays(base, CHUNK))
+        group = grp_ref[pl.ds(base // 2, CHUNK // 2), :]
         picked = [
             jnp.sum(
                 jnp.where(group[i : i + 1] == group_at, back[:, i * LANES : (i + 1) * LANES], 0.0),
                 axis=0, keepdims=True,
             )
-            for i in range(step_pairs)
+            for i in range(CHUNK // 2)
         ]
         picked = jnp.concatenate(picked, axis=0)
         swapped = pltpu.roll(picked, half, 1)
-        base = pl.multiple_of(step * step_tiles, step_tiles)
-        even, odd = pl.ds(base, step_pairs, 2), pl.ds(base + 1, step_pairs, 2)
+        even, odd = pl.ds(base, CHUNK // 2, 2), pl.ds(base + 1, CHUNK // 2, 2)
         weights = (
             jnp.where(lane_first, picked, swapped) * w_ref[even, :],
             jnp.where(lane_first, swapped, picked) * w_ref[odd, :],
         )
-        highs = [weight.astype(BF16).astype(F32) for weight in weights]
-        lows = [weight - high for weight, high in zip(weights, highs)]
         spots = (idx_ref[even, :], idx_ref[odd, :])
         lanes = [(spot & (PART - 1)).astype(F32) for spot in spots]
-        shift = PART.bit_length() - 1
         blocks = [lax.shift_right_logical(spot, shift) for spot in spots]
-        made = []
-        for i in range(step_pairs):
+        blocks[1] = blocks[1] + parts
+        for i in range(CHUNK // 2):
             left, right = [], []
             for which in (0, 1):
-                block = blocks[which][i : i + 1]
-                kept = (row_second == bool(which)) & (row_part == block)
-                both_parts = jnp.where(
-                    row_high, highs[which][i : i + 1], lows[which][i : i + 1]
-                )
-                left.append(jnp.where(kept, both_parts, 0.0))
+                kept = at_row == blocks[which][i : i + 1]
+                left.append(jnp.where(kept, weights[which][i : i + 1], 0.0))
                 lane = jnp.broadcast_to(lanes[which][i : i + 1], (16, LANES)).astype(BF16)
                 right.append(
                     jnp.concatenate([jnp.where(lane == lv, one, zero) for lv in level], axis=0)
                 )
-            out = mm_nt(
+            cells[(base // 2 + i) * rows : (base // 2 + i + 1) * rows, :] = mm_nt(
                 jnp.concatenate(left, axis=1).astype(BF16), jnp.concatenate(right, axis=1)
             )
-            made.append(out[:rows] + out[rows:])
-        count = step_pairs * rows
-        cells[pl.ds(pl.multiple_of(step * count, count), count), :] = jnp.concatenate(made, axis=0)
-        return carry
-
-    for ref, before in ((early_ref, 0), (late_ref, early)):
-        steps = ref.shape[0] // step_tiles
-        lax.fori_loop(0, steps, functools.partial(backward, ref, before // step_tiles), 0)
-    give = give_ref[...]
-    for at in range(0, depth, LANES):
-        pieces = [
-            cells[pl.ds(part, tiles, parts), :]
-            for part in range(at // PART, (at + LANES) // PART)
-        ]
-        high, low = split(jnp.concatenate(pieces, axis=1))
-        grad_ref[:, at : at + LANES] = (mm(give, high) + mm(give, low)).astype(BF16)
+        if (base + CHUNK) % GIVE == 0:
+            start = base + CHUNK - GIVE
+            pieces = [cells[pl.ds(start * parts + at, GIVE, parts), :] for at in range(parts)]
+            total += mm(
+                give_ref[:, start : start + GIVE], jnp.concatenate(pieces, axis=1).astype(BF16)
+            )
+    grad_ref[...] = total.astype(BF16)
+
+
+def cone_scratch(tiles, depth):
+    return [pltpu.VMEM((tiles, LANES), F32), pltpu.VMEM((tiles * (depth // PART), PART), F32)]
 
 
 def exchanged(values, axis):
@@ -410,11 +389,7 @@
     pred, grad = call(
         cone_body, [((groups, star_tile), F32), ((slots, depth), BF16)],
         got, early, late, idx, weight, grp, take, give, obs, var,
-        scratch=[
-            pltpu.VMEM((tiles, LANES), F32),
-            pltpu.VMEM((tiles // 2, LANES), F32),
-            pltpu.VMEM((tiles * (depth // PART), PART), F32),
-        ],
+        scratch=cone_scratch(tiles, depth),
         limit=20,
         name="cones",
     )

time: 69.7 us -> 67.3 us (0.966)
  Pallas kernels: 16.8 us -> 14.4 us
    pallas_call x10, Pallas kernels: 16.8 us -> 14.4 us  [call(): pl.pallas_call(body, out_shape=shapes, in_specs=[pl.BlockSpec(memory_spac...]
where the time goes in v4:
time: 67.3 us; the launch traced here: 66.7 us
  blocking collectives  25 us (37%)
  Pallas kernels  14.4 us (21%)
  starting transfers between devices  12.8 us (19%)
  waiting for transfers between devices  11.4 us (17%)
  local copies, waits for them, and re-layouts  1.44 us (2%)
  other arithmetic  0.97 us (1%)
  between operations  0.77 us (1%)
    pallas_call x10, Pallas kernels, call(): pl.pallas_call(body, out_shape=shapes, in_specs=[pl.BlockSpec(memory_spac...  14.4 us
    ppermute x8, starting transfers between devices, exchanged(): lax.ppermute(values, axis, [pair for i in range(first, count - 1, 2) for...  12.8 us
    all_to_all x1, blocking collectives, on_device(): back = lax.all_to_all(grad, axes, split_axis=0, concat_axis=0, tiled=True)  12.8 us
    all_to_all x1, blocking collectives, on_device(): got = lax.all_to_all(packed, axes, split_axis=0, concat_axis=0, tiled=True)  12.2 us
    ppermute x8, waiting for transfers between devices, exchanged(): lax.ppermute(values, axis, [pair for i in range(first, count - 1, 2) for...  11.4 us
  transfers between devices with their start and end apart: 8, of which 5 were waited for; matrix products, arithmetic and copies ran while one was open for 2% of the time, Pallas kernels for 8%

profile of v4, /device:TPU:12, one launch (start us, length us, event | category | flops | bytes accessed | tf_op | source)
XLA Modules:
  0.0 66.7 jit_solution(11796590504658993623)
XLA Ops:
  0.6 1.0 %bitcast_convert_fusion = bf16[256,256]{1,0:T(8,128)(2,1)S(1)} fusion(f32[16,16,256]{2,1,0:T(8,128)} %param.9), kind=kLoop, calls=%fused_computation | loop fusion | flops 65536 | bytes 393216 | tf_op jit(solution)/shard_map/convert_element_type | solution.py:340
  1.6 3.5 %collective-permute-start.1 = (bf16[256,256]{1,0:T(8,128)(2,1)S(1)}, bf16[256,256]{1,0:T(8,128)(2,1)S(1)}, u32[]{:S(2)}, u32[]{:S(2)}) collective-permute-start(bf16[256,256]{1,0:T(8,128)(2,1)S(1)} %bitcast_convert_fusion), channel_id=1, source_target_pairs={{8,16},{16,8},{9,17},{17,9},{10,18},{18,10},{11,19},{19,11},{12,20... | collective-permute-start | bytes 393224 | tf_op jit(solution)/shard_map/ppermute | solution.py:316
  5.1 0.1 collective-permute-start
  5.2 0.8 %copy.12 = s32[1,32,16]{2,1,0:T(8,128)S(1)} copy(s32[1,32,16]{1,2,0:T(8,128)} %param.17) | data formatting | bytes 4096 | tf_op args[8]
  5.9 0.7 reshape.34.after_hbm.send_hbm
  6.6 2.3 %operators.1 = (bf16[6,256,256]{2,1,0:T(8,128)(2,1)S(1)}, bf16[6,256,256]{2,1,0:T(8,128)(2,1)S(1)}, bf16[2,256,256]{2,1,0:T(8,128)(2,1)S(1)}, f32[256,256]{1,0:T(8,128)S(1)}, bf16[256,64,128]{2,1,0:T(8,128)(2,1)S(1)}) custom-call(f32[256,256]{1,0:T(8,128)} %bitcast.12, bf16[512,64,128]{2,1,0:T(8,128)(2,1)} %resp_hbm.3, s32[1,512]{1,0:T(1,128)} %reshape.34.after_hbm.send_hbm), custom_call_target="tpu_custom_call" | custom-call | bytes 14944256 | tf_op jit(solution)/shard_map/operators/pallas_call | solution.py:72
  8.9 0.0 collective-permute-done.1.far_ref
  8.9 1.2 %collective-permute-done.near_ref = bf16[256,256]{1,0:T(8,128)(2,1)S(1)} collective-permute-done((bf16[256,256]{1,0:T(8,128)(2,1)S(1)}, bf16[256,256]{1,0:T(8,128)(2,1)S(1)}, u32[]{:S(2)}, u32[]{:S(2)}) %collective-permute-start) | collective-permute-done | bytes 131104 | tf_op jit(solution)/shard_map/ppermute | solution.py:316
  10.1 0.3 along_x.1
  10.4 1.9 %collective-permute-start.3 = (bf16[256,256]{1,0:T(8,128)(2,1)S(1)}, bf16[256,256]{1,0:T(8,128)(2,1)S(1)}, u32[]{:S(2)}, u32[]{:S(2)}) collective-permute-start(bf16[256,256]{1,0:T(8,128)(2,1)S(1)} %get-tuple-element.35), channel_id=1, source_target_pairs={{1,2},{2,1},{3,4},{4,3},{5,6},{6,5},{9,10},{10,9},{11,12},{12,11},... | collective-permute-start | bytes 393224 | tf_op jit(solution)/shard_map/ppermute | solution.py:316
  12.4 1.7 %collective-permute-start.2 = (bf16[256,256]{1,0:T(8,128)(2,1)S(1)}, bf16[256,256]{1,0:T(8,128)(2,1)S(1)}, u32[]{:S(2)}, u32[]{:S(2)}) collective-permute-start(bf16[256,256]{1,0:T(8,128)(2,1)S(1)} %get-tuple-element.35), channel_id=1, source_target_pairs={{0,1},{1,0},{2,3},{3,2},{4,5},{5,4},{6,7},{7,6},{8,9},{9,8},{10,11... | collective-permute-start | bytes 393224 | tf_op jit(solution)/shard_map/ppermute | solution.py:316
  14.0 2.8 %tables.1 = (f32[256,256]{1,0:T(8,128)S(1)}, bf16[256,64,128]{2,1,0:T(8,128)(2,1)S(1)}, f32[8,128]{1,0:T(8,128)S(1)}, f32[8,128]{1,0:T(8,128)S(1)}, s32[512,128]...) custom-call(s32[64,512]{1,0:T(8,128)} %off_hbm.1, ...), custom_call_target="tpu_custom_call" | custom-call | bytes 16668672 | tf_op jit(solution)/shard_map/tables/pallas_call | solution.py:72
  16.8 1.3 %collective-permute-done.3.far_ref = bf16[256,256]{1,0:T(8,128)(2,1)S(1)} collective-permute-done((bf16[256,256]{1,0:T(8,128)(2,1)S(1)}, bf16[256,256]{1,0:T(8,128)(2,1)S(1)}, u32[]{:S(2)}, u32[]{:S(2)}) %collective-permute-start.3) | collective-permute-done | bytes 131104 | tf_op jit(solution)/shard_map/ppermute | solution.py:316
  18.1 0.0 collective-permute-done.2.near_ref
  18.1 0.9 %density.1 = (f32[256,256]{1,0:T(8,128)S(1)}, bf16[512,256]{1,0:T(8,128)(2,1)S(1)}) custom-call(f32[256,256]{1,0:T(8,128)S(1)} %get-tuple-element.34.part_ref, bf16[256,256]{1,0:T(8,128)(2,1)S(1)} %collective-permute-done.2.near_ref, bf16[256,256]{1,0:T(8,128)(2,1)S(1)} %collective-permute-done.3.far_ref, ...), custom_call_target="tpu_custom_call" | custom-call | bytes 2359296 | tf_op jit(solution)/shard_map/density/pallas_call | solution.py:72
  19.1 12.2 %all_to_all.22 = bf16[32,16,256]{2,1,0:T(8,128)(2,1)S(1)} all-to-all(bf16[32,16,256]{2,1,0:T(8,128)(2,1)S(1)} %bitcast.17), channel_id=1, replica_groups=mesh['cx'=4,'cy'=8] {'cx','cy'}, dimensions={0} | all-to-all | bytes 524288 | tf_op jit(solution)/shard_map/all_to_all | solution.py:388
  31.2 5.7 %cones.1 = (f32[8,128]{1,0:T(8,128)}, bf16[512,256]{1,0:T(8,128)(2,1)S(1)}) custom-call(bf16[512,256]{1,0:T(8,128)(2,1)S(1)} %bitcast.14, bf16[256,64,128]{2,1,0:T(8,128)(2,1)S(1)} %get-tuple-element.38.early_ref, bf16[256,64,128]{2,1,0:T(8,128)(2,1)S(1)} %get-tuple-element.39.late_ref, s32[512,128]{1,0:T(8,128)S(1)} %get-tuple-element.40.idx_ref, ...), custom_call_target="tpu_custom_call" | custom-call | bytes 10629120 | tf_op jit(solution)/shard_map/cones/pallas_call | solution.py:72
  36.9 0.0 copy-start
  36.9 12.8 %all_to_all.23 = bf16[32,16,256]{2,1,0:T(8,128)(2,1)S(1)} all-to-all(bf16[32,16,256]{2,1,0:T(8,128)(2,1)S(1)} %bitcast.16), channel_id=1, replica_groups=mesh['cx'=4,'cy'=8] {'cx','cy'}, dimensions={0} | all-to-all | bytes 524288 | tf_op jit(solution)/shard_map/all_to_all | solution.py:396
  49.7 0.5 owners.1
  50.3 2.9 %collective-permute-start.5 = (bf16[256,256]{1,0:T(8,128)(2,1)S(1)}, bf16[256,256]{1,0:T(8,128)(2,1)S(1)}, u32[]{:S(2)}, u32[]{:S(2)}) collective-permute-start(bf16[256,256]{1,0:T(8,128)(2,1)S(1)} %get-tuple-element.50), channel_id=1, source_target_pairs={{1,2},{2,1},{3,4},{4,3},{5,6},{6,5},{9,10},{10,9},{11,12},{12,11},... | collective-permute-start | bytes 393224 | tf_op jit(solution)/shard_map/ppermute | solution.py:316
  53.2 0.1 collective-permute-start.4
  53.3 0.3 own_y.1.part_ref
  53.5 4.5 %collective-permute-done.5.far_ref = bf16[256,256]{1,0:T(8,128)(2,1)S(1)} collective-permute-done((bf16[256,256]{1,0:T(8,128)(2,1)S(1)}, bf16[256,256]{1,0:T(8,128)(2,1)S(1)}, u32[]{:S(2)}, u32[]{:S(2)}) %collective-permute-start.5) | collective-permute-done | bytes 131104 | tf_op jit(solution)/shard_map/ppermute | solution.py:316
  58.1 0.0 collective-permute-done.4.near_ref
  58.1 0.3 along_y.1
  58.4 2.2 %collective-permute-start.7 = (bf16[256,256]{1,0:T(8,128)(2,1)S(1)}, bf16[256,256]{1,0:T(8,128)(2,1)S(1)}, u32[]{:S(2)}, u32[]{:S(2)}) collective-permute-start(bf16[256,256]{1,0:T(8,128)(2,1)S(1)} %get-tuple-element.52), channel_id=1, source_target_pairs={{8,16},{16,8},{9,17},{17,9},{10,18},{18,10},{11,19},{19,11},{12,20... | collective-permute-start | bytes 393224 | tf_op jit(solution)/shard_map/ppermute | solution.py:316
  60.6 0.4 collective-permute-start.6
  61.0 0.0 copy-done
  61.1 0.3 own_x.1.part_ref
  61.3 3.9 %collective-permute-done.7.far_ref = bf16[256,256]{1,0:T(8,128)(2,1)S(1)} collective-permute-done((bf16[256,256]{1,0:T(8,128)(2,1)S(1)}, bf16[256,256]{1,0:T(8,128)(2,1)S(1)}, u32[]{:S(2)}, u32[]{:S(2)}) %collective-permute-start.7) | collective-permute-done | bytes 131104 | tf_op jit(solution)/shard_map/ppermute | solution.py:316
  65.2 0.4 collective-permute-done.6.near_ref
  65.7 1.0 %finish.1 = f32[256,256]{1,0:T(8,128)} custom-call(f32[256,256]{1,0:T(8,128)S(1)} %own_x.1.part_ref, bf16[256,256]{1,0:T(8,128)(2,1)S(1)} %collective-permute-done.6.near_ref, bf16[256,256]{1,0:T(8,128)(2,1)S(1)} %collective-permute-done.7.far_ref, bf16[6,256,256]{2,1,0:T(8,128)(2,1)S(1)} %get-tuple-element.29.mats_ref), custom_call_target="tpu_custom_call" | custom-call | bytes 1572864 | tf_op jit(solution)/shard_map/finish/pallas_call | solution.py:72
Async XLA Ops:
  1.6 7.3 %collective-permute-start.1 = (bf16[256,256]{1,0:T(8,128)(2,1)S(1)}, bf16[256,256]{1,0:T(8,128)(2,1)S(1)}, u32[]{:S(2)}, u32[]{:S(2)}) collective-permute-start(bf16[256,256]{1,0:T(8,128)(2,1)S(1)} %bitcast_convert_fusion), channel_id=1, source_target_pairs={{8,16},{16,8},{9,17},{17,9},{10,18},{18,10},{11,19},{19,11},{12,20... | collective-permute-start | bytes 393224 | tf_op jit(solution)/shard_map/ppermute | solution.py:316
  5.1 5.0 %collective-permute-start = (bf16[256,256]{1,0:T(8,128)(2,1)S(1)}, bf16[256,256]{1,0:T(8,128)(2,1)S(1)}, u32[]{:S(2)}, u32[]{:S(2)}) collective-permute-start(bf16[256,256]{1,0:T(8,128)(2,1)S(1)} %bitcast_convert_fusion), channel_id=1, source_target_pairs={{0,8},{8,0},{16,24},{24,16},{1,9},{9,1},{17,25},{25,17},{2,10},{10... | collective-permute-start | bytes 393224 | tf_op jit(solution)/shard_map/ppermute | solution.py:316
  10.4 7.7 %collective-permute-start.3 = (bf16[256,256]{1,0:T(8,128)(2,1)S(1)}, bf16[256,256]{1,0:T(8,128)(2,1)S(1)}, u32[]{:S(2)}, u32[]{:S(2)}) collective-permute-start(bf16[256,256]{1,0:T(8,128)(2,1)S(1)} %get-tuple-element.35), channel_id=1, source_target_pairs={{1,2},{2,1},{3,4},{4,3},{5,6},{6,5},{9,10},{10,9},{11,12},{12,11},... | collective-permute-start | bytes 393224 | tf_op jit(solution)/shard_map/ppermute | solution.py:316
  12.4 5.8 %collective-permute-start.2 = (bf16[256,256]{1,0:T(8,128)(2,1)S(1)}, bf16[256,256]{1,0:T(8,128)(2,1)S(1)}, u32[]{:S(2)}, u32[]{:S(2)}) collective-permute-start(bf16[256,256]{1,0:T(8,128)(2,1)S(1)} %get-tuple-element.35), channel_id=1, source_target_pairs={{0,1},{1,0},{2,3},{3,2},{4,5},{5,4},{6,7},{7,6},{8,9},{9,8},{10,11... | collective-permute-start | bytes 393224 | tf_op jit(solution)/shard_map/ppermute | solution.py:316
  36.9 24.1 %copy-start = (f32[16,16,256]{2,1,0:T(8,128)S(1)}, f32[16,16,256]{2,1,0:T(8,128)}, u32[]{:S(2)}) copy-start(f32[16,16,256]{2,1,0:T(8,128)} %param.9) | copy-start | bytes 786436
  50.3 7.8 %collective-permute-start.5 = (bf16[256,256]{1,0:T(8,128)(2,1)S(1)}, bf16[256,256]{1,0:T(8,128)(2,1)S(1)}, u32[]{:S(2)}, u32[]{:S(2)}) collective-permute-start(bf16[256,256]{1,0:T(8,128)(2,1)S(1)} %get-tuple-element.50), channel_id=1, source_target_pairs={{1,2},{2,1},{3,4},{4,3},{5,6},{6,5},{9,10},{10,9},{11,12},{12,11},... | collective-permute-start | bytes 393224 | tf_op jit(solution)/shard_map/ppermute | solution.py:316
  53.2 4.9 %collective-permute-start.4 = (bf16[256,256]{1,0:T(8,128)(2,1)S(1)}, bf16[256,256]{1,0:T(8,128)(2,1)S(1)}, u32[]{:S(2)}, u32[]{:S(2)}) collective-permute-start(bf16[256,256]{1,0:T(8,128)(2,1)S(1)} %get-tuple-element.50), channel_id=1, source_target_pairs={{0,1},{1,0},{2,3},{3,2},{4,5},{5,4},{6,7},{7,6},{8,9},{9,8},{10,11... | collective-permute-start | bytes 393224 | tf_op jit(solution)/shard_map/ppermute | solution.py:316
  58.4 6.9 %collective-permute-start.7 = (bf16[256,256]{1,0:T(8,128)(2,1)S(1)}, bf16[256,256]{1,0:T(8,128)(2,1)S(1)}, u32[]{:S(2)}, u32[]{:S(2)}) collective-permute-start(bf16[256,256]{1,0:T(8,128)(2,1)S(1)} %get-tuple-element.52), channel_id=1, source_target_pairs={{8,16},{16,8},{9,17},{17,9},{10,18},{18,10},{11,19},{19,11},{12,20... | collective-permute-start | bytes 393224 | tf_op jit(solution)/shard_map/ppermute | solution.py:316
  60.6 5.0 %collective-permute-start.6 = (bf16[256,256]{1,0:T(8,128)(2,1)S(1)}, bf16[256,256]{1,0:T(8,128)(2,1)S(1)}, u32[]{:S(2)}, u32[]{:S(2)}) collective-permute-start(bf16[256,256]{1,0:T(8,128)(2,1)S(1)} %get-tuple-element.52), channel_id=1, source_target_pairs={{0,8},{8,0},{16,24},{24,16},{1,9},{9,1},{17,25},{25,17},{2,10},{10... | collective-permute-start | bytes 393224 | tf_op jit(solution)/shard_map/ppermute | solution.py:316

commit v5 on v4

--- a/solution.py
+++ b/solution.py
@@ -15,6 +15,7 @@
 AHEAD = 256
 CHUNK = 256
 GIVE = 256
+FETCHES = 4
 PART = 32
 
 
@@ -120,62 +121,91 @@
     return copies
 
 
+def fetch_rays(resp_hbm, first, resp_ref, sems):
+    chunk = resp_ref.shape[0] // FETCHES
+    return fetch(
+        [
+            (resp_hbm.at[pl.ds(first + at, chunk)], resp_ref.at[pl.ds(at, chunk)])
+            for at in range(0, resp_ref.shape[0], chunk)
+        ],
+        sems,
+    )
+
+
+def flip_rays(copies, resp_ref, flip_ref):
+    tiles, samples, star_tile = resp_ref.shape
+    chunk = tiles // FETCHES
+    for copy, first in zip(copies, range(0, tiles, chunk)):
+        copy.wait()
+        rows = resp_ref[first : first + chunk].reshape(chunk * samples, star_tile)
+        flip_ref[:, first * samples : (first + chunk) * samples] = rows.T
+
+
 def operators_body(
-    rows_x, rows_y, own_hbm, resp_hbm, after_hbm,
-    hx_ref, hy_ref, hz_ref, part_ref, resp_ref, own_ref, sems,
+    rows_x, rows_y, own_hbm, group_hbm, slot_hbm, resp_hbm,
+    hx_ref, hy_ref, hz_ref, part_ref, resp_ref, flip_ref, grp_ref, take_ref, give_ref,
+    own_ref, group_ref, slot_ref, keep, sems, ray_sems,
 ):
-    count = resp_ref.shape[0]
-    copies = fetch([(own_hbm, own_ref), (resp_hbm.at[pl.ds(0, count)], resp_ref)], sems)
+    copies = fetch([(own_hbm, own_ref), (group_hbm, group_ref), (slot_hbm, slot_ref)], sems)
+    ray_copies = fetch_rays(resp_hbm, 0, resp_ref, ray_sems)
     operators(rows_x, rows_y, hz_ref.shape[1], hx_ref, hy_ref, hz_ref)
-    copies[0].wait()
+    for copy in copies:
+        copy.wait()
     part_ref[...] = apply_left(hx_ref[0], hx_ref[1], own_ref[...])
-    copies[1].wait()
-
-
-def tables_body(
-    off_hbm, frac_hbm, group_hbm, slot_hbm, send_hbm, obs_hbm, sig_hbm, resp_hbm,
-    field_ref, hy_ref, hz_ref,
-    part_ref, resp_ref, obs_ref, var_ref, idx_ref, w_ref, grp_ref, take_ref, give_ref, pack_ref, sum_ref,
-    off_ref, frac_ref, group_ref, slot_ref, send_ref, sig_ref, keep, sems,
-):
-    count = resp_ref.shape[0]
-    copies = fetch(
-        [
-            (send_hbm, send_ref), (slot_hbm, slot_ref), (group_hbm, group_ref),
-            (off_hbm, off_ref), (frac_hbm, frac_ref), (obs_hbm, obs_ref), (sig_hbm, sig_ref),
-            (resp_hbm.at[pl.ds(resp_hbm.shape[0] - count, count)], resp_ref),
-        ],
-        sems,
-    )
-    part = apply_left(hy_ref[0], hy_ref[1], field_ref[...])
-    part_ref[...] = apply_right(part, hz_ref[0], hz_ref[1])
-    for copy in copies[:-1]:
-        copy.wait()
-    sig = sig_ref[...]
-    var_ref[...] = sig * sig
-    tiles = off_ref.shape[1]
-    slots = take_ref.shape[1]
-    cells = pack_ref.shape[1]
-    off = off_ref[...]
-    frac = frac_ref[...]
-    idx_ref[...] = jnp.concatenate([off, off + 1], axis=0).T
-    w_ref[...] = jnp.concatenate([1.0 - frac, frac], axis=0).T
+    tiles, slots = take_ref.shape
     keep[...] = jnp.broadcast_to(group_ref[...], (LANES, tiles)).T
-    first = iota((tiles // 2, LANES), 1) < LANES // 2
+    lane_first = iota((tiles // 2, LANES), 1) < LANES // 2
     grp_ref[...] = jnp.where(
-        first, keep[pl.ds(0, tiles // 2, 2), :], keep[pl.ds(1, tiles // 2, 2), :]
+        lane_first, keep[pl.ds(0, tiles // 2, 2), :], keep[pl.ds(1, tiles // 2, 2), :]
     )
     slot = slot_ref[...]
     wide = jnp.broadcast_to(slot, (LANES, tiles)).T
     for at in range(0, slots, LANES):
         take_ref[:, at : at + LANES] = one_hot(wide == iota((tiles, LANES), 1) + at)
     give_ref[...] = one_hot(jnp.broadcast_to(slot, (slots, tiles)) == iota((slots, tiles), 0))
-    send = send_ref[...]
-    wide = jnp.broadcast_to(send, (LANES, slots)).T
+    flip_rays(ray_copies, resp_ref, flip_ref)
+
+
+def tables_body(
+    off_hbm, frac_hbm, send_hbm, obs_hbm, sig_hbm, resp_hbm,
+    field_ref, hy_ref, hz_ref,
+    part_ref, resp_ref, flip_ref, obs_ref, var_ref,
+    idx_ref, w_ref, pack_ref, sum_ref,
+    off_ref, frac_ref, send_ref, sig_ref, sems, ray_sems,
+):
+    copies = fetch(
+        [
+            (off_hbm, off_ref), (frac_hbm, frac_ref), (send_hbm, send_ref),
+            (obs_hbm, obs_ref), (sig_hbm, sig_ref),
+        ],
+        sems,
+    )
+    first = resp_hbm.shape[0] - resp_ref.shape[0]
+    ray_copies = fetch_rays(resp_hbm, first, resp_ref, ray_sems)
+    part = apply_left(hy_ref[0], hy_ref[1], field_ref[...])
+    part_ref[...] = apply_right(part, hz_ref[0], hz_ref[1])
+    for copy in copies:
+        copy.wait()
+    sig = sig_ref[...]
+    var_ref[...] = sig * sig
+    slots, cells = pack_ref.shape
+    off = off_ref[...]
+    frac = frac_ref[...]
+    idx_ref[...] = jnp.concatenate([off, off + 1], axis=0).T
+    w_ref[...] = jnp.concatenate([1.0 - frac, frac], axis=0).T
+    capacity, devices = send_ref.shape
+    wide = jnp.concatenate(
+        [
+            jnp.broadcast_to(send_ref[:, at : at + 1], (capacity, LANES))
+            for at in range(devices)
+        ],
+        axis=0,
+    )
     for at in range(0, cells, LANES):
         pack_ref[:, at : at + LANES] = one_hot(wide == iota((slots, LANES), 1) + at)
+    send = wide.T[0:1]
     sum_ref[...] = one_hot(jnp.broadcast_to(send, (cells, slots)) == iota((cells, slots), 0))
-    copies[-1].wait()
+    flip_rays(ray_copies, resp_ref, flip_ref)
 
 
 def sides(mats_ref, near, far):
@@ -212,7 +242,7 @@
 
 
 def cone_body(
-    got_ref, early_ref, late_ref, idx_ref, w_ref, grp_ref, take_ref, give_ref, obs_ref, var_ref,
+    got_ref, early_ref, late_ref, flip_early_ref, flip_late_ref, idx_ref, w_ref, grp_ref, take_ref, give_ref, obs_ref, var_ref,
     pred_ref, grad_ref, both, cells,
 ):
     early, samples, star_tile = early_ref.shape
@@ -224,6 +254,10 @@
     def rays(first, count):
         ref, first = (early_ref, first) if first < early else (late_ref, first - early)
         return ref[first : first + count].reshape(count * samples, star_tile)
+
+    def flipped(first, count):
+        ref, first = (flip_early_ref, first) if first < early else (flip_late_ref, first - early)
+        return ref[:, first * samples : (first + count) * samples]
 
     group_at = iota((groups, LANES), 0)
     lane_first = iota((AHEAD // 2, LANES), 1) < half
@@ -265,7 +299,7 @@
     total = jnp.zeros(grad_ref.shape, F32)
     lane_first = iota((CHUNK // 2, LANES), 1) < half
     for base in range(0, tiles, CHUNK):
-        back = mm_nt(resid, rays(base, CHUNK))
+        back = mm(resid, flipped(base, CHUNK))
         group = grp_ref[pl.ds(base // 2, CHUNK // 2), :]
         picked = [
             jnp.sum(
@@ -335,49 +369,54 @@
     field_out = ((cells, depth), F32)
     sent_out = ((cells, depth), BF16)
 
-    send = send_index.reshape(1, slots)
+    send = send_index.reshape(devices, -1).T
+    flip_out = ((star_tile, tiles // 2 * samples), BF16)
     ray_out = ((tiles // 2, samples, star_tile), BF16)
     near, far = exchanged(own.astype(BF16), "cx")
-    hx, hy, hz, part, early = call(
+    hx, hy, hz, part, early, flip_early, grp, take, give = call(
         functools.partial(operators_body, rows_x, rows_y),
         [
             ((6, cells, cells), BF16), ((6, cells, cells), BF16), ((2, depth, depth), BF16),
-            field_out, ray_out,
-        ],
-        hbm(own), hbm(response), hbm(send),
-        scratch=[pltpu.VMEM((cells, depth), F32), pltpu.SemaphoreType.DMA((2,))],
+            field_out, ray_out, flip_out,
+            ((tiles // 2, LANES), jnp.int32), ((tiles, slots), BF16), ((slots, tiles), BF16),
+        ],
+        hbm(own), hbm(tile_group.reshape(1, tiles)), hbm(tile_slot.reshape(1, tiles)),
+        hbm(response),
+        scratch=[
+            pltpu.VMEM((cells, depth), F32),
+            pltpu.VMEM((1, tiles), jnp.int32),
+            pltpu.VMEM((1, tiles), jnp.int32),
+            pltpu.VMEM((tiles, LANES), jnp.int32),
+            pltpu.SemaphoreType.DMA((3,)),
+            pltpu.SemaphoreType.DMA((FETCHES,)),
+        ],
         name="operators",
     )
     field, sent = call(join_body, [field_out, sent_out], part, near, far, hx, name="along_x")
     near, far = exchanged(sent, "cy")
-    part, late, obs, var, idx, weight, grp, take, give, pack, add_up = call(
+    part, late, flip_late, obs, var, idx, weight, pack, add_up = call(
         tables_body,
         [
             field_out,
             ray_out,
+            flip_out,
             ((groups, star_tile), F32),
             ((groups, star_tile), F32),
             ((tiles, LANES), jnp.int32),
             ((tiles, LANES), F32),
-            ((tiles // 2, LANES), jnp.int32),
-            ((tiles, slots), BF16),
-            ((slots, tiles), BF16),
             ((slots, cells), BF16),
             ((cells, slots), BF16),
         ],
-        hbm(offsets), hbm(fractions), hbm(tile_group.reshape(1, tiles)),
-        hbm(tile_slot.reshape(1, tiles)), hbm(send),
+        hbm(offsets), hbm(fractions), hbm(send),
         hbm(observed.reshape(groups, star_tile)), hbm(sigma.reshape(groups, star_tile)),
         hbm(response), field, hy, hz,
         scratch=[
             pltpu.VMEM((samples, tiles), jnp.int32),
             pltpu.VMEM((samples, tiles), F32),
-            pltpu.VMEM((1, tiles), jnp.int32),
-            pltpu.VMEM((1, tiles), jnp.int32),
-            pltpu.VMEM((1, slots), jnp.int32),
+            pltpu.VMEM(send.shape, jnp.int32),
             pltpu.VMEM((groups, star_tile), F32),
-            pltpu.VMEM((tiles, LANES), jnp.int32),
-            pltpu.SemaphoreType.DMA((8,)),
+            pltpu.SemaphoreType.DMA((5,)),
+            pltpu.SemaphoreType.DMA((FETCHES,)),
         ],
         name="tables",
     )
@@ -388,7 +427,7 @@
     got = lax.all_to_all(packed, axes, split_axis=0, concat_axis=0, tiled=True)
     pred, grad = call(
         cone_body, [((groups, star_tile), F32), ((slots, depth), BF16)],
-        got, early, late, idx, weight, grp, take, give, obs, var,
+        got, early, late, flip_early, flip_late, idx, weight, grp, take, give, obs, var,
         scratch=cone_scratch(tiles, depth),
         limit=20,
         name="cones",

time: 67.3 us -> 66 us (0.981)
  local copies, waits for them, and re-layouts: 1.44 us -> 0.01 us
  Pallas kernels: 14.4 us -> 15.4 us
    pallas_call x10, Pallas kernels: 14.4 us -> 15.4 us  [call(): pl.pallas_call(body, out_shape=shapes, in_specs=[pl.BlockSpec(memory_spac...]
    unnamed x3 -> x2, local copies, waits for them, and re-layouts: 0.78 us -> 0.01 us
  transfers between devices with their start and end apart: 8 -> 8, of which waited for: 5 -> 5; matrix products, arithmetic and copies ran while one was open for 2% -> 0% of each run, Pallas kernels for 8% -> 12%
where the time goes in v5:
time: 66 us; the launch traced here: 65.4 us
  blocking collectives  24.7 us (37%)
  Pallas kernels  15.4 us (23%)
  starting transfers between devices  12.8 us (19%)
  waiting for transfers between devices  10.8 us (16%)
  other arithmetic  0.97 us (1%)
  between operations  0.76 us (1%)
    pallas_call x10, Pallas kernels, call(): pl.pallas_call(body, out_shape=shapes, in_specs=[pl.BlockSpec(memory_spac...  15.4 us
    ppermute x8, starting transfers between devices, exchanged(): lax.ppermute(values, axis, [pair for i in range(first, count - 1, 2) for...  12.8 us
    all_to_all x1, blocking collectives, on_device(): back = lax.all_to_all(grad, axes, split_axis=0, concat_axis=0, tiled=True)  12.8 us
    all_to_all x1, blocking collectives, on_device(): got = lax.all_to_all(packed, axes, split_axis=0, concat_axis=0, tiled=True)  12 us
    ppermute x8, waiting for transfers between devices, exchanged(): lax.ppermute(values, axis, [pair for i in range(first, count - 1, 2) for...  10.8 us
  transfers between devices with their start and end apart: 8, of which 5 were waited for; matrix products, arithmetic and copies ran while one was open for 0% of the time, Pallas kernels for 12%

profile of v5, /device:TPU:12, one launch (start us, length us, event | category | flops | bytes accessed | tf_op | source)
XLA Modules:
  0.0 65.4 jit_solution(9687870692123917102)
XLA Ops:
  0.6 1.0 %bitcast_convert_fusion = bf16[256,256]{1,0:T(8,128)(2,1)S(1)} fusion(f32[16,16,256]{2,1,0:T(8,128)} %param.9), kind=kLoop, calls=%fused_computation | loop fusion | flops 65536 | bytes 393216 | tf_op jit(solution)/shard_map/convert_element_type | solution.py:375
  1.6 3.5 %collective-permute-start.1 = (bf16[256,256]{1,0:T(8,128)(2,1)S(1)}, bf16[256,256]{1,0:T(8,128)(2,1)S(1)}, u32[]{:S(2)}, u32[]{:S(2)}) collective-permute-start(bf16[256,256]{1,0:T(8,128)(2,1)S(1)} %bitcast_convert_fusion), channel_id=1, source_target_pairs={{8,16},{16,8},{9,17},{17,9},{10,18},{18,10},{11,19},{19,11},{12,20... | collective-permute-start | bytes 393224 | tf_op jit(solution)/shard_map/ppermute | solution.py:350
  5.1 0.1 collective-permute-start
  5.2 3.5 %operators.1 = (bf16[6,256,256]{2,1,0:T(8,128)(2,1)S(1)}, bf16[6,256,256]{2,1,0:T(8,128)(2,1)S(1)}, bf16[2,256,256]{2,1,0:T(8,128)(2,1)S(1)}, f32[256,256]{1,0:T...) custom-call(f32[256,256]{1,0:T(8,128)} %bitcast.15, ...), custom_call_target="tpu_custom_call" | custom-call | bytes 20320256 | tf_op jit(solution)/shard_map/operators/pallas_call | solution.py:73
  8.7 0.0 collective-permute-done.1.far_ref
  8.7 1.4 %collective-permute-done.near_ref = bf16[256,256]{1,0:T(8,128)(2,1)S(1)} collective-permute-done((bf16[256,256]{1,0:T(8,128)(2,1)S(1)}, bf16[256,256]{1,0:T(8,128)(2,1)S(1)}, u32[]{:S(2)}, u32[]{:S(2)}) %collective-permute-start) | collective-permute-done | bytes 131104 | tf_op jit(solution)/shard_map/ppermute | solution.py:350
  10.1 0.3 along_x.1
  10.4 1.9 %collective-permute-start.3 = (bf16[256,256]{1,0:T(8,128)(2,1)S(1)}, bf16[256,256]{1,0:T(8,128)(2,1)S(1)}, u32[]{:S(2)}, u32[]{:S(2)}) collective-permute-start(bf16[256,256]{1,0:T(8,128)(2,1)S(1)} %get-tuple-element.37), channel_id=1, source_target_pairs={{1,2},{2,1},{3,4},{4,3},{5,6},{6,5},{9,10},{10,9},{11,12},{12,11},... | collective-permute-start | bytes 393224 | tf_op jit(solution)/shard_map/ppermute | solution.py:350
  12.4 1.7 %collective-permute-start.2 = (bf16[256,256]{1,0:T(8,128)(2,1)S(1)}, bf16[256,256]{1,0:T(8,128)(2,1)S(1)}, u32[]{:S(2)}, u32[]{:S(2)}) collective-permute-start(bf16[256,256]{1,0:T(8,128)(2,1)S(1)} %get-tuple-element.37), channel_id=1, source_target_pairs={{0,1},{1,0},{2,3},{3,2},{4,5},{5,4},{6,7},{7,6},{8,9},{9,8},{10,11... | collective-permute-start | bytes 393224 | tf_op jit(solution)/shard_map/ppermute | solution.py:350
  14.0 3.6 %tables.1 = (f32[256,256]{1,0:T(8,128)S(1)}, bf16[256,64,128]{2,1,0:T(8,128)(2,1)S(1)}, bf16[128,16384]{1,0:T(8,128)(2,1)S(1)}, f32[8,128]{1,0:T(8,128)S(1)}, f3...) custom-call(s32[64,512]{1,0:T(8,128)} %off_hbm.1, ...), custom_call_target="tpu_custom_call" | custom-call | bytes 19679232 | tf_op jit(solution)/shard_map/tables/pallas_call | solution.py:73
  17.6 0.5 collective-permute-done.3.far_ref
  18.1 0.0 collective-permute-done.2.near_ref
  18.1 0.9 %density.1 = (f32[256,256]{1,0:T(8,128)S(1)}, bf16[512,256]{1,0:T(8,128)(2,1)S(1)}) custom-call(f32[256,256]{1,0:T(8,128)S(1)} %get-tuple-element.36.part_ref, bf16[256,256]{1,0:T(8,128)(2,1)S(1)} %collective-permute-done.2.near_ref, bf16[256,256]{1,0:T(8,128)(2,1)S(1)} %collective-permute-done.3.far_ref, ...), custom_call_target="tpu_custom_call" | custom-call | bytes 2359296 | tf_op jit(solution)/shard_map/density/pallas_call | solution.py:73
  19.1 12.0 %all_to_all.22 = bf16[32,16,256]{2,1,0:T(8,128)(2,1)S(1)} all-to-all(bf16[32,16,256]{2,1,0:T(8,128)(2,1)S(1)} %bitcast.20), channel_id=1, replica_groups=mesh['cx'=4,'cy'=8] {'cx','cy'}, dimensions={0} | all-to-all | bytes 524288 | tf_op jit(solution)/shard_map/all_to_all | solution.py:427
  31.0 4.7 %cones.1 = (f32[8,128]{1,0:T(8,128)}, bf16[512,256]{1,0:T(8,128)(2,1)S(1)}) custom-call(bf16[512,256]{1,0:T(8,128)(2,1)S(1)} %bitcast.17, bf16[256,64,128]{2,1,0:T(8,128)(2,1)S(1)} %get-tuple-element.40.early_ref, bf16[256,64,128]{2,1,0:T(8,128)(2,1)S(1)} %get-tuple-element.41.late_ref, bf16[128,16384]{1,0:T(8,128)(2,1)S(1)} %get-tuple-element.42.flip_early_ref, ...), custom_call_target="tpu_custom_call" | custom-call | bytes 19017728 | tf_op jit(solution)/shard_map/cones/pallas_call | solution.py:73
  35.7 0.0 copy-start
  35.7 12.8 %all_to_all.23 = bf16[32,16,256]{2,1,0:T(8,128)(2,1)S(1)} all-to-all(bf16[32,16,256]{2,1,0:T(8,128)(2,1)S(1)} %bitcast.19), channel_id=1, replica_groups=mesh['cx'=4,'cy'=8] {'cx','cy'}, dimensions={0} | all-to-all | bytes 524288 | tf_op jit(solution)/shard_map/all_to_all | solution.py:435
  48.5 0.5 owners.1
  49.0 2.9 %collective-permute-start.5 = (bf16[256,256]{1,0:T(8,128)(2,1)S(1)}, bf16[256,256]{1,0:T(8,128)(2,1)S(1)}, u32[]{:S(2)}, u32[]{:S(2)}) collective-permute-start(bf16[256,256]{1,0:T(8,128)(2,1)S(1)} %get-tuple-element.54), channel_id=1, source_target_pairs={{1,2},{2,1},{3,4},{4,3},{5,6},{6,5},{9,10},{10,9},{11,12},{12,11},... | collective-permute-start | bytes 393224 | tf_op jit(solution)/shard_map/ppermute | solution.py:350
  51.9 0.1 collective-permute-start.4
  52.0 0.3 own_y.1.part_ref
  52.3 4.5 %collective-permute-done.5.far_ref = bf16[256,256]{1,0:T(8,128)(2,1)S(1)} collective-permute-done((bf16[256,256]{1,0:T(8,128)(2,1)S(1)}, bf16[256,256]{1,0:T(8,128)(2,1)S(1)}, u32[]{:S(2)}, u32[]{:S(2)}) %collective-permute-start.5) | collective-permute-done | bytes 131104 | tf_op jit(solution)/shard_map/ppermute | solution.py:350
  56.8 0.0 collective-permute-done.4.near_ref
  56.8 0.3 along_y.1
  57.2 2.2 %collective-permute-start.7 = (bf16[256,256]{1,0:T(8,128)(2,1)S(1)}, bf16[256,256]{1,0:T(8,128)(2,1)S(1)}, u32[]{:S(2)}, u32[]{:S(2)}) collective-permute-start(bf16[256,256]{1,0:T(8,128)(2,1)S(1)} %get-tuple-element.56), channel_id=1, source_target_pairs={{8,16},{16,8},{9,17},{17,9},{10,18},{18,10},{11,19},{19,11},{12,20... | collective-permute-start | bytes 393224 | tf_op jit(solution)/shard_map/ppermute | solution.py:350
  59.4 0.4 collective-permute-start.6
  59.8 0.0 copy-done
  59.8 0.3 own_x.1.part_ref
  60.1 3.9 %collective-permute-done.7.far_ref = bf16[256,256]{1,0:T(8,128)(2,1)S(1)} collective-permute-done((bf16[256,256]{1,0:T(8,128)(2,1)S(1)}, bf16[256,256]{1,0:T(8,128)(2,1)S(1)}, u32[]{:S(2)}, u32[]{:S(2)}) %collective-permute-start.7) | collective-permute-done | bytes 131104 | tf_op jit(solution)/shard_map/ppermute | solution.py:350
  64.0 0.4 collective-permute-done.6.near_ref
  64.4 1.0 %finish.1 = f32[256,256]{1,0:T(8,128)} custom-call(f32[256,256]{1,0:T(8,128)S(1)} %own_x.1.part_ref, bf16[256,256]{1,0:T(8,128)(2,1)S(1)} %collective-permute-done.6.near_ref, bf16[256,256]{1,0:T(8,128)(2,1)S(1)} %collective-permute-done.7.far_ref, bf16[6,256,256]{2,1,0:T(8,128)(2,1)S(1)} %get-tuple-element.31.mats_ref), custom_call_target="tpu_custom_call" | custom-call | bytes 1572864 | tf_op jit(solution)/shard_map/finish/pallas_call | solution.py:73
Async XLA Ops:
  1.6 7.1 %collective-permute-start.1 = (bf16[256,256]{1,0:T(8,128)(2,1)S(1)}, bf16[256,256]{1,0:T(8,128)(2,1)S(1)}, u32[]{:S(2)}, u32[]{:S(2)}) collective-permute-start(bf16[256,256]{1,0:T(8,128)(2,1)S(1)} %bitcast_convert_fusion), channel_id=1, source_target_pairs={{8,16},{16,8},{9,17},{17,9},{10,18},{18,10},{11,19},{19,11},{12,20... | collective-permute-start | bytes 393224 | tf_op jit(solution)/shard_map/ppermute | solution.py:350
  5.1 5.0 %collective-permute-start = (bf16[256,256]{1,0:T(8,128)(2,1)S(1)}, bf16[256,256]{1,0:T(8,128)(2,1)S(1)}, u32[]{:S(2)}, u32[]{:S(2)}) collective-permute-start(bf16[256,256]{1,0:T(8,128)(2,1)S(1)} %bitcast_convert_fusion), channel_id=1, source_target_pairs={{0,8},{8,0},{16,24},{24,16},{1,9},{9,1},{17,25},{25,17},{2,10},{10... | collective-permute-start | bytes 393224 | tf_op jit(solution)/shard_map/ppermute | solution.py:350
  10.4 7.7 %collective-permute-start.3 = (bf16[256,256]{1,0:T(8,128)(2,1)S(1)}, bf16[256,256]{1,0:T(8,128)(2,1)S(1)}, u32[]{:S(2)}, u32[]{:S(2)}) collective-permute-start(bf16[256,256]{1,0:T(8,128)(2,1)S(1)} %get-tuple-element.37), channel_id=1, source_target_pairs={{1,2},{2,1},{3,4},{4,3},{5,6},{6,5},{9,10},{10,9},{11,12},{12,11},... | collective-permute-start | bytes 393224 | tf_op jit(solution)/shard_map/ppermute | solution.py:350
  12.4 5.8 %collective-permute-start.2 = (bf16[256,256]{1,0:T(8,128)(2,1)S(1)}, bf16[256,256]{1,0:T(8,128)(2,1)S(1)}, u32[]{:S(2)}, u32[]{:S(2)}) collective-permute-start(bf16[256,256]{1,0:T(8,128)(2,1)S(1)} %get-tuple-element.37), channel_id=1, source_target_pairs={{0,1},{1,0},{2,3},{3,2},{4,5},{5,4},{6,7},{7,6},{8,9},{9,8},{10,11... | collective-permute-start | bytes 393224 | tf_op jit(solution)/shard_map/ppermute | solution.py:350
  35.7 24.1 %copy-start = (f32[16,16,256]{2,1,0:T(8,128)S(1)}, f32[16,16,256]{2,1,0:T(8,128)}, u32[]{:S(2)}) copy-start(f32[16,16,256]{2,1,0:T(8,128)} %param.9) | copy-start | bytes 786436
  49.0 7.8 %collective-permute-start.5 = (bf16[256,256]{1,0:T(8,128)(2,1)S(1)}, bf16[256,256]{1,0:T(8,128)(2,1)S(1)}, u32[]{:S(2)}, u32[]{:S(2)}) collective-permute-start(bf16[256,256]{1,0:T(8,128)(2,1)S(1)} %get-tuple-element.54), channel_id=1, source_target_pairs={{1,2},{2,1},{3,4},{4,3},{5,6},{6,5},{9,10},{10,9},{11,12},{12,11},... | collective-permute-start | bytes 393224 | tf_op jit(solution)/shard_map/ppermute | solution.py:350
  51.9 4.9 %collective-permute-start.4 = (bf16[256,256]{1,0:T(8,128)(2,1)S(1)}, bf16[256,256]{1,0:T(8,128)(2,1)S(1)}, u32[]{:S(2)}, u32[]{:S(2)}) collective-permute-start(bf16[256,256]{1,0:T(8,128)(2,1)S(1)} %get-tuple-element.54), channel_id=1, source_target_pairs={{0,1},{1,0},{2,3},{3,2},{4,5},{5,4},{6,7},{7,6},{8,9},{9,8},{10,11... | collective-permute-start | bytes 393224 | tf_op jit(solution)/shard_map/ppermute | solution.py:350
  57.2 6.9 %collective-permute-start.7 = (bf16[256,256]{1,0:T(8,128)(2,1)S(1)}, bf16[256,256]{1,0:T(8,128)(2,1)S(1)}, u32[]{:S(2)}, u32[]{:S(2)}) collective-permute-start(bf16[256,256]{1,0:T(8,128)(2,1)S(1)} %get-tuple-element.56), channel_id=1, source_target_pairs={{8,16},{16,8},{9,17},{17,9},{10,18},{18,10},{11,19},{19,11},{12,20... | collective-permute-start | bytes 393224 | tf_op jit(solution)/shard_map/ppermute | solution.py:350
  59.4 5.0 %collective-permute-start.6 = (bf16[256,256]{1,0:T(8,128)(2,1)S(1)}, bf16[256,256]{1,0:T(8,128)(2,1)S(1)}, u32[]{:S(2)}, u32[]{:S(2)}) collective-permute-start(bf16[256,256]{1,0:T(8,128)(2,1)S(1)} %get-tuple-element.56), channel_id=1, source_target_pairs={{0,8},{8,0},{16,24},{24,16},{1,9},{9,1},{17,25},{25,17},{2,10},{10... | collective-permute-start | bytes 393224 | tf_op jit(solution)/shard_map/ppermute | solution.py:350

commit v6 on v5

--- a/solution.py
+++ b/solution.py
@@ -47,7 +47,7 @@
 
 def apply_left(mat_high, mat_low, values):
     if values.dtype == BF16:
-        return mm(mat_high, values) + mm(mat_low, values)
+        return mm(mat_high, values)
     high, low = split(values)
     return mm(mat_high, high) + (mm(mat_high, low) + mm(mat_low, high))
 
@@ -236,7 +236,7 @@
 
 def owner_body(sum_ref, back_ref, dens_ref, hz_ref, out_ref, sent_ref):
     grad = dens_ref[...] * mm(sum_ref[...], back_ref[...])
-    out = apply_right(grad, hz_ref[0], hz_ref[1])
+    out = mm(grad.astype(BF16), hz_ref[0])
     out_ref[...] = out
     sent_ref[...] = out.astype(sent_ref.dtype)
 

time: 66 us -> 65.5 us (level)
  no operation moved by 1% of the time
where the time goes in v6:
time: 65.5 us; the launch traced here: 64.9 us
  blocking collectives  24.8 us (38%)
  Pallas kernels  14.9 us (23%)
  starting transfers between devices  12.8 us (20%)
  waiting for transfers between devices  10.8 us (16%)
  other arithmetic  0.97 us (1%)
  between operations  0.76 us (1%)
    pallas_call x10, Pallas kernels, call(): pl.pallas_call(body, out_shape=shapes, in_specs=[pl.BlockSpec(memory_spac...  14.9 us
    ppermute x8, starting transfers between devices, exchanged(): lax.ppermute(values, axis, [pair for i in range(first, count - 1, 2) for...  12.8 us
    all_to_all x1, blocking collectives, on_device(): back = lax.all_to_all(grad, axes, split_axis=0, concat_axis=0, tiled=True)  12.8 us
    all_to_all x1, blocking collectives, on_device(): got = lax.all_to_all(packed, axes, split_axis=0, concat_axis=0, tiled=True)  12 us
    ppermute x8, waiting for transfers between devices, exchanged(): lax.ppermute(values, axis, [pair for i in range(first, count - 1, 2) for...  10.8 us
  transfers between devices with their start and end apart: 8, of which 5 were waited for; matrix products, arithmetic and copies ran while one was open for 0% of the time, Pallas kernels for 12%

profile of v6, /device:TPU:12, one launch (start us, length us, event | category | flops | bytes accessed | tf_op | source)
XLA Modules:
  0.0 64.9 jit_solution(7729655531612800501)
XLA Ops:
  0.6 1.0 %bitcast_convert_fusion = bf16[256,256]{1,0:T(8,128)(2,1)S(1)} fusion(f32[16,16,256]{2,1,0:T(8,128)} %param.9), kind=kLoop, calls=%fused_computation | loop fusion | flops 65536 | bytes 393216 | tf_op jit(solution)/shard_map/convert_element_type | solution.py:375
  1.6 3.5 %collective-permute-start.1 = (bf16[256,256]{1,0:T(8,128)(2,1)S(1)}, bf16[256,256]{1,0:T(8,128)(2,1)S(1)}, u32[]{:S(2)}, u32[]{:S(2)}) collective-permute-start(bf16[256,256]{1,0:T(8,128)(2,1)S(1)} %bitcast_convert_fusion), channel_id=1, source_target_pairs={{8,16},{16,8},{9,17},{17,9},{10,18},{18,10},{11,19},{19,11},{12,20... | collective-permute-start | bytes 393224 | tf_op jit(solution)/shard_map/ppermute | solution.py:350
  5.1 0.1 collective-permute-start
  5.2 3.5 %operators.1 = (bf16[6,256,256]{2,1,0:T(8,128)(2,1)S(1)}, bf16[6,256,256]{2,1,0:T(8,128)(2,1)S(1)}, bf16[2,256,256]{2,1,0:T(8,128)(2,1)S(1)}, f32[256,256]{1,0:T...) custom-call(f32[256,256]{1,0:T(8,128)} %bitcast.15, ...), custom_call_target="tpu_custom_call" | custom-call | bytes 20320256 | tf_op jit(solution)/shard_map/operators/pallas_call | solution.py:73
  8.7 0.0 collective-permute-done.1.far_ref
  8.7 1.4 %collective-permute-done.near_ref = bf16[256,256]{1,0:T(8,128)(2,1)S(1)} collective-permute-done((bf16[256,256]{1,0:T(8,128)(2,1)S(1)}, bf16[256,256]{1,0:T(8,128)(2,1)S(1)}, u32[]{:S(2)}, u32[]{:S(2)}) %collective-permute-start) | collective-permute-done | bytes 131104 | tf_op jit(solution)/shard_map/ppermute | solution.py:350
  10.1 0.2 along_x.1
  10.4 1.9 %collective-permute-start.3 = (bf16[256,256]{1,0:T(8,128)(2,1)S(1)}, bf16[256,256]{1,0:T(8,128)(2,1)S(1)}, u32[]{:S(2)}, u32[]{:S(2)}) collective-permute-start(bf16[256,256]{1,0:T(8,128)(2,1)S(1)} %get-tuple-element.37), channel_id=1, source_target_pairs={{1,2},{2,1},{3,4},{4,3},{5,6},{6,5},{9,10},{10,9},{11,12},{12,11},... | collective-permute-start | bytes 393224 | tf_op jit(solution)/shard_map/ppermute | solution.py:350
  12.3 1.7 %collective-permute-start.2 = (bf16[256,256]{1,0:T(8,128)(2,1)S(1)}, bf16[256,256]{1,0:T(8,128)(2,1)S(1)}, u32[]{:S(2)}, u32[]{:S(2)}) collective-permute-start(bf16[256,256]{1,0:T(8,128)(2,1)S(1)} %get-tuple-element.37), channel_id=1, source_target_pairs={{0,1},{1,0},{2,3},{3,2},{4,5},{5,4},{6,7},{7,6},{8,9},{9,8},{10,11... | collective-permute-start | bytes 393224 | tf_op jit(solution)/shard_map/ppermute | solution.py:350
  13.9 3.6 %tables.1 = (f32[256,256]{1,0:T(8,128)S(1)}, bf16[256,64,128]{2,1,0:T(8,128)(2,1)S(1)}, bf16[128,16384]{1,0:T(8,128)(2,1)S(1)}, f32[8,128]{1,0:T(8,128)S(1)}, f3...) custom-call(s32[64,512]{1,0:T(8,128)} %off_hbm.1, ...), custom_call_target="tpu_custom_call" | custom-call | bytes 19679232 | tf_op jit(solution)/shard_map/tables/pallas_call | solution.py:73
  17.5 0.5 collective-permute-done.3.far_ref
  18.0 0.0 collective-permute-done.2.near_ref
  18.1 0.8 %density.1 = (f32[256,256]{1,0:T(8,128)S(1)}, bf16[512,256]{1,0:T(8,128)(2,1)S(1)}) custom-call(f32[256,256]{1,0:T(8,128)S(1)} %get-tuple-element.36.part_ref, bf16[256,256]{1,0:T(8,128)(2,1)S(1)} %collective-permute-done.2.near_ref, bf16[256,256]{1,0:T(8,128)(2,1)S(1)} %collective-permute-done.3.far_ref, ...), custom_call_target="tpu_custom_call" | custom-call | bytes 2359296 | tf_op jit(solution)/shard_map/density/pallas_call | solution.py:73
  18.8 12.0 %all_to_all.22 = bf16[32,16,256]{2,1,0:T(8,128)(2,1)S(1)} all-to-all(bf16[32,16,256]{2,1,0:T(8,128)(2,1)S(1)} %bitcast.20), channel_id=1, replica_groups=mesh['cx'=4,'cy'=8] {'cx','cy'}, dimensions={0} | all-to-all | bytes 524288 | tf_op jit(solution)/shard_map/all_to_all | solution.py:427
  30.8 4.7 %cones.1 = (f32[8,128]{1,0:T(8,128)}, bf16[512,256]{1,0:T(8,128)(2,1)S(1)}) custom-call(bf16[512,256]{1,0:T(8,128)(2,1)S(1)} %bitcast.17, bf16[256,64,128]{2,1,0:T(8,128)(2,1)S(1)} %get-tuple-element.40.early_ref, bf16[256,64,128]{2,1,0:T(8,128)(2,1)S(1)} %get-tuple-element.41.late_ref, bf16[128,16384]{1,0:T(8,128)(2,1)S(1)} %get-tuple-element.42.flip_early_ref, ...), custom_call_target="tpu_custom_call" | custom-call | bytes 19017728 | tf_op jit(solution)/shard_map/cones/pallas_call | solution.py:73
  35.5 0.0 copy-start
  35.5 12.8 %all_to_all.23 = bf16[32,16,256]{2,1,0:T(8,128)(2,1)S(1)} all-to-all(bf16[32,16,256]{2,1,0:T(8,128)(2,1)S(1)} %bitcast.19), channel_id=1, replica_groups=mesh['cx'=4,'cy'=8] {'cx','cy'}, dimensions={0} | all-to-all | bytes 524288 | tf_op jit(solution)/shard_map/all_to_all | solution.py:435
  48.3 0.4 owners.1
  48.6 2.9 %collective-permute-start.5 = (bf16[256,256]{1,0:T(8,128)(2,1)S(1)}, bf16[256,256]{1,0:T(8,128)(2,1)S(1)}, u32[]{:S(2)}, u32[]{:S(2)}) collective-permute-start(bf16[256,256]{1,0:T(8,128)(2,1)S(1)} %get-tuple-element.54), channel_id=1, source_target_pairs={{1,2},{2,1},{3,4},{4,3},{5,6},{6,5},{9,10},{10,9},{11,12},{12,11},... | collective-permute-start | bytes 393224 | tf_op jit(solution)/shard_map/ppermute | solution.py:350
  51.6 0.1 collective-permute-start.4
  51.7 0.3 own_y.1.part_ref
  51.9 4.5 %collective-permute-done.5.far_ref = bf16[256,256]{1,0:T(8,128)(2,1)S(1)} collective-permute-done((bf16[256,256]{1,0:T(8,128)(2,1)S(1)}, bf16[256,256]{1,0:T(8,128)(2,1)S(1)}, u32[]{:S(2)}, u32[]{:S(2)}) %collective-permute-start.5) | collective-permute-done | bytes 131104 | tf_op jit(solution)/shard_map/ppermute | solution.py:350
  56.5 0.0 collective-permute-done.4.near_ref
  56.5 0.2 along_y.1
  56.7 2.2 %collective-permute-start.7 = (bf16[256,256]{1,0:T(8,128)(2,1)S(1)}, bf16[256,256]{1,0:T(8,128)(2,1)S(1)}, u32[]{:S(2)}, u32[]{:S(2)}) collective-permute-start(bf16[256,256]{1,0:T(8,128)(2,1)S(1)} %get-tuple-element.56), channel_id=1, source_target_pairs={{8,16},{16,8},{9,17},{17,9},{10,18},{18,10},{11,19},{19,11},{12,20... | collective-permute-start | bytes 393224 | tf_op jit(solution)/shard_map/ppermute | solution.py:350
  59.0 0.4 collective-permute-start.6
  59.4 0.0 copy-done
  59.4 0.3 own_x.1.part_ref
  59.7 3.9 %collective-permute-done.7.far_ref = bf16[256,256]{1,0:T(8,128)(2,1)S(1)} collective-permute-done((bf16[256,256]{1,0:T(8,128)(2,1)S(1)}, bf16[256,256]{1,0:T(8,128)(2,1)S(1)}, u32[]{:S(2)}, u32[]{:S(2)}) %collective-permute-start.7) | collective-permute-done | bytes 131104 | tf_op jit(solution)/shard_map/ppermute | solution.py:350
  63.6 0.4 collective-permute-done.6.near_ref
  64.0 0.9 %finish.1 = f32[256,256]{1,0:T(8,128)} custom-call(f32[256,256]{1,0:T(8,128)S(1)} %own_x.1.part_ref, bf16[256,256]{1,0:T(8,128)(2,1)S(1)} %collective-permute-done.6.near_ref, bf16[256,256]{1,0:T(8,128)(2,1)S(1)} %collective-permute-done.7.far_ref, bf16[6,256,256]{2,1,0:T(8,128)(2,1)S(1)} %get-tuple-element.31.mats_ref), custom_call_target="tpu_custom_call" | custom-call | bytes 1572864 | tf_op jit(solution)/shard_map/finish/pallas_call | solution.py:73
Async XLA Ops:
  1.6 7.1 %collective-permute-start.1 = (bf16[256,256]{1,0:T(8,128)(2,1)S(1)}, bf16[256,256]{1,0:T(8,128)(2,1)S(1)}, u32[]{:S(2)}, u32[]{:S(2)}) collective-permute-start(bf16[256,256]{1,0:T(8,128)(2,1)S(1)} %bitcast_convert_fusion), channel_id=1, source_target_pairs={{8,16},{16,8},{9,17},{17,9},{10,18},{18,10},{11,19},{19,11},{12,20... | collective-permute-start | bytes 393224 | tf_op jit(solution)/shard_map/ppermute | solution.py:350
  5.1 5.0 %collective-permute-start = (bf16[256,256]{1,0:T(8,128)(2,1)S(1)}, bf16[256,256]{1,0:T(8,128)(2,1)S(1)}, u32[]{:S(2)}, u32[]{:S(2)}) collective-permute-start(bf16[256,256]{1,0:T(8,128)(2,1)S(1)} %bitcast_convert_fusion), channel_id=1, source_target_pairs={{0,8},{8,0},{16,24},{24,16},{1,9},{9,1},{17,25},{25,17},{2,10},{10... | collective-permute-start | bytes 393224 | tf_op jit(solution)/shard_map/ppermute | solution.py:350
  10.4 7.7 %collective-permute-start.3 = (bf16[256,256]{1,0:T(8,128)(2,1)S(1)}, bf16[256,256]{1,0:T(8,128)(2,1)S(1)}, u32[]{:S(2)}, u32[]{:S(2)}) collective-permute-start(bf16[256,256]{1,0:T(8,128)(2,1)S(1)} %get-tuple-element.37), channel_id=1, source_target_pairs={{1,2},{2,1},{3,4},{4,3},{5,6},{6,5},{9,10},{10,9},{11,12},{12,11},... | collective-permute-start | bytes 393224 | tf_op jit(solution)/shard_map/ppermute | solution.py:350
  12.3 5.8 %collective-permute-start.2 = (bf16[256,256]{1,0:T(8,128)(2,1)S(1)}, bf16[256,256]{1,0:T(8,128)(2,1)S(1)}, u32[]{:S(2)}, u32[]{:S(2)}) collective-permute-start(bf16[256,256]{1,0:T(8,128)(2,1)S(1)} %get-tuple-element.37), channel_id=1, source_target_pairs={{0,1},{1,0},{2,3},{3,2},{4,5},{5,4},{6,7},{7,6},{8,9},{9,8},{10,11... | collective-permute-start | bytes 393224 | tf_op jit(solution)/shard_map/ppermute | solution.py:350
  35.5 23.9 %copy-start = (f32[16,16,256]{2,1,0:T(8,128)S(1)}, f32[16,16,256]{2,1,0:T(8,128)}, u32[]{:S(2)}) copy-start(f32[16,16,256]{2,1,0:T(8,128)} %param.9) | copy-start | bytes 786436
  48.6 7.8 %collective-permute-start.5 = (bf16[256,256]{1,0:T(8,128)(2,1)S(1)}, bf16[256,256]{1,0:T(8,128)(2,1)S(1)}, u32[]{:S(2)}, u32[]{:S(2)}) collective-permute-start(bf16[256,256]{1,0:T(8,128)(2,1)S(1)} %get-tuple-element.54), channel_id=1, source_target_pairs={{1,2},{2,1},{3,4},{4,3},{5,6},{6,5},{9,10},{10,9},{11,12},{12,11},... | collective-permute-start | bytes 393224 | tf_op jit(solution)/shard_map/ppermute | solution.py:350
  51.6 4.9 %collective-permute-start.4 = (bf16[256,256]{1,0:T(8,128)(2,1)S(1)}, bf16[256,256]{1,0:T(8,128)(2,1)S(1)}, u32[]{:S(2)}, u32[]{:S(2)}) collective-permute-start(bf16[256,256]{1,0:T(8,128)(2,1)S(1)} %get-tuple-element.54), channel_id=1, source_target_pairs={{0,1},{1,0},{2,3},{3,2},{4,5},{5,4},{6,7},{7,6},{8,9},{9,8},{10,11... | collective-permute-start | bytes 393224 | tf_op jit(solution)/shard_map/ppermute | solution.py:350
  56.7 6.9 %collective-permute-start.7 = (bf16[256,256]{1,0:T(8,128)(2,1)S(1)}, bf16[256,256]{1,0:T(8,128)(2,1)S(1)}, u32[]{:S(2)}, u32[]{:S(2)}) collective-permute-start(bf16[256,256]{1,0:T(8,128)(2,1)S(1)} %get-tuple-element.56), channel_id=1, source_target_pairs={{8,16},{16,8},{9,17},{17,9},{10,18},{18,10},{11,19},{19,11},{12,20... | collective-permute-start | bytes 393224 | tf_op jit(solution)/shard_map/ppermute | solution.py:350
  59.0 5.0 %collective-permute-start.6 = (bf16[256,256]{1,0:T(8,128)(2,1)S(1)}, bf16[256,256]{1,0:T(8,128)(2,1)S(1)}, u32[]{:S(2)}, u32[]{:S(2)}) collective-permute-start(bf16[256,256]{1,0:T(8,128)(2,1)S(1)} %get-tuple-element.56), channel_id=1, source_target_pairs={{0,8},{8,0},{16,24},{24,16},{1,9},{9,1},{17,25},{25,17},{2,10},{10... | collective-permute-start | bytes 393224 | tf_op jit(solution)/shard_map/ppermute | solution.py:350

commit v7 on v6

--- a/solution.py
+++ b/solution.py
@@ -15,7 +15,7 @@
 AHEAD = 256
 CHUNK = 256
 GIVE = 256
-FETCHES = 4
+FETCHES = 8
 PART = 32
 
 

time: 65.5 us -> 65.9 us (level)
  waiting for transfers between devices: 10.8 us -> 9.98 us
  Pallas kernels: 14.9 us -> 15.7 us
    ppermute x8, waiting for transfers between devices: 10.8 us -> 9.98 us  [exchanged(): lax.ppermute(values, axis, [pair for i in range(first, count - 1, 2) for...]
    pallas_call x10, Pallas kernels: 14.9 us -> 15.7 us  [call(): pl.pallas_call(body, out_shape=shapes, in_specs=[pl.BlockSpec(memory_spac...]
  transfers between devices with their start and end apart: 8 -> 8, of which waited for: 5 -> 5; matrix products, arithmetic and copies ran while one was open for 0% -> 0% of each run, Pallas kernels for 12% -> 13%
where the time goes in v7:
time: 65.9 us; the launch traced here: 65.3 us
  blocking collectives  25.2 us (38%)
  Pallas kernels  15.7 us (24%)
  starting transfers between devices  12.8 us (19%)
  waiting for transfers between devices  9.98 us (15%)
  other arithmetic  0.97 us (1%)
  between operations  0.77 us (1%)
    pallas_call x10, Pallas kernels, call(): pl.pallas_call(body, out_shape=shapes, in_specs=[pl.BlockSpec(memory_spac...  15.7 us
    ppermute x8, starting transfers between devices, exchanged(): lax.ppermute(values, axis, [pair for i in range(first, count - 1, 2) for...  12.8 us
    all_to_all x1, blocking collectives, on_device(): back = lax.all_to_all(grad, axes, split_axis=0, concat_axis=0, tiled=True)  12.8 us
    all_to_all x1, blocking collectives, on_device(): got = lax.all_to_all(packed, axes, split_axis=0, concat_axis=0, tiled=True)  12.4 us
    ppermute x8, waiting for transfers between devices, exchanged(): lax.ppermute(values, axis, [pair for i in range(first, count - 1, 2) for...  9.98 us
  transfers between devices with their start and end apart: 8, of which 5 were waited for; matrix products, arithmetic and copies ran while one was open for 0% of the time, Pallas kernels for 13%

profile of v7, /device:TPU:12, one launch (start us, length us, event | category | flops | bytes accessed | tf_op | source)
XLA Modules:
  0.0 65.3 jit_solution(6790955301297310886)
XLA Ops:
  0.6 1.0 %bitcast_convert_fusion = bf16[256,256]{1,0:T(8,128)(2,1)S(1)} fusion(f32[16,16,256]{2,1,0:T(8,128)} %param.9), kind=kLoop, calls=%fused_computation | loop fusion | flops 65536 | bytes 393216 | tf_op jit(solution)/shard_map/convert_element_type | solution.py:375
  1.6 3.5 %collective-permute-start.1 = (bf16[256,256]{1,0:T(8,128)(2,1)S(1)}, bf16[256,256]{1,0:T(8,128)(2,1)S(1)}, u32[]{:S(2)}, u32[]{:S(2)}) collective-permute-start(bf16[256,256]{1,0:T(8,128)(2,1)S(1)} %bitcast_convert_fusion), channel_id=1, source_target_pairs={{8,16},{16,8},{9,17},{17,9},{10,18},{18,10},{11,19},{19,11},{12,20... | collective-permute-start | bytes 393224 | tf_op jit(solution)/shard_map/ppermute | solution.py:350
  5.1 0.1 collective-permute-start
  5.2 3.9 %operators.1 = (bf16[6,256,256]{2,1,0:T(8,128)(2,1)S(1)}, bf16[6,256,256]{2,1,0:T(8,128)(2,1)S(1)}, bf16[2,256,256]{2,1,0:T(8,128)(2,1)S(1)}, f32[256,256]{1,0:T...) custom-call(f32[256,256]{1,0:T(8,128)} %bitcast.15, ...), custom_call_target="tpu_custom_call" | custom-call | bytes 20320256 | tf_op jit(solution)/shard_map/operators/pallas_call | solution.py:73
  9.1 0.0 collective-permute-done.1.far_ref
  9.1 1.0 %collective-permute-done.near_ref = bf16[256,256]{1,0:T(8,128)(2,1)S(1)} collective-permute-done((bf16[256,256]{1,0:T(8,128)(2,1)S(1)}, bf16[256,256]{1,0:T(8,128)(2,1)S(1)}, u32[]{:S(2)}, u32[]{:S(2)}) %collective-permute-start) | collective-permute-done | bytes 131104 | tf_op jit(solution)/shard_map/ppermute | solution.py:350
  10.1 0.2 along_x.1
  10.4 1.9 %collective-permute-start.3 = (bf16[256,256]{1,0:T(8,128)(2,1)S(1)}, bf16[256,256]{1,0:T(8,128)(2,1)S(1)}, u32[]{:S(2)}, u32[]{:S(2)}) collective-permute-start(bf16[256,256]{1,0:T(8,128)(2,1)S(1)} %get-tuple-element.37), channel_id=1, source_target_pairs={{1,2},{2,1},{3,4},{4,3},{5,6},{6,5},{9,10},{10,9},{11,12},{12,11},... | collective-permute-start | bytes 393224 | tf_op jit(solution)/shard_map/ppermute | solution.py:350
  12.3 1.7 %collective-permute-start.2 = (bf16[256,256]{1,0:T(8,128)(2,1)S(1)}, bf16[256,256]{1,0:T(8,128)(2,1)S(1)}, u32[]{:S(2)}, u32[]{:S(2)}) collective-permute-start(bf16[256,256]{1,0:T(8,128)(2,1)S(1)} %get-tuple-element.37), channel_id=1, source_target_pairs={{0,1},{1,0},{2,3},{3,2},{4,5},{5,4},{6,7},{7,6},{8,9},{9,8},{10,11... | collective-permute-start | bytes 393224 | tf_op jit(solution)/shard_map/ppermute | solution.py:350
  13.9 4.0 %tables.1 = (f32[256,256]{1,0:T(8,128)S(1)}, bf16[256,64,128]{2,1,0:T(8,128)(2,1)S(1)}, bf16[128,16384]{1,0:T(8,128)(2,1)S(1)}, f32[8,128]{1,0:T(8,128)S(1)}, f3...) custom-call(s32[64,512]{1,0:T(8,128)} %off_hbm.1, ...), custom_call_target="tpu_custom_call" | custom-call | bytes 19679232 | tf_op jit(solution)/shard_map/tables/pallas_call | solution.py:73
  17.9 0.1 collective-permute-done.3.far_ref
  18.0 0.0 collective-permute-done.2.near_ref
  18.1 0.8 %density.1 = (f32[256,256]{1,0:T(8,128)S(1)}, bf16[512,256]{1,0:T(8,128)(2,1)S(1)}) custom-call(f32[256,256]{1,0:T(8,128)S(1)} %get-tuple-element.36.part_ref, bf16[256,256]{1,0:T(8,128)(2,1)S(1)} %collective-permute-done.2.near_ref, bf16[256,256]{1,0:T(8,128)(2,1)S(1)} %collective-permute-done.3.far_ref, ...), custom_call_target="tpu_custom_call" | custom-call | bytes 2359296 | tf_op jit(solution)/shard_map/density/pallas_call | solution.py:73
  18.8 12.4 %all_to_all.22 = bf16[32,16,256]{2,1,0:T(8,128)(2,1)S(1)} all-to-all(bf16[32,16,256]{2,1,0:T(8,128)(2,1)S(1)} %bitcast.20), channel_id=1, replica_groups=mesh['cx'=4,'cy'=8] {'cx','cy'}, dimensions={0} | all-to-all | bytes 524288 | tf_op jit(solution)/shard_map/all_to_all | solution.py:427
  31.2 4.6 %cones.1 = (f32[8,128]{1,0:T(8,128)}, bf16[512,256]{1,0:T(8,128)(2,1)S(1)}) custom-call(bf16[512,256]{1,0:T(8,128)(2,1)S(1)} %bitcast.17, bf16[256,64,128]{2,1,0:T(8,128)(2,1)S(1)} %get-tuple-element.40.early_ref, bf16[256,64,128]{2,1,0:T(8,128)(2,1)S(1)} %get-tuple-element.41.late_ref, bf16[128,16384]{1,0:T(8,128)(2,1)S(1)} %get-tuple-element.42.flip_early_ref, ...), custom_call_target="tpu_custom_call" | custom-call | bytes 19017728 | tf_op jit(solution)/shard_map/cones/pallas_call | solution.py:73
  35.9 0.0 copy-start
  35.9 12.8 %all_to_all.23 = bf16[32,16,256]{2,1,0:T(8,128)(2,1)S(1)} all-to-all(bf16[32,16,256]{2,1,0:T(8,128)(2,1)S(1)} %bitcast.19), channel_id=1, replica_groups=mesh['cx'=4,'cy'=8] {'cx','cy'}, dimensions={0} | all-to-all | bytes 524288 | tf_op jit(solution)/shard_map/all_to_all | solution.py:435
  48.7 0.4 owners.1
  49.1 2.9 %collective-permute-start.5 = (bf16[256,256]{1,0:T(8,128)(2,1)S(1)}, bf16[256,256]{1,0:T(8,128)(2,1)S(1)}, u32[]{:S(2)}, u32[]{:S(2)}) collective-permute-start(bf16[256,256]{1,0:T(8,128)(2,1)S(1)} %get-tuple-element.54), channel_id=1, source_target_pairs={{1,2},{2,1},{3,4},{4,3},{5,6},{6,5},{9,10},{10,9},{11,12},{12,11},... | collective-permute-start | bytes 393224 | tf_op jit(solution)/shard_map/ppermute | solution.py:350
  52.0 0.1 collective-permute-start.4
  52.1 0.3 own_y.1.part_ref
  52.3 4.5 %collective-permute-done.5.far_ref = bf16[256,256]{1,0:T(8,128)(2,1)S(1)} collective-permute-done((bf16[256,256]{1,0:T(8,128)(2,1)S(1)}, bf16[256,256]{1,0:T(8,128)(2,1)S(1)}, u32[]{:S(2)}, u32[]{:S(2)}) %collective-permute-start.5) | collective-permute-done | bytes 131104 | tf_op jit(solution)/shard_map/ppermute | solution.py:350
  56.9 0.0 collective-permute-done.4.near_ref
  56.9 0.2 along_y.1
  57.1 2.2 %collective-permute-start.7 = (bf16[256,256]{1,0:T(8,128)(2,1)S(1)}, bf16[256,256]{1,0:T(8,128)(2,1)S(1)}, u32[]{:S(2)}, u32[]{:S(2)}) collective-permute-start(bf16[256,256]{1,0:T(8,128)(2,1)S(1)} %get-tuple-element.56), channel_id=1, source_target_pairs={{8,16},{16,8},{9,17},{17,9},{10,18},{18,10},{11,19},{19,11},{12,20... | collective-permute-start | bytes 393224 | tf_op jit(solution)/shard_map/ppermute | solution.py:350
  59.4 0.4 collective-permute-start.6
  59.8 0.0 copy-done
  59.8 0.3 own_x.1.part_ref
  60.1 3.9 %collective-permute-done.7.far_ref = bf16[256,256]{1,0:T(8,128)(2,1)S(1)} collective-permute-done((bf16[256,256]{1,0:T(8,128)(2,1)S(1)}, bf16[256,256]{1,0:T(8,128)(2,1)S(1)}, u32[]{:S(2)}, u32[]{:S(2)}) %collective-permute-start.7) | collective-permute-done | bytes 131104 | tf_op jit(solution)/shard_map/ppermute | solution.py:350
  64.0 0.4 collective-permute-done.6.near_ref
  64.4 0.9 %finish.1 = f32[256,256]{1,0:T(8,128)} custom-call(f32[256,256]{1,0:T(8,128)S(1)} %own_x.1.part_ref, bf16[256,256]{1,0:T(8,128)(2,1)S(1)} %collective-permute-done.6.near_ref, bf16[256,256]{1,0:T(8,128)(2,1)S(1)} %collective-permute-done.7.far_ref, bf16[6,256,256]{2,1,0:T(8,128)(2,1)S(1)} %get-tuple-element.31.mats_ref), custom_call_target="tpu_custom_call" | custom-call | bytes 1572864 | tf_op jit(solution)/shard_map/finish/pallas_call | solution.py:73
Async XLA Ops:
  1.6 7.5 %collective-permute-start.1 = (bf16[256,256]{1,0:T(8,128)(2,1)S(1)}, bf16[256,256]{1,0:T(8,128)(2,1)S(1)}, u32[]{:S(2)}, u32[]{:S(2)}) collective-permute-start(bf16[256,256]{1,0:T(8,128)(2,1)S(1)} %bitcast_convert_fusion), channel_id=1, source_target_pairs={{8,16},{16,8},{9,17},{17,9},{10,18},{18,10},{11,19},{19,11},{12,20... | collective-permute-start | bytes 393224 | tf_op jit(solution)/shard_map/ppermute | solution.py:350
  5.1 5.0 %collective-permute-start = (bf16[256,256]{1,0:T(8,128)(2,1)S(1)}, bf16[256,256]{1,0:T(8,128)(2,1)S(1)}, u32[]{:S(2)}, u32[]{:S(2)}) collective-permute-start(bf16[256,256]{1,0:T(8,128)(2,1)S(1)} %bitcast_convert_fusion), channel_id=1, source_target_pairs={{0,8},{8,0},{16,24},{24,16},{1,9},{9,1},{17,25},{25,17},{2,10},{10... | collective-permute-start | bytes 393224 | tf_op jit(solution)/shard_map/ppermute | solution.py:350
  10.4 7.7 %collective-permute-start.3 = (bf16[256,256]{1,0:T(8,128)(2,1)S(1)}, bf16[256,256]{1,0:T(8,128)(2,1)S(1)}, u32[]{:S(2)}, u32[]{:S(2)}) collective-permute-start(bf16[256,256]{1,0:T(8,128)(2,1)S(1)} %get-tuple-element.37), channel_id=1, source_target_pairs={{1,2},{2,1},{3,4},{4,3},{5,6},{6,5},{9,10},{10,9},{11,12},{12,11},... | collective-permute-start | bytes 393224 | tf_op jit(solution)/shard_map/ppermute | solution.py:350
  12.3 5.8 %collective-permute-start.2 = (bf16[256,256]{1,0:T(8,128)(2,1)S(1)}, bf16[256,256]{1,0:T(8,128)(2,1)S(1)}, u32[]{:S(2)}, u32[]{:S(2)}) collective-permute-start(bf16[256,256]{1,0:T(8,128)(2,1)S(1)} %get-tuple-element.37), channel_id=1, source_target_pairs={{0,1},{1,0},{2,3},{3,2},{4,5},{5,4},{6,7},{7,6},{8,9},{9,8},{10,11... | collective-permute-start | bytes 393224 | tf_op jit(solution)/shard_map/ppermute | solution.py:350
  35.9 23.9 %copy-start = (f32[16,16,256]{2,1,0:T(8,128)S(1)}, f32[16,16,256]{2,1,0:T(8,128)}, u32[]{:S(2)}) copy-start(f32[16,16,256]{2,1,0:T(8,128)} %param.9) | copy-start | bytes 786436
  49.1 7.8 %collective-permute-start.5 = (bf16[256,256]{1,0:T(8,128)(2,1)S(1)}, bf16[256,256]{1,0:T(8,128)(2,1)S(1)}, u32[]{:S(2)}, u32[]{:S(2)}) collective-permute-start(bf16[256,256]{1,0:T(8,128)(2,1)S(1)} %get-tuple-element.54), channel_id=1, source_target_pairs={{1,2},{2,1},{3,4},{4,3},{5,6},{6,5},{9,10},{10,9},{11,12},{12,11},... | collective-permute-start | bytes 393224 | tf_op jit(solution)/shard_map/ppermute | solution.py:350
  52.0 4.9 %collective-permute-start.4 = (bf16[256,256]{1,0:T(8,128)(2,1)S(1)}, bf16[256,256]{1,0:T(8,128)(2,1)S(1)}, u32[]{:S(2)}, u32[]{:S(2)}) collective-permute-start(bf16[256,256]{1,0:T(8,128)(2,1)S(1)} %get-tuple-element.54), channel_id=1, source_target_pairs={{0,1},{1,0},{2,3},{3,2},{4,5},{5,4},{6,7},{7,6},{8,9},{9,8},{10,11... | collective-permute-start | bytes 393224 | tf_op jit(solution)/shard_map/ppermute | solution.py:350
  57.1 6.9 %collective-permute-start.7 = (bf16[256,256]{1,0:T(8,128)(2,1)S(1)}, bf16[256,256]{1,0:T(8,128)(2,1)S(1)}, u32[]{:S(2)}, u32[]{:S(2)}) collective-permute-start(bf16[256,256]{1,0:T(8,128)(2,1)S(1)} %get-tuple-element.56), channel_id=1, source_target_pairs={{8,16},{16,8},{9,17},{17,9},{10,18},{18,10},{11,19},{19,11},{12,20... | collective-permute-start | bytes 393224 | tf_op jit(solution)/shard_map/ppermute | solution.py:350
  59.4 5.0 %collective-permute-start.6 = (bf16[256,256]{1,0:T(8,128)(2,1)S(1)}, bf16[256,256]{1,0:T(8,128)(2,1)S(1)}, u32[]{:S(2)}, u32[]{:S(2)}) collective-permute-start(bf16[256,256]{1,0:T(8,128)(2,1)S(1)} %get-tuple-element.56), channel_id=1, source_target_pairs={{0,8},{8,0},{16,24},{24,16},{1,9},{9,1},{17,25},{25,17},{2,10},{10... | collective-permute-start | bytes 393224 | tf_op jit(solution)/shard_map/ppermute | solution.py:350
